TPU v7x, 32 devices: a whole 2x2x4 slice. The times are simulated.
32 devices in a mesh: seq: 8 (over y, x, core), tp: 4 (over z).
Axes of the slice: x: 2, y: 2, z: 4, core: 2. Of those that a mesh axis runs over, the one named last changes fastest.
Arguments:
- inputs: bfloat16 [1024, 4096], P('seq', 'tp'), may hold values from -6 to 6
- target: bfloat16 [1024, 4096], P('seq', 'tp'), may hold values from -6 to 6
- feature_slots: int32 [1024, 8, 8], P(None, 'seq'), may hold values from -1 to 8191, as said below
- w_enc: bfloat16 [65536, 4096], P('seq', 'tp'), may hold values from -0.09375 to 0.09375
- b_enc: float32 [65536], P('seq'), may hold values from -1 to 1
- w_dec: bfloat16 [65536, 4096], P('seq', 'tp'), may hold values from -0.75 to 0.75
- b_dec: float32 [4096], P('tp'), may hold values from -3 to 3
- w_skip: bfloat16 [4096, 4096], P('seq', 'tp'), may hold values from -0.09375 to 0.09375
Outputs:
- reconstruction: bfloat16 [1024, 4096], P('seq', 'tp')
- grad_enc: bfloat16 [65536, 4096], P('seq', 'tp')
- grad_dec: bfloat16 [65536, 4096], P('seq', 'tp')
- grad_benc: float32 [65536], P('seq')
- grad_bdec: float32 [4096], P('tp')
- grad_skip: bfloat16 [4096, 4096], P('seq', 'tp')
Inputs may be any that keep to these rules, and one draw needn't show every extreme that they name: feature_slots[t, o, j] is a feature number inside block o of 8192 features, or -1 for an empty slot; each token has exactly 64 live slots naming distinct features, at most 8 in one block, and every token fills all 8 slots of at least one block.
All inputs are finite; a program needn't handle non-finite values.
Results may differ from a plain program's by a relative error of at most 0.0059.
Values may be sent and summed in bfloat16 or wider, within the bound.
No kernel may reach another device: no remote copies, remote signals or barrier semaphores. Data moves between devices by JAX's collectives and lax.ppermute only.
A program may use at most 256 MiB of HBM per device.

v0:
```python
import math

import jax
import jax.numpy as jnp
from jax import lax
from jax.sharding import PartitionSpec as P


def spread(value, axis, source):
    kept = jnp.where(lax.axis_index(axis) == source, value, 0).astype(value.dtype)
    return lax.psum(kept, axis)


def shards(inputs, target, feature_slots, w_enc, b_enc, w_dec, b_dec, w_skip):
    local_ids = feature_slots[:, 0, :]
    live_float = (local_ids >= 0).astype(jnp.float32)
    index_table = jnp.maximum(local_ids, 0)
    all_tokens = lax.all_gather(inputs, "seq", axis=0, tiled=True)
    total_rows = all_tokens.shape[0]
    block_rows = min(512, total_rows)
    block_count = total_rows // block_rows
    feat_cols = inputs.shape[1]
    skip_height = w_skip.shape[0]
    block_feats = w_enc.shape[0]

    def encode_block(position):
        first_row = position * block_rows
        tok_rows = lax.dynamic_slice_in_dim(all_tokens, first_row, block_rows, 0)
        id_rows = lax.dynamic_slice_in_dim(index_table, first_row, block_rows, 0)
        return jnp.einsum(
            "bd,bsd->bs", tok_rows, w_enc[id_rows], preferred_element_type=jnp.float32
        )

    partial_pre = lax.map(encode_block, jnp.arange(block_count)).reshape(total_rows, -1)
    summed_pre = lax.psum(partial_pre, "tp")
    preact = summed_pre + b_enc[index_table]
    active = (jnp.maximum(preact, 0.0) * live_float).astype(jnp.bfloat16)
    seq_index = lax.axis_index("seq")
    offset = seq_index * skip_height % feat_cols
    root_index = seq_index * skip_height // feat_cols
    own_piece = lax.dynamic_slice_in_dim(all_tokens, offset, skip_height, 1)
    skip_inputs = spread(own_piece, "tp", root_index)
    row_count = inputs.shape[0] * lax.axis_size("seq")
    sub_rows = math.gcd(row_count, 512)

    def decode_block(position):
        first_row = position * sub_rows
        id_rows = lax.dynamic_slice_in_dim(index_table, first_row, sub_rows, 0)
        act_rows = lax.dynamic_slice_in_dim(active, first_row, sub_rows, 0)
        partial_value = jnp.einsum(
            "bs,bsd->bd", act_rows, w_dec[id_rows], preferred_element_type=jnp.float32
        )
        skip_part = lax.dynamic_slice_in_dim(skip_inputs, first_row, sub_rows, 0)
        partial_value = partial_value + jnp.dot(
            skip_part, w_skip, preferred_element_type=jnp.float32
        )
        return partial_value

    decoded = lax.psum_scatter(
        lax.map(decode_block, jnp.arange(row_count // sub_rows)).reshape(row_count, -1),
        "seq",
        scatter_dimension=0,
        tiled=True,
    )
    predicted = decoded + b_dec
    reconstruction = predicted.astype(jnp.bfloat16)
    residual = (predicted - target.astype(jnp.float32)).astype(jnp.bfloat16)
    all_resid = lax.all_gather(residual, "seq", axis=0, tiled=True)

    def back_block(position):
        first_row = position * block_rows
        res_rows = lax.dynamic_slice_in_dim(all_resid, first_row, block_rows, 0)
        id_rows = lax.dynamic_slice_in_dim(index_table, first_row, block_rows, 0)
        return jnp.einsum(
            "bd,bsd->bs", res_rows, w_dec[id_rows], preferred_element_type=jnp.float32
        )

    partial_back = lax.map(back_block, jnp.arange(block_count)).reshape(total_rows, -1)
    summed_back = lax.psum(partial_back, "tp")
    slope = summed_back * (preact > 0.0).astype(jnp.float32) * live_float
    grad_benc = (
        jnp.zeros(b_enc.shape, jnp.float32).at[index_table.reshape(-1)].add(slope.reshape(-1))
    )
    slope_half = slope.astype(jnp.bfloat16)
    row_numbers = jnp.arange(block_rows, dtype=jnp.int32)[:, None]
    contract_rows = (((0,), (0,)), ((), ()))

    def grad_block(carry, position):
        enc_total, dec_total = carry
        first_row = position * block_rows
        tok_rows = lax.dynamic_slice_in_dim(all_tokens, first_row, block_rows, 0)
        res_rows = lax.dynamic_slice_in_dim(all_resid, first_row, block_rows, 0)
        id_rows = lax.dynamic_slice_in_dim(index_table, first_row, block_rows, 0)
        slope_rows = lax.dynamic_slice_in_dim(slope_half, first_row, block_rows, 0)
        act_rows = lax.dynamic_slice_in_dim(active, first_row, block_rows, 0)
        empty_table = jnp.zeros((block_rows, block_feats), jnp.bfloat16)
        slope_table = empty_table.at[row_numbers, id_rows].add(slope_rows)
        act_table = empty_table.at[row_numbers, id_rows].add(act_rows)
        enc_total = enc_total + lax.dot_general(
            slope_table, tok_rows, contract_rows, preferred_element_type=jnp.float32
        )
        dec_total = dec_total + lax.dot_general(
            act_table, res_rows, contract_rows, preferred_element_type=jnp.float32
        )
        return ((enc_total, dec_total), position)

    zero_grads = jnp.zeros(w_enc.shape, jnp.float32)
    totals = lax.scan(grad_block, (zero_grads, zero_grads), jnp.arange(block_count))[0]
    grad_bdec = jnp.sum(all_resid.astype(jnp.float32), axis=0)
    grad_skip = jnp.dot(skip_inputs.T, all_resid, preferred_element_type=jnp.float32).astype(
        jnp.bfloat16
    )
    return (
        reconstruction,
        totals[0].astype(jnp.bfloat16),
        totals[1].astype(jnp.bfloat16),
        grad_benc,
        grad_bdec,
        grad_skip,
    )


def solution(mesh):
    in_specs = (
        P("seq", "tp"),
        P("seq", "tp"),
        P(None, "seq", None),
        P("seq", "tp"),
        P("seq"),
        P("seq", "tp"),
        P("tp"),
        P("seq", "tp"),
    )
    out_specs = (P("seq", "tp"), P("seq", "tp"), P("seq", "tp"), P("seq"), P("tp"), P("seq", "tp"))
    return jax.shard_map(shards, mesh=mesh, in_specs=in_specs, out_specs=out_specs, check_vma=False)
```

profile of v0, /device:TPU:0, one launch (start us, length us, event | category | flops | bytes accessed | tf_op | source)
XLA Modules:
  0.0 814.3 jit_solution(7075159640835346540)
XLA Ops:
  10.2 45.5 %gather_fusion.3 = f32[8192]{0:T(1024)S(1)} fusion(f32[8192]{0:T(1024)S(1)} %copy-done, s32[8192]{0:T(1024)S(1)} %broadcast_clamp_fusion.3), kind=kCustom, calls=%fused_computation.3 | custom fusion | bytes 98304 | tf_op jit(solution)/shard_map/gather | solution.py:36
  58.8 79.4 %while.43 = (s32[]{:T(128)}, f32[2,512,8]{1,2,0:T(8,128)S(1)}, s32[2]{0:T(128)S(1)}, bf16[1024,1024]{1,0:T(8,128)(2,1)}, s32[1024,8]{1,0:T(8,128)S(1)}, /*index=...) while((s32[]{:T(128)}, f32[2,512,8]{1,2,0:T(8,128)S(1)}, s32[2]{0:T(128)S(1)}, ...), condition=%wide.region_1.2_spmd, body=%wide.region_0.1_spmd.sunk | while | flops 8404998 | bytes 28508340 | solution.py:34
  61.5 28.9 %gather_fusion = bf16[4096,1024]{1,0:T(8,128)(2,1)} fusion(bf16[8192,1024]{1,0:T(8,128)(2,1)} %get-tuple-element.511, s32[4096]{0:T(1024)S(1)} %broadcast_clamp_fusion.7), kind=kCustom, calls=%fused_computation.clone.1 | custom fusion | bytes 16793600 | tf_op jit(solution)/shard_map/while/body/eval_jaxpr/gather | solution.py:31
  101.3 28.8 %gather_fusion = bf16[4096,1024]{1,0:T(8,128)(2,1)} fusion(bf16[8192,1024]{1,0:T(8,128)(2,1)} %get-tuple-element.511, s32[4096]{0:T(1024)S(1)} %broadcast_clamp_fusion.7), kind=kCustom, calls=%fused_computation.clone.1 | custom fusion | bytes 16793600 | tf_op jit(solution)/shard_map/while/body/eval_jaxpr/gather | solution.py:31
  139.2 32.8 %psum.21 = f32[1024,8]{1,0:T(8,128)S(1)} all-reduce(f32[1024,8]{1,0:T(8,128)} %bitcast.89), channel_id=1, replica_groups=mesh['seq'=8,'tp'=4] {'tp'}, use_global_device_ids=true, to_apply=%region_2.3 | all-reduce | flops 8192 | bytes 65536 | tf_op jit(solution)/shard_map/psum | solution.py:35
  174.7 76.6 %while.44 = (s32[]{:T(128)}, f32[2,512,1024]{2,1,0:T(8,128)}, s32[2]{0:T(128)S(1)}, bf16[1024,8]{0,1:T(8,128)(2,1)S(1)}, s32[1024,8]{1,0:T(8,128)S(1)}, /*index=...) while((s32[]{:T(128)}, f32[2,512,1024]{2,1,0:T(8,128)}, ...), condition=%wide.region_5.6_spmd, body=%wide.region_4.5_spmd.sunk | while | flops 545800192 | bytes 37380320 | solution.py:60
  176.4 28.7 %gather_fusion.1 = bf16[4096,1024]{1,0:T(8,128)(2,1)} fusion(bf16[8192,1024]{1,0:T(8,128)(2,1)} %get-tuple-element.545, s32[4096]{0:T(1024)S(1)} %broadcast_clamp_fusion.8), kind=kCustom, calls=%fused_computation.1.clone.1 | custom fusion | bytes 16793600 | tf_op jit(solution)/shard_map/while/body/eval_jaxpr/gather | solution.py:51
  214.7 28.7 %gather_fusion.1 = bf16[4096,1024]{1,0:T(8,128)(2,1)} fusion(bf16[8192,1024]{1,0:T(8,128)(2,1)} %get-tuple-element.545, s32[4096]{0:T(1024)S(1)} %broadcast_clamp_fusion.8), kind=kCustom, calls=%fused_computation.1.clone.1 | custom fusion | bytes 16793600 | tf_op jit(solution)/shard_map/while/body/eval_jaxpr/gather | solution.py:51
  251.8 49.4 %reduce-scatter.2.cloned.1.call-done = f32[128,1024]{1,0:T(8,128)} async-done(((f32[1024,1024]{1,0:T(8,128)}), f32[128,1024]{1,0:T(8,128)}) %reduce-scatter.2.cloned.1.call-update) | async-done | bytes 524304 | tf_op jit(solution)/shard_map/reduce_scatter | solution.py:59
  303.4 28.0 %all-gather.5.cloned.1.call-done = bf16[1024,1024]{1,0:T(8,128)(2,1)} async-done(((bf16[128,1024]{1,0:T(8,128)(2,1)}), bf16[1024,1024]{1,0:T(8,128)(2,1)}) %all-gather.5.cloned.1.call-update) | async-done | bytes 2097168 | tf_op jit(solution)/shard_map/all_gather | solution.py:68
  331.4 79.0 %while.45 = (s32[]{:T(128)}, f32[2,512,8]{1,2,0:T(8,128)S(1)}, s32[2]{0:T(128)S(1)}, bf16[1024,1024]{1,0:T(8,128)(2,1)}, s32[1024,8]{1,0:T(8,128)S(1)}, /*index=...) while((s32[]{:T(128)}, f32[2,512,8]{1,2,0:T(8,128)S(1)}, s32[2]{0:T(128)S(1)}, ...), condition=%wide.region_8.9_spmd, body=%wide.region_7.8_spmd.sunk | while | flops 8404998 | bytes 28508340 | solution.py:78
  334.2 28.7 %gather_fusion.2 = bf16[4096,1024]{1,0:T(8,128)(2,1)} fusion(bf16[8192,1024]{1,0:T(8,128)(2,1)} %get-tuple-element.577, s32[4096]{0:T(1024)S(1)} %broadcast_clamp_fusion.9), kind=kCustom, calls=%fused_computation.2.clone.1 | custom fusion | bytes 16793600 | tf_op jit(solution)/shard_map/while/body/eval_jaxpr/gather | solution.py:75
  373.7 28.7 %gather_fusion.2 = bf16[4096,1024]{1,0:T(8,128)(2,1)} fusion(bf16[8192,1024]{1,0:T(8,128)(2,1)} %get-tuple-element.577, s32[4096]{0:T(1024)S(1)} %broadcast_clamp_fusion.9), kind=kCustom, calls=%fused_computation.2.clone.1 | custom fusion | bytes 16793600 | tf_op jit(solution)/shard_map/while/body/eval_jaxpr/gather | solution.py:75
  410.7 30.1 %psum.23 = f32[1024,8]{1,0:T(8,128)S(1)} all-reduce(f32[1024,8]{1,0:T(8,128)S(1)} %bitcast.90), channel_id=1, replica_groups=mesh['seq'=8,'tp'=4] {'tp'}, use_global_device_ids=true, to_apply=%region_9.10 | all-reduce | flops 8192 | bytes 65536 | tf_op jit(solution)/shard_map/psum | solution.py:79
  442.5 283.9 %while.46 = (s32[]{:T(128)}, f32[8192,1024]{1,0:T(8,128)}, f32[8192,1024]{1,0:T(8,128)}, s32[2]{0:T(128)S(1)}, s32[1024,8]{0,1:T(8,128)S(1)}, /*index=5*/bf16[10...) while((s32[]{:T(128)}, f32[8192,1024]{1,0:T(8,128)}, ...), condition=%wide.region_13.14_spmd.clone, body=%wide.region_10.13_spmd.clone.sunk | while | flops 17213505536 | bytes 212115760 | solution.py:108
  445.7 33.8 %scatter_custom_fusion.15 = bf16[4194304]{0:T(1024)(128)(2,1)} fusion(s32[4096]{0:T(1024)S(1)} %reshape.207, bf16[4096]{0:T(1024)(128)(2,1)S(1)} %reshape.210, bf16[]{:T(256)} %constant.77.clone.2..sunk), kind=kCustom, calls=%fused_computation.33.clone.1 | custom fusion | flops 4096 | bytes 8388610 | tf_op jit(solution)/shard_map/while
  492.9 33.8 %scatter_custom_fusion.14 = bf16[4194304]{0:T(1024)(128)(2,1)} fusion(s32[4096]{0:T(1024)S(1)} %reshape.207, bf16[4096]{0:T(1024)(128)(2,1)S(1)} %reshape.208, bf16[]{:T(256)} %constant.77.clone.2..sunk), kind=kCustom, calls=%fused_computation.35.clone.1 | custom fusion | flops 4096 | bytes 8388610 | tf_op jit(solution)/shard_map/while
  557.2 17.3 %select_add_fusion.5 = f32[8192,1024]{1,0:T(8,128)} fusion(f32[8192,1024]{1,0:T(8,128)} %get-tuple-element.600, pred[]{:T(512)S(6)} %compare.18, bf16[512,8192]{1,0:T(8,128)(2,1)} %reshape.211, bf16[1024,1024]{1,0:T(8,128)(2,1)S(1)} %copy-done.3, s32[]{:T(128)S(6)} %select_n.98), kind=kOutput, calls=%fused_computation.31.clone.1 | convolution fusion | flops 8606711808 | bytes 76546056 | tf_op jit(solution)/shard_map/while/body/eval_jaxpr/dot_general | solution.py:102
  577.6 33.8 %scatter_custom_fusion.15 = bf16[4194304]{0:T(1024)(128)(2,1)} fusion(s32[4096]{0:T(1024)S(1)} %reshape.207, bf16[4096]{0:T(1024)(128)(2,1)S(1)} %reshape.210, bf16[]{:T(256)} %constant.77.clone.2..sunk), kind=kCustom, calls=%fused_computation.33.clone.1 | custom fusion | flops 4096 | bytes 8388610 | tf_op jit(solution)/shard_map/while
  624.7 33.8 %scatter_custom_fusion.14 = bf16[4194304]{0:T(1024)(128)(2,1)} fusion(s32[4096]{0:T(1024)S(1)} %reshape.207, bf16[4096]{0:T(1024)(128)(2,1)S(1)} %reshape.208, bf16[]{:T(256)} %constant.77.clone.2..sunk), kind=kCustom, calls=%fused_computation.35.clone.1 | custom fusion | flops 4096 | bytes 8388610 | tf_op jit(solution)/shard_map/while
  671.8 28.8 %select_add_fusion.4 = f32[8192,1024]{1,0:T(8,128)} fusion(f32[8192,1024]{1,0:T(8,128)} %get-tuple-element.599, pred[]{:T(512)S(6)} %compare.18, bf16[512,8192]{1,0:T(8,128)(2,1)} %reshape.209, bf16[1024,1024]{1,0:T(8,128)(2,1)} %get-tuple-element.620, s32[]{:T(128)S(6)} %select_n.98), kind=kOutput, calls=%fused_computation.32.clone.1 | convolution fusion | flops 8606711808 | bytes 76546056 | tf_op jit(solution)/shard_map/while/body/eval_jaxpr/dot_general | solution.py:99
  700.6 25.6 %select_add_fusion.5 = f32[8192,1024]{1,0:T(8,128)} fusion(f32[8192,1024]{1,0:T(8,128)} %get-tuple-element.600, pred[]{:T(512)S(6)} %compare.18, bf16[512,8192]{1,0:T(8,128)(2,1)} %reshape.211, bf16[1024,1024]{1,0:T(8,128)(2,1)S(1)} %copy-done.3, s32[]{:T(128)S(6)} %select_n.98), kind=kOutput, calls=%fused_computation.31.clone.1 | convolution fusion | flops 8606711808 | bytes 76546056 | tf_op jit(solution)/shard_map/while/body/eval_jaxpr/dot_general | solution.py:102
  726.4 17.8 %convert_element_type.37 = bf16[8192,1024]{1,0:T(8,128)(2,1)} convert(f32[8192,1024]{1,0:T(8,128)} %get-tuple-element.169) | non-fusion elementwise | flops 8388608 | bytes 50331648 | tf_op jit(solution)/shard_map/convert_element_type | solution.py:116
  760.1 44.2 %scatter_custom_fusion.2 = f32[8192]{0:T(1024)} fusion(s32[8192]{0:T(1024)} %copy-done.18, f32[8192]{0:T(1024)} %reshape.141, f32[]{:T(128)} %constant.111.clone.1), kind=kCustom, calls=%fused_computation.59 | custom fusion | flops 8192 | bytes 33280 | tf_op jit(solution)/shard_map/scatter-add | solution.py:82
  (159 shorter events, 166.6 us)
Async XLA Ops:
  7.2 48.9 %all-gather.3.cloned.1.call-start = ((), (), s32[]{:S(2)}) async-start(), calls=%async_computation.1 | async-start | bytes 2359296 | tf_op jit(solution)/shard_map/all_gather | solution.py:18
  7.9 166.2 %all-reduce.2.cloned.1.call-start = ((), (), s32[]{:S(2)}) async-start(), calls=%async_computation.2 | async-start | bytes 2097152 | tf_op jit(solution)/shard_map/psum | solution.py:11
  10.2 45.6 %copy-start.18 = (s32[8192]{0:T(1024)}, s32[8192]{0:T(1024)S(1)}, u32[]{:S(2)}) copy-start(s32[8192]{0:T(1024)S(1)} %reshape.119) | copy-start | bytes 98308
  10.2 48.5 %copy-start.5 = (s32[1024,8]{1,0:T(8,128)S(1)}, s32[1024,8]{1,0:T(8,128)}, u32[]{:S(2)}) copy-start(s32[1024,8]{1,0:T(8,128)} %get-tuple-element.556) | copy-start | bytes 98308
  56.1 115.9 %copy-start.11 = (f32[1024,8]{1,0:T(8,128)}, f32[1024,8]{1,0:T(8,128)S(1)}, u32[]{:S(2)}) copy-start(f32[1024,8]{1,0:T(8,128)S(1)} %reshape.118) | copy-start | bytes 98308
  58.7 242.5 %reduce-scatter.2.cloned.1.call-start = ((), (), s32[]{:S(2)}) async-start(), calls=%async_computation.3 | async-start | bytes 4718592 | tf_op jit(solution)/shard_map/reduce_scatter | solution.py:59
  58.8 115.4 %copy-start.6 = (bf16[512,1024]{1,0:T(8,128)(2,1)S(1)}, bf16[512,1024]{1,0:T(8,128)(2,1)}, u32[]{:S(2)}) copy-start(bf16[512,1024]{1,0:T(8,128)(2,1)} %param.23) | copy-start | bytes 3145732
  174.2 127.1 %copy-start.17 = (bf16[128,1024]{1,0:T(8,128)(2,1)S(1)}, bf16[128,1024]{1,0:T(8,128)(2,1)}, u32[]{:S(2)}) copy-start(bf16[128,1024]{1,0:T(8,128)(2,1)} %param.17) | copy-start | bytes 786436
  174.2 127.1 %copy-start.21 = (f32[1024]{0:T(1024)S(1)}, f32[1024]{0:T(1024)}, u32[]{:S(2)}) copy-start(f32[1024]{0:T(1024)} %param.22) | copy-start | bytes 12292
  205.1 5.8 copy-start.7
  243.4 5.8 copy-start.7
  251.3 80.0 %all-gather.5.cloned.1.call-start = ((), (), s32[]{:S(2)}) async-start(), calls=%async_computation.4 | async-start | bytes 2359296 | tf_op jit(solution)/shard_map/all_gather | solution.py:68
  331.4 109.5 %copy-start.12 = (f32[1024,8]{1,0:T(8,128)S(1)}, f32[1024,8]{1,0:T(8,128)}, u32[]{:S(2)}) copy-start(f32[1024,8]{1,0:T(8,128)} %copy-done.11) | copy-start | bytes 98308
  331.4 109.5 %copy-start.14 = (f32[1024,8]{1,0:T(8,128)S(1)}, f32[1024,8]{1,0:T(8,128)}, u32[]{:S(2)}) copy-start(f32[1024,8]{1,0:T(8,128)} %copy-done.13) | copy-start | bytes 98308
  331.4 109.5 %copy-start.16 = (pred[1024,1,8]{2,0,1:T(8,128)(4,1)S(1)}, pred[1024,1,8]{2,0,1:T(8,128)(4,1)}, u32[]{:S(2)}) copy-start(pred[1024,1,8]{2,0,1:T(8,128)(4,1)} %get-tuple-element.297) | copy-start | bytes 24580
  331.4 111.1 %copy-start.10 = (bf16[1024,8]{1,0:T(8,128)(2,1)S(1)}, bf16[1024,8]{1,0:T(8,128)(2,1)}, u32[]{:S(2)}) copy-start(bf16[1024,8]{1,0:T(8,128)(2,1)} %copy-done.9) | copy-start | bytes 49156
  331.4 111.1 %copy-start.19 = (s32[2]{0:T(128)S(1)}, s32[2]{0:T(128)}, u32[]{:S(2)}) copy-start(s32[2]{0:T(128)} %constant.184) | copy-start | bytes 28
  331.4 111.1 %copy-start.20 = (s32[2]{0:T(128)S(1)}, s32[2]{0:T(128)}, u32[]{:S(2)}) copy-start(s32[2]{0:T(128)} %constant.183) | copy-start | bytes 28
  540.0 17.3 %copy-start.3 = (bf16[1024,1024]{1,0:T(8,128)(2,1)S(1)}, bf16[1024,1024]{1,0:T(8,128)(2,1)}, u32[]{:S(2)}) copy-start(bf16[1024,1024]{1,0:T(8,128)(2,1)} %get-tuple-element.622) | copy-start | bytes 6291460 | tf_op jit(solution)/shard_map/while
  671.8 28.8 %copy-start.3 = (bf16[1024,1024]{1,0:T(8,128)(2,1)S(1)}, bf16[1024,1024]{1,0:T(8,128)(2,1)}, u32[]{:S(2)}) copy-start(bf16[1024,1024]{1,0:T(8,128)(2,1)} %get-tuple-element.622) | copy-start | bytes 6291460 | tf_op jit(solution)/shard_map/while
  726.4 26.2 %copy-start.2 = (f32[8192,1024]{1,0:T(8,128)S(1)}, f32[8192,1024]{1,0:T(8,128)}, u32[]{:S(2)}) copy-start(f32[8192,1024]{1,0:T(8,128)} %get-tuple-element.168) | copy-start | bytes 100663296
  752.6 51.7 %copy-start.4 = (bf16[1024,1024]{1,0:T(8,128)(2,1)S(1)}, bf16[1024,1024]{1,0:T(8,128)(2,1)}, u32[]{:S(2)}) copy-start(bf16[1024,1024]{1,0:T(8,128)(2,1)} %get-tuple-element.637) | copy-start | bytes 6291460
  752.6 51.7 %copy-start.8 = (bf16[1024,512]{1,0:T(8,128)(2,1)S(1)}, bf16[1024,512]{1,0:T(8,128)(2,1)}, u32[]{:S(2)}) copy-start(bf16[1024,512]{1,0:T(8,128)(2,1)} %get-tuple-element.643) | copy-start | bytes 3145732
  752.6 54.9 %copy-start.1 = (f32[8192]{0:T(1024)S(1)}, f32[8192]{0:T(1024)}, u32[]{:S(2)}) copy-start(f32[8192]{0:T(1024)} %param.20) | copy-start | bytes 98308
  (4 other events, 7.2 us)
Sparse Core Ops, SparseCore 0:
  9.9 30.4 all-gather.2
  58.8 54.6 all-reduce.1
  251.5 49.7 reduce-scatter.1
  303.6 27.7 all-gather.4
where the time goes:
time: 823 us; the launch traced here: 814 us
  local copies, waits for them, and re-layouts  299 us (36%)
  other arithmetic  215 us (26%)
  matrix products  139 us (17%)
  waiting for transfers between devices  78.2 us (10%)
  blocking collectives  62.9 us (8%)
  between operations  14.4 us (2%)
    while x10, other arithmetic  136 us
    gather x2, local copies, waits for them, and re-layouts, encode_block(): w_enc[id_rows]  57.6 us
    gather x2, local copies, waits for them, and re-layouts, decode_block(): w_dec[id_rows]  57.4 us
    gather x2, local copies, waits for them, and re-layouts, back_block(): w_dec[id_rows]  57.4 us
    reduce_scatter x1, waiting for transfers between devices, shards(): lax.psum_scatter(lax.map(decode_block, jnp.arange(row_count // sub_rows))...  49.4 us
    dot_general x2, matrix products, grad_block(): lax.dot_general(slope_table, tok_rows, contract_rows, preferred_element_t...  46 us
    gather x2, local copies, waits for them, and re-layouts, shards(): preact = summed_pre + b_enc[index_table]  45.8 us
    scatter-add x1, other arithmetic, shards(): jnp.zeros(b_enc.shape, jnp.float32).at[index_table.reshape(-1)]  44.2 us
  transfers between devices with their start and end apart: 4, of which 2 were waited for; matrix products, arithmetic and copies ran while one was open for 16% of the time, Pallas kernels for 0%

commit v1 on v0

v1 whole, which is shorter than its diff:
```python
import functools

import jax
import jax.numpy as jnp
from jax import lax
from jax.experimental import pallas as pl
from jax.experimental.pallas import tpu as pltpu
from jax.sharding import PartitionSpec as P

VMEM_BYTES = 60 << 20
F32 = jnp.float32
BF16 = jnp.bfloat16


def pick_kernel(sub, ids_ref, x_ref, w_ref, out_ref):
    step = pl.program_id(0)
    tile = w_ref.shape[0]

    @pl.when(step == 0)
    def _():
        out_ref[...] = jnp.zeros_like(out_ref)

    for s in range(tile // sub):
        dots = lax.dot_general(
            w_ref[s * sub : (s + 1) * sub, :],
            x_ref[...],
            (((1,), (1,)), ((), ())),
            preferred_element_type=F32,
        )
        for block in range(out_ref.shape[1] // 128):
            cols = slice(block * 128, (block + 1) * 128)
            ids = ids_ref[:, cols]
            low = ids & 7
            high = (ids >> 3) - (step * (tile // 8) + s * (sub // 8))
            kept = out_ref[:, cols]
            for g in range(sub // 8):
                found = jnp.take_along_axis(dots[g * 8 : (g + 1) * 8, cols], low, axis=0)
                kept = jnp.where(high == g, found, kept)
            out_ref[:, cols] = kept


def pick(ids, x, w, name):
    features, width = w.shape
    slots, tokens = ids.shape
    tile = min(1024, features)
    return pl.pallas_call(
        functools.partial(pick_kernel, min(256, tile)),
        grid=(features // tile,),
        in_specs=[
            pl.BlockSpec((slots, tokens), lambda i: (0, 0)),
            pl.BlockSpec((tokens, width), lambda i: (0, 0)),
            pl.BlockSpec((tile, width), lambda i: (i, 0)),
        ],
        out_specs=pl.BlockSpec((slots, tokens), lambda i: (0, 0)),
        out_shape=jax.ShapeDtypeStruct((slots, tokens), F32),
        compiler_params=pltpu.CompilerParams(vmem_limit_bytes=VMEM_BYTES),
        cost_estimate=pl.CostEstimate(
            flops=2 * features * width * tokens,
            bytes_accessed=2 * features * width,
            transcendentals=0,
        ),
        name=name,
    )(ids, x, w)


def fill_table(ids_ref, val_ref, table, base, block):
    slots = ids_ref.shape[0]
    cols = slice(block * 128, (block + 1) * 128)
    ids = ids_ref[:, cols]
    iota = lax.broadcasted_iota(jnp.int32, (16, 128), 0).astype(BF16)
    vals = [jnp.broadcast_to(val_ref[j : j + 1, cols], (16, 128)) for j in range(slots)]
    for q in range(table.shape[0] // 256):
        near = jnp.clip(ids - (base + q * 256), -1, 256).astype(BF16)
        away = [jnp.broadcast_to(near[j : j + 1], (16, 128)) - iota for j in range(slots)]
        for g in range(16):
            kept = jnp.zeros((16, 128), BF16)
            for j in range(slots):
                kept = jnp.where(away[j] == 16 * g, vals[j], kept)
            table[q * 256 + g * 16 : q * 256 + (g + 1) * 16, cols] = kept


def grad_kernel(sub, ids_ref, val_ref, y_ref, out_ref, table):
    step = pl.program_id(0)
    tile = out_ref.shape[0]
    for s in range(tile // sub):
        rows = slice(s * sub, (s + 1) * sub)
        for block in range(y_ref.shape[0] // 128):
            fill_table(ids_ref, val_ref, table.at[rows], step * tile + s * sub, block)
        out_ref[rows, :] = jnp.dot(
            table[rows, :], y_ref[...], preferred_element_type=F32
        ).astype(out_ref.dtype)


def grad_rows(ids, val, y, features, name):
    slots, tokens = ids.shape
    width = y.shape[1]
    tile = min(1024, features)
    return pl.pallas_call(
        functools.partial(grad_kernel, min(256, tile)),
        grid=(features // tile,),
        in_specs=[
            pl.BlockSpec((slots, tokens), lambda i: (0, 0)),
            pl.BlockSpec((slots, tokens), lambda i: (0, 0)),
            pl.BlockSpec((tokens, width), lambda i: (0, 0)),
        ],
        out_specs=pl.BlockSpec((tile, width), lambda i: (i, 0)),
        out_shape=jax.ShapeDtypeStruct((features, width), BF16),
        scratch_shapes=[pltpu.VMEM((tile, tokens), BF16)],
        compiler_params=pltpu.CompilerParams(vmem_limit_bytes=VMEM_BYTES),
        cost_estimate=pl.CostEstimate(
            flops=2 * features * width * tokens,
            bytes_accessed=2 * features * width,
            transcendentals=0,
        ),
        name=name,
    )(ids, val, y)


def decode_kernel(sub, ids_ref, val_ref, w_ref, out_ref, table):
    step = pl.program_id(0)
    tile = w_ref.shape[0]

    @pl.when(step == 0)
    def _():
        out_ref[...] = jnp.zeros_like(out_ref)

    for block in range(out_ref.shape[0] // 128):
        for s in range(tile // sub):
            part = table.at[s * sub : (s + 1) * sub]
            fill_table(ids_ref, val_ref, part, step * tile + s * sub, block)
        rows = slice(block * 128, (block + 1) * 128)
        out_ref[rows, :] += lax.dot_general(
            table[:, rows], w_ref[...], (((0,), (0,)), ((), ())), preferred_element_type=F32
        )


def decode(ids, val, w):
    features, width = w.shape
    slots, tokens = ids.shape
    tile = min(1024, features)
    return pl.pallas_call(
        functools.partial(decode_kernel, min(256, tile)),
        grid=(features // tile,),
        in_specs=[
            pl.BlockSpec((slots, tokens), lambda i: (0, 0)),
            pl.BlockSpec((slots, tokens), lambda i: (0, 0)),
            pl.BlockSpec((tile, width), lambda i: (i, 0)),
        ],
        out_specs=pl.BlockSpec((tokens, width), lambda i: (0, 0)),
        out_shape=jax.ShapeDtypeStruct((tokens, width), F32),
        scratch_shapes=[pltpu.VMEM((tile, tokens), BF16)],
        compiler_params=pltpu.CompilerParams(vmem_limit_bytes=VMEM_BYTES),
        cost_estimate=pl.CostEstimate(
            flops=2 * features * width * tokens,
            bytes_accessed=2 * features * width,
            transcendentals=0,
        ),
        name="decode",
    )(ids, val, w)


def bias_kernel(ids_ref, b_ref, out_ref):
    for block in range(out_ref.shape[1] // 128):
        cols = slice(block * 128, (block + 1) * 128)
        ids = ids_ref[:, cols]
        low = ids & 127
        high = ids >> 7
        kept = jnp.zeros(ids.shape, F32)
        for a in range(b_ref.shape[0]):
            row = jnp.broadcast_to(b_ref[a : a + 1, :], ids.shape)
            kept = jnp.where(high == a, jnp.take_along_axis(row, low, axis=1), kept)
        out_ref[:, cols] = kept


def bias_of(ids, bias):
    table = bias.reshape(-1, 128)
    return pl.pallas_call(
        bias_kernel,
        out_shape=jax.ShapeDtypeStruct(ids.shape, F32),
        cost_estimate=pl.CostEstimate(flops=1 << 20, bytes_accessed=1 << 20, transcendentals=0),
        name="bias_of",
    )(ids, table)


def bias_grad_kernel(ids_ref, slope_ref, out_ref):
    slots, tokens = ids_ref.shape
    groups = out_ref.shape[0]
    total = jnp.zeros((groups, 128), F32)
    for j in range(slots):
        ids = ids_ref[j : j + 1, :]
        slope = slope_ref[j : j + 1, :]
        first = slope.astype(BF16).astype(F32)
        second = (slope - first).astype(BF16).astype(F32)
        third = slope - first - second
        high = lax.broadcasted_iota(jnp.int32, (groups, tokens), 0) == (ids >> 7)
        low = lax.broadcasted_iota(jnp.int32, (128, tokens), 0) == (ids & 127)
        low = jnp.where(low, 1.0, 0.0).astype(BF16)
        for part in (first, second, third):
            spread = jnp.where(high, part, 0.0).astype(BF16)
            total = total + lax.dot_general(
                spread, low, (((1,), (1,)), ((), ())), preferred_element_type=F32
            )
    out_ref[...] = total


def bias_grad(ids, slope, features):
    out = pl.pallas_call(
        bias_grad_kernel,
        out_shape=jax.ShapeDtypeStruct((features // 128, 128), F32),
        cost_estimate=pl.CostEstimate(flops=1 << 28, bytes_accessed=1 << 20, transcendentals=0),
        name="bias_grad",
    )(ids, slope)
    return out.reshape(features)


def swap(value, axis, mask):
    size = lax.axis_size(axis)
    return lax.ppermute(value, axis, [(i, i ^ mask) for i in range(size)])


def sum_over(value, axis):
    mask = 1
    while mask < lax.axis_size(axis):
        value = value + swap(value, axis, mask)
        mask *= 2
    return value


def gather_rows(value):
    size = lax.axis_size("seq")
    even = jnp.concatenate([value] + [swap(value, "seq", d) for d in range(2, size, 2)], axis=0)
    return jnp.concatenate([even, swap(even, "seq", 1)], axis=0)


def relative_slots(ids, size):
    slots, tokens = ids.shape
    me = lax.axis_index("seq")
    bits = size.bit_length() - 1
    shaped = ids.reshape((slots,) + (2,) * bits + (tokens // size,))
    for b in range(bits):
        axis = bits - b
        flipped = jnp.flip(shaped, axis)
        shaped = jnp.where((me >> b) & 1 == 1, flipped, shaped)
    shaped = shaped.reshape(slots, size // 2, 2, tokens // size)
    return jnp.swapaxes(shaped, 1, 2).reshape(slots, tokens)


def tree_sum(parts):
    while len(parts) > 1:
        parts = [parts[i] + parts[i + 1] for i in range(0, len(parts), 2)]
    return parts[0]


def skip_columns(inputs, height):
    size, wide = lax.axis_size("seq"), lax.axis_size("tp")
    me, column = lax.axis_index("seq"), lax.axis_index("tp")
    ratio = inputs.shape[1] // height
    pieces = jnp.stack([inputs] + [swap(inputs, "tp", m) for m in range(1, wide)])

    def for_group(mask):
        return lax.dynamic_index_in_dim(pieces, ((me ^ mask) // ratio) ^ column, 0, False)

    even = jnp.concatenate(
        [for_group(0)] + [swap(for_group(d), "seq", d) for d in range(2, size, 2)], axis=0
    )
    mine = lax.dynamic_slice_in_dim(even, (me % 2) * height, height, 1)
    other = lax.dynamic_slice_in_dim(even, (1 - me % 2) * height, height, 1)
    return jnp.concatenate([mine, swap(other, "seq", 1)], axis=0)


def shards(inputs, target, feature_slots, w_enc, b_enc, w_dec, b_dec, w_skip):
    size = lax.axis_size("seq")
    rows = inputs.shape[0]
    half = rows * size // 2
    features = w_enc.shape[0]
    ids = relative_slots(feature_slots[:, 0, :].T, size)
    live = ids >= 0
    all_tokens = gather_rows(inputs)
    skip_inputs = skip_columns(inputs, w_skip.shape[0])

    preact = sum_over(pick(ids, all_tokens, w_enc, "encode"), "tp") + bias_of(ids, b_enc)
    gate = live & (preact > 0.0)
    active = jnp.where(gate, preact, 0.0).astype(BF16)

    terms = decode(ids, active, w_dec)
    terms = terms + jnp.dot(skip_inputs, w_skip, preferred_element_type=F32)
    far = swap(terms[half:].astype(BF16), "seq", 1)
    near = terms[:half] + far.astype(F32)
    sent = near.astype(BF16)
    parts = [near[:rows]] + [
        swap(sent[i * rows : (i + 1) * rows], "seq", 2 * i).astype(F32) for i in range(1, size // 2)
    ]
    predicted = tree_sum(parts) + b_dec
    reconstruction = predicted.astype(BF16)
    residual = (predicted - target.astype(F32)).astype(BF16)

    all_resid = gather_rows(residual)
    slope = sum_over(pick(ids, all_resid, w_dec, "backward"), "tp")
    slope = jnp.where(gate, slope, 0.0)
    grad_dec = grad_rows(ids, active, all_resid, features, "grad_dec")
    grad_enc = grad_rows(ids, slope.astype(BF16), all_tokens, features, "grad_enc")
    grad_benc = bias_grad(ids, slope, features)
    sums = jnp.sum(all_resid.reshape(2, size // 2, rows, -1).astype(F32), axis=2)
    sums = jnp.swapaxes(sums, 0, 1).reshape(size, -1)
    grad_bdec = tree_sum([sums[i] for i in range(size)])
    grad_skip = lax.dot_general(
        skip_inputs, all_resid, (((0,), (0,)), ((), ())), preferred_element_type=F32
    ).astype(BF16)
    return reconstruction, grad_enc, grad_dec, grad_benc, grad_bdec, grad_skip


def solution(mesh):
    in_specs = (
        P("seq", "tp"),
        P("seq", "tp"),
        P(None, "seq", None),
        P("seq", "tp"),
        P("seq"),
        P("seq", "tp"),
        P("tp"),
        P("seq", "tp"),
    )
    out_specs = (P("seq", "tp"), P("seq", "tp"), P("seq", "tp"), P("seq"), P("tp"), P("seq", "tp"))
    return jax.shard_map(shards, mesh=mesh, in_specs=in_specs, out_specs=out_specs, check_vma=False)
```

time: 823 us -> 256 us (0.31)
  local copies, waits for them, and re-layouts: 299 us -> 6.35 us
  other arithmetic: 215 us -> 12.3 us
  Pallas kernels: 0 us -> 144 us
  matrix products: 139 us -> 7.6 us
  blocking collectives: 62.9 us -> 0 us
  starting transfers between devices: 0.56 us -> 26.8 us
  waiting for transfers between devices: 78.2 us -> 57.4 us
  between operations: 14.4 us -> 0.94 us
    gather x8 -> x0, local copies, waits for them, and re-layouts: 218 us -> none  [the longest x2 57.6 us: encode_block(): w_enc[id_rows]]
    pallas_call x0 -> x7, Pallas kernels: none -> 144 us  [the longest x2 59.1 us: grad_rows(): pl.pallas_call(functools.partial(grad_kernel, min(256, tile)), grid=(feat...]
    while x10 -> x0, other arithmetic: 136 us -> none
    dot_general x13 -> x2, matrix products: 139 us -> 7.6 us  [the longest x1 4.32 us: shards(): terms = terms + jnp.dot(skip_inputs, w_skip, preferred_element_type=F32)]
    psum x2 -> x0, blocking collectives: 62.9 us -> none  [the longest x1 32.8 us: shards(): summed_pre = lax.psum(partial_pre, 'tp')]
    ppermute x0 -> x23, waiting for transfers between devices: none -> 57.4 us  [swap(): return lax.ppermute(value, axis, [(i, i ^ mask) for i in range(size)])]
    scatter-add x4 -> x0, local copies, waits for them, and re-layouts: 53.3 us -> none  [the longest x2 26.7 us: grad_block(): act_table = empty_table.at[row_numbers, id_rows].add(act_rows)]
    reduce_scatter x1 -> x0, waiting for transfers between devices: 49.4 us -> none  [shards(): lax.psum_scatter(lax.map(decode_block, jnp.arange(row_count // sub_rows))...]
  transfers between devices with their start and end apart: 4 -> 23, of which waited for: 2 -> 16; matrix products, arithmetic and copies ran while one was open for 16% -> 6% of each run, Pallas kernels for 0% -> 9%
where the time goes in v1:
time: 256 us; the launch traced here: 255 us
  Pallas kernels  144 us (56%)
  waiting for transfers between devices  57.4 us (22%)
  starting transfers between devices  26.8 us (10%)
  other arithmetic  12.3 us (5%)
  matrix products  7.6 us (3%)
  local copies, waits for them, and re-layouts  6.35 us (2%)
    pallas_call x2, Pallas kernels, grad_rows(): pl.pallas_call(functools.partial(grad_kernel, min(256, tile)), grid=(feat...  59.1 us
    ppermute x23, waiting for transfers between devices, swap(): return lax.ppermute(value, axis, [(i, i ^ mask) for i in range(size)])  57.4 us
    pallas_call x2, Pallas kernels, pick(): pl.pallas_call(functools.partial(pick_kernel, min(256, tile)), grid=(feat...  44 us
    pallas_call x1, Pallas kernels, decode(): pl.pallas_call(functools.partial(decode_kernel, min(256, tile)), grid=(fe...  35 us
    ppermute x23, starting transfers between devices, swap(): return lax.ppermute(value, axis, [(i, i ^ mask) for i in range(size)])  26.8 us
  transfers between devices with their start and end apart: 23, of which 16 were waited for; matrix products, arithmetic and copies ran while one was open for 6% of the time, Pallas kernels for 9%

profile of v1, /device:TPU:0, one launch (start us, length us, event | category | flops | bytes accessed | tf_op | source)
XLA Modules:
  0.0 255.1 jit_solution(11494941937683890043)
XLA Ops:
  0.7 3.1 %collective-permute-start.6 = (bf16[128,1024]{1,0:T(8,128)(2,1)}, bf16[128,1024]{1,0:T(8,128)(2,1)}, u32[]{:S(2)}, u32[]{:S(2)}) collective-permute-start(bf16[128,1024]{1,0:T(8,128)(2,1)} %param.8), channel_id=1, source_target_pairs={{0,1},{1,0},{2,3},{3,2},{4,5},{5,4},{6,7},{7,6},{8,9},{9,8},{10,11... | collective-permute-start | bytes 786440 | tf_op jit(solution)/shard_map/ppermute | solution.py:218
  3.8 2.4 collective-permute-start.2
  7.3 2.5 collective-permute-start.8
  10.6 3.5 %collective-permute-done.2 = bf16[128,1024]{1,0:T(8,128)(2,1)S(1)} collective-permute-done((bf16[128,1024]{1,0:T(8,128)(2,1)}, bf16[128,1024]{1,0:T(8,128)(2,1)S(1)}, u32[]{:S(2)}, u32[]{:S(2)}) %collective-permute-start.2) | collective-permute-done | bytes 262176 | tf_op jit(solution)/shard_map/ppermute | solution.py:218
  14.1 2.6 %collective-permute-start.7 = (bf16[128,1024]{1,0:T(8,128)(2,1)}, bf16[128,1024]{1,0:T(8,128)(2,1)}, u32[]{:S(2)}, u32[]{:S(2)}) collective-permute-start(bf16[128,1024]{1,0:T(8,128)(2,1)} %param.8), channel_id=1, source_target_pairs={{0,2},{1,3},{2,0},{3,1},{4,6},{5,7},{6,4},{7,5},{8,10},{9,11},{10,... | collective-permute-start | bytes 786440 | tf_op jit(solution)/shard_map/ppermute | solution.py:218
  21.6 10.7 %collective-permute-done.7 = bf16[128,1024]{1,0:T(8,128)(2,1)} collective-permute-done((bf16[128,1024]{1,0:T(8,128)(2,1)}, bf16[128,1024]{1,0:T(8,128)(2,1)}, u32[]{:S(2)}, u32[]{:S(2)}) %collective-permute-start.7) | collective-permute-done | bytes 262176 | tf_op jit(solution)/shard_map/ppermute | solution.py:218
  33.7 2.5 collective-permute-start.11
  37.3 6.5 %collective-permute-done.11 = bf16[128,1024]{1,0:T(8,128)(2,1)S(1)} collective-permute-done((bf16[128,1024]{1,0:T(8,128)(2,1)S(1)}, bf16[128,1024]{1,0:T(8,128)(2,1)S(1)}, u32[]{:S(2)}, u32[]{:S(2)}) %collective-permute-start.11) | collective-permute-done | bytes 262176 | tf_op jit(solution)/shard_map/ppermute | solution.py:218
  43.8 2.9 %collective-permute-done.10 = bf16[128,1024]{1,0:T(8,128)(2,1)S(1)} collective-permute-done((bf16[128,1024]{1,0:T(8,128)(2,1)S(1)}, bf16[128,1024]{1,0:T(8,128)(2,1)S(1)}, u32[]{:S(2)}, u32[]{:S(2)}) %collective-permute-start.10) | collective-permute-done | bytes 262176 | tf_op jit(solution)/shard_map/ppermute | solution.py:218
  49.4 22.0 %encode.1 = f32[8,1024]{1,0:T(8,128)} custom-call(s32[8,1024]{1,0:T(8,128)} %bitcast.32, bf16[1024,1024]{1,0:T(8,128)(2,1)} %copy-done.16, bf16[8192,1024]{1,0:T(8,128)(2,1)} %w_ref.3), custom_call_target="tpu_custom_call" | custom-call | flops 17179869184 | bytes 16777216 | tf_op jit(solution)/shard_map/encode/pallas_call | solution.py:46
  78.0 4.3 %fusion = f32[1024,1024]{1,0:T(8,128)} fusion(bf16[512,1024]{1,0:T(8,128)(2,1)S(1)} %copy-done, bf16[512,512]{1,0:T(8,128)(2,1)} %collective-permute-done.12, bf16[512,512]{1,0:T(8,128)(2,1)S(1)} %copy-done.11), kind=kOutput, calls=%fused_computation.9 | convolution fusion | flops 1075838976 | bytes 6291456 | tf_op jit(solution)/shard_map/dot_general | solution.py:286
  82.9 35.0 %decode.1 = f32[1024,1024]{1,0:T(8,128)} custom-call(s32[8,1024]{1,0:T(8,128)} %bitcast.34, bf16[8,1024]{1,0:T(8,128)(2,1)} %get-tuple-element.12.val_ref, bf16[8192,1024]{1,0:T(8,128)(2,1)} %w_ref.5), custom_call_target="tpu_custom_call" | custom-call | flops 17179869184 | bytes 16777216 | tf_op jit(solution)/shard_map/decode/pallas_call | solution.py:141
  117.9 4.4 %add.106 = f32[1024,1024]{1,0:T(8,128)S(1)} add(f32[1024,1024]{1,0:T(8,128)} %decode.1, f32[1024,1024]{1,0:T(8,128)} %fusion) | non-fusion elementwise | flops 1048576 | bytes 12582912 | tf_op jit(solution)/shard_map/add | solution.py:286
  122.6 2.6 %collective-permute-done.13 = bf16[512,1024]{1,0:T(8,128)(2,1)S(1)} collective-permute-done((bf16[512,1024]{1,0:T(8,128)(2,1)S(1)}, bf16[512,1024]{1,0:T(8,128)(2,1)S(1)}, u32[]{:S(2)}, u32[]{:S(2)}) %collective-permute-start.13) | collective-permute-done | bytes 1048608 | tf_op jit(solution)/shard_map/ppermute | solution.py:218
  129.3 5.7 %collective-permute-done.14 = bf16[128,1024]{1,0:T(8,128)(2,1)S(1)} collective-permute-done((bf16[128,1024]{1,0:T(8,128)(2,1)S(1)}, bf16[128,1024]{1,0:T(8,128)(2,1)S(1)}, u32[]{:S(2)}, u32[]{:S(2)}) %collective-permute-start.14) | collective-permute-done | bytes 262176 | tf_op jit(solution)/shard_map/ppermute | solution.py:218
  135.0 5.8 %collective-permute-done.16 = bf16[128,1024]{1,0:T(8,128)(2,1)S(1)} collective-permute-done((bf16[128,1024]{1,0:T(8,128)(2,1)S(1)}, bf16[128,1024]{1,0:T(8,128)(2,1)S(1)}, u32[]{:S(2)}, u32[]{:S(2)}) %collective-permute-start.16) | collective-permute-done | bytes 262176 | tf_op jit(solution)/shard_map/ppermute | solution.py:218
  145.9 6.3 %collective-permute-done.19 = bf16[128,1024]{1,0:T(8,128)(2,1)S(1)} collective-permute-done((bf16[128,1024]{1,0:T(8,128)(2,1)S(1)}, bf16[128,1024]{1,0:T(8,128)(2,1)S(1)}, u32[]{:S(2)}, u32[]{:S(2)}) %collective-permute-start.19) | collective-permute-done | bytes 262176 | tf_op jit(solution)/shard_map/ppermute | solution.py:218
  152.2 2.8 %collective-permute-done.18 = bf16[128,1024]{1,0:T(8,128)(2,1)S(1)} collective-permute-done((bf16[128,1024]{1,0:T(8,128)(2,1)S(1)}, bf16[128,1024]{1,0:T(8,128)(2,1)S(1)}, u32[]{:S(2)}, u32[]{:S(2)}) %collective-permute-start.18) | collective-permute-done | bytes 262176 | tf_op jit(solution)/shard_map/ppermute | solution.py:218
  159.2 22.0 %backward.1 = f32[8,1024]{1,0:T(8,128)} custom-call(s32[8,1024]{1,0:T(8,128)} %bitcast.35, bf16[1024,1024]{1,0:T(8,128)(2,1)} %copy-done.2, bf16[8192,1024]{1,0:T(8,128)(2,1)} %w_ref.5), custom_call_target="tpu_custom_call" | custom-call | flops 17179869184 | bytes 16777216 | tf_op jit(solution)/shard_map/backward/pallas_call | solution.py:46
  181.2 29.6 %grad_dec.1 = bf16[8192,1024]{1,0:T(8,128)(2,1)} custom-call(s32[8,1024]{1,0:T(8,128)} %bitcast.36, bf16[8,1024]{1,0:T(8,128)(2,1)} %get-tuple-element.12.val_ref, bf16[1024,1024]{1,0:T(8,128)(2,1)} %copy-done.2), custom_call_target="tpu_custom_call" | custom-call | flops 17179869184 | bytes 16777216 | tf_op jit(solution)/shard_map/grad_dec/pallas_call | solution.py:98
  212.6 3.3 %convolution_convert_fusion = bf16[512,1024]{1,0:T(8,128)(2,1)} fusion(bf16[1024,1024]{1,0:T(8,128)(2,1)S(1)} %copy-done.3, bf16[512,512]{1,0:T(8,128)(2,1)} %collective-permute-done.12, bf16[512,512]{1,0:T(8,128)(2,1)S(1)} %copy-done.11), kind=kOutput, calls=%fused_computation.3 | convolution fusion | flops 1076363264 | bytes 4194304 | tf_op jit(solution)/shard_map/dot_general | solution.py:306
  217.5 3.7 %collective-permute-done.22 = f32[8,1024]{1,0:T(8,128)S(1)} collective-permute-done((f32[8,1024]{1,0:T(8,128)S(1)}, f32[8,1024]{1,0:T(8,128)S(1)}, u32[]{:S(2)}, u32[]{:S(2)}) %collective-permute-start.22) | collective-permute-done | bytes 32800 | tf_op jit(solution)/shard_map/ppermute | solution.py:218
  221.9 3.7 %bias_grad.1 = f32[64,128]{1,0:T(8,128)} custom-call(s32[8,1024]{1,0:T(8,128)} %bitcast.37, f32[8,1024]{1,0:T(8,128)} %get-tuple-element.7.slope_ref), custom_call_target="tpu_custom_call" | custom-call | flops 268435456 | bytes 1048576 | tf_op jit(solution)/shard_map/bias_grad/pallas_call | solution.py:207
  225.6 29.5 %grad_enc.1 = bf16[8192,1024]{1,0:T(8,128)(2,1)} custom-call(s32[8,1024]{1,0:T(8,128)} %bitcast.38, bf16[8,1024]{1,0:T(8,128)(2,1)} %get-tuple-element.6.val_ref, bf16[1024,1024]{1,0:T(8,128)(2,1)} %copy-done.16), custom_call_target="tpu_custom_call" | custom-call | flops 17179869184 | bytes 16777216 | tf_op jit(solution)/shard_map/grad_enc/pallas_call | solution.py:98
  (100 shorter events, 36.7 us)
Async XLA Ops:
  0.6 77.3 %copy-start = (bf16[512,1024]{1,0:T(8,128)(2,1)S(1)}, bf16[512,1024]{1,0:T(8,128)(2,1)}, u32[]{:S(2)}) copy-start(bf16[512,1024]{1,0:T(8,128)(2,1)} %param.15) | copy-start | bytes 3145732
  0.7 20.9 %collective-permute-start.6 = (bf16[128,1024]{1,0:T(8,128)(2,1)}, bf16[128,1024]{1,0:T(8,128)(2,1)}, u32[]{:S(2)}, u32[]{:S(2)}) collective-permute-start(bf16[128,1024]{1,0:T(8,128)(2,1)} %param.8), channel_id=1, source_target_pairs={{0,1},{1,0},{2,3},{3,2},{4,5},{5,4},{6,7},{7,6},{8,9},{9,8},{10,11... | collective-permute-start | bytes 786440 | tf_op jit(solution)/shard_map/ppermute | solution.py:218
  3.8 10.3 %collective-permute-start.2 = (bf16[128,1024]{1,0:T(8,128)(2,1)}, bf16[128,1024]{1,0:T(8,128)(2,1)S(1)}, u32[]{:S(2)}, u32[]{:S(2)}) collective-permute-start(bf16[128,1024]{1,0:T(8,128)(2,1)} %param.8), channel_id=1, source_target_pairs={{0,24},{4,28},{8,16},{12,20},{16,8},{20,12},{24,0},{28,4},{1,25},{... | collective-permute-start | bytes 786440 | tf_op jit(solution)/shard_map/ppermute | solution.py:218
  6.2 12.0 %collective-permute-start.1 = (bf16[128,1024]{1,0:T(8,128)(2,1)}, bf16[128,1024]{1,0:T(8,128)(2,1)S(1)}, u32[]{:S(2)}, u32[]{:S(2)}) collective-permute-start(bf16[128,1024]{1,0:T(8,128)(2,1)} %param.8), channel_id=1, source_target_pairs={{0,16},{4,20},{8,24},{12,28},{16,0},{20,4},{24,8},{28,12},{1,17},{... | collective-permute-start | bytes 786440 | tf_op jit(solution)/shard_map/ppermute | solution.py:218
  6.7 11.6 %collective-permute-start = (bf16[128,1024]{1,0:T(8,128)(2,1)}, bf16[128,1024]{1,0:T(8,128)(2,1)S(1)}, u32[]{:S(2)}, u32[]{:S(2)}) collective-permute-start(bf16[128,1024]{1,0:T(8,128)(2,1)} %param.8), channel_id=1, source_target_pairs={{0,8},{4,12},{8,0},{12,4},{16,24},{20,28},{24,16},{28,20},{1,9},{5... | collective-permute-start | bytes 786440 | tf_op jit(solution)/shard_map/ppermute | solution.py:218
  7.3 14.3 %collective-permute-start.8 = (bf16[128,1024]{1,0:T(8,128)(2,1)}, bf16[128,1024]{1,0:T(8,128)(2,1)}, u32[]{:S(2)}, u32[]{:S(2)}) collective-permute-start(bf16[128,1024]{1,0:T(8,128)(2,1)} %param.8), channel_id=1, source_target_pairs={{0,3},{1,2},{2,1},{3,0},{4,7},{5,6},{6,5},{7,4},{8,11},{9,10},{10,... | collective-permute-start | bytes 786440 | tf_op jit(solution)/shard_map/ppermute | solution.py:218
  14.1 18.1 %collective-permute-start.7 = (bf16[128,1024]{1,0:T(8,128)(2,1)}, bf16[128,1024]{1,0:T(8,128)(2,1)}, u32[]{:S(2)}, u32[]{:S(2)}) collective-permute-start(bf16[128,1024]{1,0:T(8,128)(2,1)} %param.8), channel_id=1, source_target_pairs={{0,2},{1,3},{2,0},{3,1},{4,6},{5,7},{6,4},{7,5},{8,10},{9,11},{10,... | collective-permute-start | bytes 786440 | tf_op jit(solution)/shard_map/ppermute | solution.py:218
  20.7 27.3 %collective-permute-start.3 = (bf16[512,1024]{1,0:T(8,128)(2,1)S(1)}, bf16[512,1024]{1,0:T(8,128)(2,1)S(1)}, u32[]{:S(2)}, u32[]{:S(2)}) collective-permute-start(bf16[512,1024]{1,0:T(8,128)(2,1)S(1)} %pad_maximum_fusion), channel_id=1, source_target_pairs={{0,4},{4,0},{8,12},{12,8},{16,20},{20,16},{24,28},{28,24},{1,5},{5... | collective-permute-start | bytes 3145736 | tf_op jit(solution)/shard_map/ppermute | solution.py:218
  33.7 10.2 %collective-permute-start.11 = (bf16[128,1024]{1,0:T(8,128)(2,1)S(1)}, bf16[128,1024]{1,0:T(8,128)(2,1)S(1)}, u32[]{:S(2)}, u32[]{:S(2)}) collective-permute-start(bf16[128,1024]{1,0:T(8,128)(2,1)S(1)} %get-tuple-element.20), channel_id=1, source_target_pairs={{0,24},{4,28},{8,16},{12,20},{16,8},{20,12},{24,0},{28,4},{1,25},{... | collective-permute-start | bytes 786440 | tf_op jit(solution)/shard_map/ppermute | solution.py:218
  36.2 10.6 %collective-permute-start.10 = (bf16[128,1024]{1,0:T(8,128)(2,1)S(1)}, bf16[128,1024]{1,0:T(8,128)(2,1)S(1)}, u32[]{:S(2)}, u32[]{:S(2)}) collective-permute-start(bf16[128,1024]{1,0:T(8,128)(2,1)S(1)} %get-tuple-element.21), channel_id=1, source_target_pairs={{0,16},{4,20},{8,24},{12,28},{16,0},{20,4},{24,8},{28,12},{1,17},{... | collective-permute-start | bytes 786440 | tf_op jit(solution)/shard_map/ppermute | solution.py:218
  36.7 10.2 %collective-permute-start.9 = (bf16[128,1024]{1,0:T(8,128)(2,1)S(1)}, bf16[128,1024]{1,0:T(8,128)(2,1)S(1)}, u32[]{:S(2)}, u32[]{:S(2)}) collective-permute-start(bf16[128,1024]{1,0:T(8,128)(2,1)S(1)} %get-tuple-element.22), channel_id=1, source_target_pairs={{0,8},{4,12},{8,0},{12,4},{16,24},{20,28},{24,16},{28,20},{1,9},{5... | collective-permute-start | bytes 786440 | tf_op jit(solution)/shard_map/ppermute | solution.py:218
  48.0 30.0 %collective-permute-start.12 = (bf16[512,512]{1,0:T(8,128)(2,1)}, bf16[512,512]{1,0:T(8,128)(2,1)}, u32[]{:S(2)}, u32[]{:S(2)}) collective-permute-start(bf16[512,512]{1,0:T(8,128)(2,1)} %get-tuple-element.18), channel_id=1, source_target_pairs={{0,4},{4,0},{8,12},{12,8},{16,20},{20,16},{24,28},{28,24},{1,5},{5... | collective-permute-start | bytes 1572872 | tf_op jit(solution)/shard_map/ppermute | solution.py:218
  71.5 4.1 %collective-permute-start.4 = (f32[8,1024]{1,0:T(8,128)}, f32[8,1024]{1,0:T(8,128)S(1)}, u32[]{:S(2)}, u32[]{:S(2)}) collective-permute-start(f32[8,1024]{1,0:T(8,128)} %encode.1), channel_id=1, source_target_pairs={{0,1},{1,0},{2,3},{3,2},{4,5},{5,4},{6,7},{7,6},{8,9},{9,8},{10,11... | collective-permute-start | bytes 98312 | tf_op jit(solution)/shard_map/ppermute | solution.py:218
  76.3 6.0 %collective-permute-start.5 = (f32[8,1024]{1,0:T(8,128)S(1)}, f32[8,1024]{1,0:T(8,128)S(1)}, u32[]{:S(2)}, u32[]{:S(2)}) collective-permute-start(f32[8,1024]{1,0:T(8,128)S(1)} %add.96), channel_id=1, source_target_pairs={{0,2},{1,3},{2,0},{3,1},{4,6},{5,7},{6,4},{7,5},{8,10},{9,11},{10,... | collective-permute-start | bytes 98312 | tf_op jit(solution)/shard_map/ppermute | solution.py:218
  122.5 2.7 %collective-permute-start.13 = (bf16[512,1024]{1,0:T(8,128)(2,1)S(1)}, bf16[512,1024]{1,0:T(8,128)(2,1)S(1)}, u32[]{:S(2)}, u32[]{:S(2)}) collective-permute-start(bf16[512,1024]{1,0:T(8,128)(2,1)S(1)} %slice.102), channel_id=1, source_target_pairs={{0,4},{4,0},{8,12},{12,8},{16,20},{20,16},{24,28},{28,24},{1,5},{5... | collective-permute-start | bytes 3145736 | tf_op jit(solution)/shard_map/ppermute | solution.py:218
  125.7 9.2 %collective-permute-start.14 = (bf16[128,1024]{1,0:T(8,128)(2,1)S(1)}, bf16[128,1024]{1,0:T(8,128)(2,1)S(1)}, u32[]{:S(2)}, u32[]{:S(2)}) collective-permute-start(bf16[128,1024]{1,0:T(8,128)(2,1)S(1)} %get-tuple-element.14), channel_id=1, source_target_pairs={{0,8},{4,12},{8,0},{12,4},{16,24},{20,28},{24,16},{28,20},{1,9},{5... | collective-permute-start | bytes 786440 | tf_op jit(solution)/shard_map/ppermute | solution.py:218
  127.3 13.4 %collective-permute-start.16 = (bf16[128,1024]{1,0:T(8,128)(2,1)S(1)}, bf16[128,1024]{1,0:T(8,128)(2,1)S(1)}, u32[]{:S(2)}, u32[]{:S(2)}) collective-permute-start(bf16[128,1024]{1,0:T(8,128)(2,1)S(1)} %get-tuple-element.15), channel_id=1, source_target_pairs={{0,24},{4,28},{8,16},{12,20},{16,8},{20,12},{24,0},{28,4},{1,25},{... | collective-permute-start | bytes 786440 | tf_op jit(solution)/shard_map/ppermute | solution.py:218
  128.7 13.4 %collective-permute-start.15 = (bf16[128,1024]{1,0:T(8,128)(2,1)S(1)}, bf16[128,1024]{1,0:T(8,128)(2,1)S(1)}, u32[]{:S(2)}, u32[]{:S(2)}) collective-permute-start(bf16[128,1024]{1,0:T(8,128)(2,1)S(1)} %get-tuple-element.16), channel_id=1, source_target_pairs={{0,16},{4,20},{8,24},{12,28},{16,0},{20,4},{24,8},{28,12},{1,17},{... | collective-permute-start | bytes 786440 | tf_op jit(solution)/shard_map/ppermute | solution.py:218
  142.3 9.9 %collective-permute-start.19 = (bf16[128,1024]{1,0:T(8,128)(2,1)S(1)}, bf16[128,1024]{1,0:T(8,128)(2,1)S(1)}, u32[]{:S(2)}, u32[]{:S(2)}) collective-permute-start(bf16[128,1024]{1,0:T(8,128)(2,1)S(1)} %get-tuple-element.9), channel_id=1, source_target_pairs={{0,24},{4,28},{8,16},{12,20},{16,8},{20,12},{24,0},{28,4},{1,25},{... | collective-permute-start | bytes 786440 | tf_op jit(solution)/shard_map/ppermute | solution.py:218
  143.9 11.1 %collective-permute-start.18 = (bf16[128,1024]{1,0:T(8,128)(2,1)S(1)}, bf16[128,1024]{1,0:T(8,128)(2,1)S(1)}, u32[]{:S(2)}, u32[]{:S(2)}) collective-permute-start(bf16[128,1024]{1,0:T(8,128)(2,1)S(1)} %get-tuple-element.9), channel_id=1, source_target_pairs={{0,16},{4,20},{8,24},{12,28},{16,0},{20,4},{24,8},{28,12},{1,17},{... | collective-permute-start | bytes 786440 | tf_op jit(solution)/shard_map/ppermute | solution.py:218
  144.7 10.3 %collective-permute-start.17 = (bf16[128,1024]{1,0:T(8,128)(2,1)S(1)}, bf16[128,1024]{1,0:T(8,128)(2,1)S(1)}, u32[]{:S(2)}, u32[]{:S(2)}) collective-permute-start(bf16[128,1024]{1,0:T(8,128)(2,1)S(1)} %get-tuple-element.9), channel_id=1, source_target_pairs={{0,8},{4,12},{8,0},{12,4},{16,24},{20,28},{24,16},{28,20},{1,9},{5... | collective-permute-start | bytes 786440 | tf_op jit(solution)/shard_map/ppermute | solution.py:218
  155.1 2.7 %collective-permute-start.20 = (bf16[512,1024]{1,0:T(8,128)(2,1)S(1)}, bf16[512,1024]{1,0:T(8,128)(2,1)S(1)}, u32[]{:S(2)}, u32[]{:S(2)}) collective-permute-start(bf16[512,1024]{1,0:T(8,128)(2,1)S(1)} %pad_maximum_fusion.4), channel_id=1, source_target_pairs={{0,4},{4,0},{8,12},{12,8},{16,20},{20,16},{24,28},{28,24},{1,5},{5... | collective-permute-start | bytes 3145736 | tf_op jit(solution)/shard_map/ppermute | solution.py:218
  210.8 5.6 %collective-permute-start.21 = (f32[8,1024]{1,0:T(8,128)S(1)}, f32[8,1024]{1,0:T(8,128)S(1)}, u32[]{:S(2)}, u32[]{:S(2)}) collective-permute-start(f32[8,1024]{1,0:T(8,128)S(1)} %copy-done.15), channel_id=1, source_target_pairs={{0,1},{1,0},{2,3},{3,2},{4,5},{5,4},{6,7},{7,6},{8,9},{9,8},{10,11... | collective-permute-start | bytes 98312 | tf_op jit(solution)/shard_map/ppermute | solution.py:218
  216.4 4.9 %collective-permute-start.22 = (f32[8,1024]{1,0:T(8,128)S(1)}, f32[8,1024]{1,0:T(8,128)S(1)}, u32[]{:S(2)}, u32[]{:S(2)}) collective-permute-start(f32[8,1024]{1,0:T(8,128)S(1)} %add.113), channel_id=1, source_target_pairs={{0,2},{1,3},{2,0},{3,1},{4,6},{5,7},{6,4},{7,5},{8,10},{9,11},{10,... | collective-permute-start | bytes 98312 | tf_op jit(solution)/shard_map/ppermute | solution.py:218
  (17 other events, 209.9 us)

commit v2 on v1

v2 whole, which is shorter than its diff:
```python
import functools

import jax
import jax.numpy as jnp
from jax import lax
from jax.experimental import pallas as pl
from jax.experimental.pallas import tpu as pltpu
from jax.sharding import PartitionSpec as P

VMEM_BYTES = 60 << 20
F32 = jnp.float32
BF16 = jnp.bfloat16
GRAD_WIDE = 256
DECODE_WIDE = 256


def whole(i):
    return (0, 0)


def params():
    return pltpu.CompilerParams(vmem_limit_bytes=VMEM_BYTES)


def cost(features, width, tokens):
    return pl.CostEstimate(
        flops=2 * features * width * tokens,
        bytes_accessed=2 * features * width,
        transcendentals=0,
    )


def lay_out(pieces, rows_ref):
    first = 0
    for piece in pieces:
        rows_ref[first : first + piece.shape[0], :] = piece[...]
        first += piece.shape[0]


def tree_sum(parts):
    while len(parts) > 1:
        parts = [parts[i] + parts[i + 1] for i in range(0, len(parts), 2)]
    return parts[0]


def pick_kernel(sub, count, ids_ref, w_ref, *refs):
    pieces, out_ref, rows_ref = refs[:count], refs[count], refs[count + 1]
    step = pl.program_id(0)
    tile = w_ref.shape[0]

    @pl.when(step == 0)
    def _():
        out_ref[...] = jnp.zeros_like(out_ref)
        lay_out(pieces, rows_ref)

    for s in range(tile // sub):
        dots = lax.dot_general(
            w_ref[s * sub : (s + 1) * sub, :],
            rows_ref[...],
            (((1,), (1,)), ((), ())),
            preferred_element_type=F32,
        )
        for block in range(out_ref.shape[1] // 128):
            cols = slice(block * 128, (block + 1) * 128)
            ids = ids_ref[:, cols]
            low = ids & 7
            high = (ids >> 3) - (step * (tile // 8) + s * (sub // 8))
            kept = out_ref[:, cols]
            for g in range(sub // 8):
                found = jnp.take_along_axis(dots[g * 8 : (g + 1) * 8, cols], low, axis=0)
                kept = jnp.where(high == g, found, kept)
            out_ref[:, cols] = kept


def pick(ids, pieces, w, name):
    features, width = w.shape
    slots, tokens = ids.shape
    tile = min(1024, features)
    return pl.pallas_call(
        functools.partial(pick_kernel, min(256, tile), len(pieces)),
        grid=(features // tile,),
        in_specs=[
            pl.BlockSpec((slots, tokens), whole),
            pl.BlockSpec((tile, width), lambda i: (i, 0)),
        ]
        + [pl.BlockSpec(piece.shape, whole) for piece in pieces],
        out_specs=pl.BlockSpec((slots, tokens), whole),
        out_shape=jax.ShapeDtypeStruct((slots, tokens), F32),
        scratch_shapes=[pltpu.VMEM((tokens, width), BF16)],
        compiler_params=params(),
        cost_estimate=cost(features, width, tokens),
        name=name,
    )(ids, w, *pieces)


def slots_at(ids_ref, val_ref, block):
    slots = ids_ref.shape[0]
    cols = slice(block * 128, (block + 1) * 128)
    vals = [jnp.broadcast_to(val_ref[j : j + 1, cols], (16, 128)) for j in range(slots)]
    return ids_ref[:, cols], vals


def table_part(ids, vals, base):
    slots = len(vals)
    iota = lax.broadcasted_iota(jnp.int32, (16, 128), 0).astype(BF16)
    near = jnp.clip(ids - base, -1, 256).astype(BF16)
    away = [jnp.broadcast_to(near[j : j + 1], (16, 128)) - iota for j in range(slots)]
    part = []
    for g in range(16):
        kept = jnp.zeros((16, 128), BF16)
        for j in range(slots):
            kept = jnp.where(away[j] == 16 * g, vals[j], kept)
        part.append(kept)
    return part


def grad_kernel(sub, wide, count, ids_ref, val_ref, *refs):
    pieces, out_ref, rows_ref, tables = refs[:count], refs[count], refs[count + 1], refs[count + 2 :]
    step = pl.program_id(0)
    tile, width = out_ref.shape
    blocks = ids_ref.shape[1] // 128
    subs = tile // sub
    chunks = width // wide

    def build(table, number, some):
        for block in some:
            cols = slice(block * 128, (block + 1) * 128)
            ids, vals = slots_at(ids_ref, val_ref, block)
            for q in range(sub // 256):
                part = table_part(ids, vals, number * sub + q * 256)
                for g in range(16):
                    first = q * 256 + g * 16
                    table[first : first + 16, cols] = part[g]

    @pl.when(step == 0)
    def _():
        lay_out(pieces, rows_ref)
        build(tables[0], 0, range(blocks))

    for s in range(subs):
        here, after = tables[s % 2], tables[(s + 1) % 2]
        for n in range(chunks):
            cols = slice(n * wide, (n + 1) * wide)
            out_ref[s * sub : (s + 1) * sub, cols] = jnp.dot(
                here[...], rows_ref[:, cols], preferred_element_type=F32
            ).astype(out_ref.dtype)
            some = range(n * blocks // chunks, (n + 1) * blocks // chunks)
            build(after, step * subs + s + 1, some)


def grad_rows(ids, val, pieces, features, name):
    slots, tokens = ids.shape
    width = pieces[0].shape[1]
    tile, sub = min(1024, features), 256
    assert (tile // sub) % 2 == 0
    return pl.pallas_call(
        functools.partial(grad_kernel, sub, min(GRAD_WIDE, width), len(pieces)),
        grid=(features // tile,),
        in_specs=[pl.BlockSpec((slots, tokens), whole)] * 2
        + [pl.BlockSpec(piece.shape, whole) for piece in pieces],
        out_specs=pl.BlockSpec((tile, width), lambda i: (i, 0)),
        out_shape=jax.ShapeDtypeStruct((features, width), BF16),
        scratch_shapes=[pltpu.VMEM((tokens, width), BF16)]
        + [pltpu.VMEM((sub, tokens), BF16)] * 2,
        compiler_params=params(),
        cost_estimate=cost(features, width, tokens),
        name=name,
    )(ids, val, *pieces)


def decode_kernel(sub, wide, ids_ref, val_ref, w_ref, keep_ref, send_ref, total, *tables):
    step = pl.program_id(0)
    tile, width = w_ref.shape
    tokens = ids_ref.shape[1]
    subs = tokens // sub
    chunks = width // wide
    work = [(b, q) for b in range(sub // 128) for q in range(tile // 256)]

    def build(table, number, base, n):
        for b, q in work[n * len(work) // chunks : (n + 1) * len(work) // chunks]:
            ids, vals = slots_at(ids_ref, val_ref, number * (sub // 128) + b)
            part = table_part(ids, vals, base + q * 256)
            table[b * 128 : (b + 1) * 128, q * 256 : (q + 1) * 256] = jnp.concatenate(
                part, axis=0
            ).T

    @pl.when(step == 0)
    def _():
        total[...] = jnp.zeros_like(total)
        for n in range(chunks):
            build(tables[0], 0, 0, n)

    for s in range(subs):
        following = (s + 1) % subs
        here, after = tables[s % len(tables)], tables[following % len(tables)]
        base = (step + (s + 1) // subs) * tile
        rows = slice(s * sub, (s + 1) * sub)
        for n in range(chunks):
            cols = slice(n * wide, (n + 1) * wide)
            total[rows, cols] += jnp.dot(here[...], w_ref[:, cols], preferred_element_type=F32)
            build(after, following, base, n)

    @pl.when(step == pl.num_programs(0) - 1)
    def _():
        half = tokens // 2
        keep_ref[...] = total[:half, :]
        send_ref[...] = total[half:, :].astype(BF16)


def decode(ids, val, w, name):
    features, width = w.shape
    slots, tokens = ids.shape
    tile = min(1024, features)
    sub = min(256, tokens // 2)
    subs = tokens // sub
    half = (tokens // 2, width)
    return pl.pallas_call(
        functools.partial(decode_kernel, sub, min(DECODE_WIDE, width)),
        grid=(features // tile,),
        in_specs=[pl.BlockSpec((slots, tokens), whole)] * 2
        + [pl.BlockSpec((tile, width), lambda i: (i, 0))],
        out_specs=[pl.BlockSpec(half, whole)] * 2,
        out_shape=[jax.ShapeDtypeStruct(half, F32), jax.ShapeDtypeStruct(half, BF16)],
        scratch_shapes=[pltpu.VMEM((tokens, width), F32)]
        + [pltpu.VMEM((sub, tile), BF16)] * (2 if subs % 2 == 0 else subs),
        compiler_params=params(),
        cost_estimate=cost(features, width, tokens),
        name=name,
    )(ids, val, w)


def bias_kernel(ids_ref, b_ref, out_ref):
    for block in range(out_ref.shape[1] // 128):
        cols = slice(block * 128, (block + 1) * 128)
        ids = ids_ref[:, cols]
        low = ids & 127
        high = ids >> 7
        kept = jnp.zeros(ids.shape, F32)
        for a in range(b_ref.shape[0]):
            row = jnp.broadcast_to(b_ref[a : a + 1, :], ids.shape)
            kept = jnp.where(high == a, jnp.take_along_axis(row, low, axis=1), kept)
        out_ref[:, cols] = kept


def bias_of(ids, bias):
    table = bias.reshape(-1, 128)
    return pl.pallas_call(
        bias_kernel,
        out_shape=jax.ShapeDtypeStruct(ids.shape, F32),
        cost_estimate=pl.CostEstimate(flops=1 << 20, bytes_accessed=1 << 20, transcendentals=0),
        name="bias_of",
    )(ids, table)


def bias_grad_kernel(ids_ref, slope_ref, out_ref):
    slots, tokens = ids_ref.shape
    groups = out_ref.shape[0]
    total = jnp.zeros((3 * groups, 128), F32)
    for j in range(slots):
        ids = ids_ref[j : j + 1, :]
        slope = slope_ref[j : j + 1, :]
        first = slope.astype(BF16).astype(F32)
        second = (slope - first).astype(BF16).astype(F32)
        third = slope - first - second
        high = lax.broadcasted_iota(jnp.int32, (groups, tokens), 0) == (ids >> 7)
        low = lax.broadcasted_iota(jnp.int32, (128, tokens), 0) == (ids & 127)
        low = jnp.where(low, 1.0, 0.0).astype(BF16)
        spread = jnp.concatenate(
            [jnp.where(high, part, 0.0) for part in (first, second, third)], axis=0
        ).astype(BF16)
        total = total + lax.dot_general(
            spread, low, (((1,), (1,)), ((), ())), preferred_element_type=F32
        )
    out_ref[...] = total[:groups] + total[groups : 2 * groups] + total[2 * groups :]


def bias_grad(ids, slope, features):
    out = pl.pallas_call(
        bias_grad_kernel,
        out_shape=jax.ShapeDtypeStruct((features // 128, 128), F32),
        cost_estimate=pl.CostEstimate(flops=1 << 28, bytes_accessed=1 << 20, transcendentals=0),
        name="bias_grad",
    )(ids, slope)
    return out.reshape(features)


def skip_grad_kernel(count, *refs):
    columns, resid = refs[:count], refs[count : 2 * count]
    out_ref, sum_ref, left, right = refs[2 * count :]
    lay_out(columns, left)
    lay_out(resid, right)
    out_ref[...] = lax.dot_general(
        left[...], right[...], (((0,), (0,)), ((), ())), preferred_element_type=F32
    ).astype(BF16)
    sums = [jnp.sum(piece[...].astype(F32), axis=0, keepdims=True) for piece in resid]
    order = piece_order(count)
    sum_ref[...] = tree_sum([sums[order.index(d)] for d in range(count)])


def skip_grad(columns, resid):
    rows, width = resid[0].shape
    height = columns[0].shape[1]
    count = len(resid)
    out, sums = pl.pallas_call(
        functools.partial(skip_grad_kernel, count),
        out_shape=[
            jax.ShapeDtypeStruct((height, width), BF16),
            jax.ShapeDtypeStruct((1, width), F32),
        ],
        scratch_shapes=[
            pltpu.VMEM((count * rows, height), BF16),
            pltpu.VMEM((count * rows, width), BF16),
        ],
        compiler_params=params(),
        cost_estimate=cost(height, width, count * rows),
        name="skip_grad",
    )(*columns, *resid)
    return out, sums.reshape(width)


def swap(value, axis, mask):
    size = lax.axis_size(axis)
    return lax.ppermute(value, axis, [(i, i ^ mask) for i in range(size)])


def sum_over(value, axis):
    mask = 1
    while mask < lax.axis_size(axis):
        value = value + swap(value, axis, mask)
        mask *= 2
    return value


def piece_order(size):
    return [0, 1] + list(range(2, size, 2)) + list(range(3, size, 2))


def exchange(value):
    size = lax.axis_size("seq")
    near = [value, swap(value, "seq", 1)]
    even = [swap(value, "seq", d) for d in range(2, size, 2)]
    return near, even + [swap(piece, "seq", 1) for piece in even]


def relative_slots(ids, size):
    slots, tokens = ids.shape
    me = lax.axis_index("seq")
    bits = size.bit_length() - 1
    shaped = ids.reshape((slots,) + (2,) * bits + (tokens // size,))
    for b in range(bits):
        axis = bits - b
        flipped = jnp.flip(shaped, axis)
        shaped = jnp.where((me >> b) & 1 == 1, flipped, shaped)
    shaped = shaped.reshape(slots, size, tokens // size)
    return jnp.concatenate([shaped[:, d] for d in piece_order(size)], axis=1)


def skip_groups(inputs, height, after):
    size, wide = lax.axis_size("seq"), lax.axis_size("tp")
    me, column = lax.axis_index("seq"), lax.axis_index("tp")
    assert 2 * height == inputs.shape[1]
    pieces = jnp.stack([inputs] + [swap(inputs, "tp", m) for m in range(1, wide)])
    pieces, after = lax.optimization_barrier((pieces, after))

    def for_group(mask):
        return lax.dynamic_index_in_dim(pieces, ((me ^ mask) // 2) ^ column, 0, False)

    groups = [for_group(0)] + [swap(for_group(d), "seq", d) for d in range(2, size, 2)]
    return groups, after


def shards(inputs, target, feature_slots, w_enc, b_enc, w_dec, b_dec, w_skip):
    size = lax.axis_size("seq")
    me = lax.axis_index("seq")
    rows = inputs.shape[0]
    features = w_enc.shape[0]
    height = w_skip.shape[0]
    ids = relative_slots(feature_slots[:, 0, :].T, size)
    near_ids, far_ids = ids[:, : 2 * rows], ids[:, 2 * rows :]
    live = ids >= 0

    other_skip = swap(w_skip, "seq", 1)
    near_tokens, far_tokens = exchange(inputs)
    near_pre = pick(near_ids, near_tokens, w_enc, "encode_near")
    far_pre = pick(far_ids, far_tokens, w_enc, "encode_far")
    groups, far_pre = skip_groups(inputs, height, far_pre)
    preact = sum_over(jnp.concatenate([near_pre, far_pre], axis=1), "tp") + bias_of(ids, b_enc)
    gate = live & (preact > 0.0)
    active = jnp.where(gate, preact, 0.0).astype(BF16)

    far_keep, far_send = decode(far_ids, active[:, 2 * rows :], w_dec, "decode_far")
    group = jnp.concatenate(groups, axis=0)
    mine = lax.dynamic_slice_in_dim(group, (me % 2) * height, height, 1)
    other = lax.dynamic_slice_in_dim(group, (1 - me % 2) * height, height, 1)
    skip = jnp.dot(mine, w_skip, preferred_element_type=F32) + jnp.dot(
        other, other_skip, preferred_element_type=F32
    )
    sent = (far_keep + swap(far_send, "seq", 1).astype(F32) + skip[rows:]).astype(BF16)
    near_active, sent = lax.optimization_barrier((active[:, : 2 * rows], sent))
    near_keep, near_send = decode(near_ids, near_active, w_dec, "decode_near")
    parts = [near_keep + swap(near_send, "seq", 1).astype(F32) + skip[:rows]] + [
        swap(sent[i * rows : (i + 1) * rows], "seq", 2 * i + 2).astype(F32)
        for i in range(size // 2 - 1)
    ]
    predicted = tree_sum(parts) + b_dec
    reconstruction = predicted.astype(BF16)
    residual = (predicted - target.astype(F32)).astype(BF16)

    near_resid, far_resid = exchange(residual)
    near_slope = pick(near_ids, near_resid, w_dec, "backward_near")
    far_slope = pick(far_ids, far_resid, w_dec, "backward_far")
    slope = sum_over(jnp.concatenate([near_slope, far_slope], axis=1), "tp")
    slope = jnp.where(gate, slope, 0.0)
    resid = near_resid + far_resid
    grad_dec = grad_rows(ids, active, resid, features, "grad_dec")
    grad_enc = grad_rows(ids, slope.astype(BF16), near_tokens + far_tokens, features, "grad_enc")
    grad_benc = bias_grad(ids, slope, features)
    mine = [mine[i * rows : (i + 1) * rows] for i in range(size // 2)]
    others = swap(other, "seq", 1)
    others = [others[i * rows : (i + 1) * rows] for i in range(size // 2)]
    columns = [mine[0], others[0]] + mine[1:] + others[1:]
    grad_skip, grad_bdec = skip_grad(columns, resid)
    return reconstruction, grad_enc, grad_dec, grad_benc, grad_bdec, grad_skip


def solution(mesh):
    in_specs = (
        P("seq", "tp"),
        P("seq", "tp"),
        P(None, "seq", None),
        P("seq", "tp"),
        P("seq"),
        P("seq", "tp"),
        P("tp"),
        P("seq", "tp"),
    )
    out_specs = (P("seq", "tp"), P("seq", "tp"), P("seq", "tp"), P("seq"), P("tp"), P("seq", "tp"))
    return jax.shard_map(shards, mesh=mesh, in_specs=in_specs, out_specs=out_specs, check_vma=False)
```

time: 256 us -> 245 us (0.957)
  waiting for transfers between devices: 57.4 us -> 22.2 us
  Pallas kernels: 144 us -> 156 us
  starting transfers between devices: 26.8 us -> 37.8 us
  local copies, waits for them, and re-layouts: 6.35 us -> 13.2 us
  matrix products: 7.6 us -> 2.58 us
    ppermute x23 -> x31, waiting for transfers between devices: 57.4 us -> 22.2 us  [swap(): return lax.ppermute(value, axis, [(i, i ^ mask) for i in range(size)])]
    pallas_call x5 -> x9, Pallas kernels: 138 us -> 152 us  [the longest x4 58.3 us: pick(): pl.pallas_call(functools.partial(pick_kernel, min(256, tile), len(pieces)...]
    ppermute x23 -> x31, starting transfers between devices: 26.8 us -> 37.8 us  [swap(): return lax.ppermute(value, axis, [(i, i ^ mask) for i in range(size)])]
    dot_general x2, matrix products: 7.6 us -> 2.58 us  [the longest x1 1.84 us: shards(): jnp.dot(other, other_skip, preferred_element_type=F32)]
    add x2 -> x0, other arithmetic: 5.01 us -> none  [the longest x1 4.4 us: shards(): terms = terms + jnp.dot(skip_inputs, w_skip, preferred_element_type=F32)]
    slice x1 -> x4, local copies, waits for them, and re-layouts: 0.15 us -> 3.91 us  [the longest x1 1.91 us: shards(): others = [others[i * rows:(i + 1) * rows] for i in range(size // 2)]]
    unnamed x43 -> x62, local copies, waits for them, and re-layouts: 4.17 us -> 5.65 us
  transfers between devices with their start and end apart: 23 -> 31, of which waited for: 16 -> 10; matrix products, arithmetic and copies ran while one was open for 6% -> 7% of each run, Pallas kernels for 9% -> 39%
where the time goes in v2:
time: 245 us; the launch traced here: 243 us
  Pallas kernels  156 us (64%)
  starting transfers between devices  37.8 us (15%)
  waiting for transfers between devices  22.2 us (9%)
  local copies, waits for them, and re-layouts  13.2 us (5%)
  other arithmetic  10.3 us (4%)
  matrix products  2.58 us (1%)
    pallas_call x4, Pallas kernels, pick(): pl.pallas_call(functools.partial(pick_kernel, min(256, tile), len(pieces)...  58.3 us
    pallas_call x2, Pallas kernels, grad_rows(): pl.pallas_call(functools.partial(grad_kernel, sub, min(GRAD_WIDE, width),...  55.8 us
    ppermute x31, starting transfers between devices, swap(): return lax.ppermute(value, axis, [(i, i ^ mask) for i in range(size)])  37.8 us
    pallas_call x2, Pallas kernels, decode(): pl.pallas_call(functools.partial(decode_kernel, sub, min(DECODE_WIDE, wid...  33.6 us
    ppermute x31, waiting for transfers between devices, swap(): return lax.ppermute(value, axis, [(i, i ^ mask) for i in range(size)])  22.2 us
    unnamed x62, local copies, waits for them, and re-layouts  5.65 us
  transfers between devices with their start and end apart: 31, of which 10 were waited for; matrix products, arithmetic and copies ran while one was open for 7% of the time, Pallas kernels for 39%

profile of v2, /device:TPU:0, one launch (start us, length us, event | category | flops | bytes accessed | tf_op | source)
XLA Modules:
  0.0 243.5 jit_solution(3046995901232943282)
XLA Ops:
  0.6 3.1 %collective-permute-start.5 = (bf16[128,1024]{1,0:T(8,128)(2,1)}, bf16[128,1024]{1,0:T(8,128)(2,1)}, u32[]{:S(2)}, u32[]{:S(2)}) collective-permute-start(bf16[128,1024]{1,0:T(8,128)(2,1)} %refs_0_.3), channel_id=1, source_target_pairs={{0,16},{4,20},{8,24},{12,28},{16,0},{20,4},{24,8},{28,12},{1,17},{... | collective-permute-start | bytes 786440 | tf_op jit(solution)/shard_map/ppermute | solution.py:323
  5.2 3.6 %collective-permute-start.3 = (bf16[128,1024]{1,0:T(8,128)(2,1)}, bf16[128,1024]{1,0:T(8,128)(2,1)S(1)}, u32[]{:S(2)}, u32[]{:S(2)}) collective-permute-start(bf16[128,1024]{1,0:T(8,128)(2,1)} %refs_0_.3), channel_id=1, source_target_pairs={{0,3},{1,2},{2,1},{3,0},{4,7},{5,6},{6,5},{7,4},{8,11},{9,10},{10,... | collective-permute-start | bytes 786440 | tf_op jit(solution)/shard_map/ppermute | solution.py:323
  10.9 2.5 %collective-permute-start.2 = (bf16[128,1024]{1,0:T(8,128)(2,1)}, bf16[128,1024]{1,0:T(8,128)(2,1)S(1)}, u32[]{:S(2)}, u32[]{:S(2)}) collective-permute-start(bf16[128,1024]{1,0:T(8,128)(2,1)} %refs_0_.3), channel_id=1, source_target_pairs={{0,2},{1,3},{2,0},{3,1},{4,6},{5,7},{6,4},{7,5},{8,10},{9,11},{10,... | collective-permute-start | bytes 786440 | tf_op jit(solution)/shard_map/ppermute | solution.py:323
  16.3 2.4 collective-permute-done.6.refs_2_.refs_4_
  18.7 11.6 %encode_near.1 = f32[8,256]{1,0:T(8,128)} custom-call(s32[8,256]{1,0:T(8,128)} %pad_add_fusion.ids_ref, bf16[8192,1024]{1,0:T(8,128)(2,1)} %w_ref.7, bf16[128,1024]{1,0:T(8,128)(2,1)} %refs_0_.3, bf16[128,1024]{1,0:T(8,128)(2,1)} %copy-done.5), custom_call_target="tpu_custom_call" | custom-call | flops 4294967296 | bytes 16777216 | tf_op jit(solution)/shard_map/encode_near/pallas_call | solution.py:79
  32.7 17.6 %encode_far.1 = f32[8,768]{1,0:T(8,128)} custom-call(s32[8,768]{1,0:T(8,128)} %copy-done.19, bf16[8192,1024]{1,0:T(8,128)(2,1)} %w_ref.7, bf16[128,1024]{1,0:T(8,128)(2,1)} %collective-permute-done.4.refs_0_.refs_2_, bf16[128,1024]{1,0:T(8,128)(2,1)} %collective-permute-done.5.refs_1_.refs_3_, bf16[128,1024]{1,0:T(8,128)(2,1)} %collective-permute-done.6.refs_2_.refs_4_, ...), custom_call_target="tpu_custom_call" | custom-call | flops 12884901888 | bytes 16777216 | tf_op jit(solution)/shard_map/encode_far/pallas_call | solution.py:79
  51.0 8.7 %collective-permute-start.10 = (f32[8,1024]{1,0:T(8,128)S(1)}, f32[8,1024]{1,0:T(8,128)S(1)}, u32[]{:S(2)}, u32[]{:S(2)}) collective-permute-start(f32[8,1024]{1,0:T(8,128)S(1)} %pad_maximum_fusion.2), channel_id=1, source_target_pairs={{0,1},{1,0},{2,3},{3,2},{4,5},{5,4},{6,7},{7,6},{8,9},{9,8},{10,11... | collective-permute-start | bytes 98312 | tf_op jit(solution)/shard_map/ppermute | solution.py:323
  60.3 2.0 bias_of.1
  63.1 3.0 %collective-permute-start.11 = (f32[8,1024]{1,0:T(8,128)S(1)}, f32[8,1024]{1,0:T(8,128)S(1)}, u32[]{:S(2)}, u32[]{:S(2)}) collective-permute-start(f32[8,1024]{1,0:T(8,128)S(1)} %fusion.7), channel_id=1, source_target_pairs={{0,2},{1,3},{2,0},{3,1},{4,6},{5,7},{6,4},{7,5},{8,10},{9,11},{10,... | collective-permute-start | bytes 98312 | tf_op jit(solution)/shard_map/ppermute | solution.py:323
  71.0 21.2 %decode_far.1 = (f32[384,1024]{1,0:T(8,128)}, bf16[384,1024]{1,0:T(8,128)(2,1)}) custom-call(s32[8,768]{1,0:T(8,128)} %copy-done.19, bf16[8,768]{1,0:T(8,128)(2,1)} %slice.105.val_ref, bf16[8192,1024]{1,0:T(8,128)(2,1)} %w_ref.11), custom_call_target="tpu_custom_call" | custom-call | flops 12884901888 | bytes 16777216 | tf_op jit(solution)/shard_map/decode_far/pallas_call | solution.py:217
  100.9 12.4 %decode_near.1 = (f32[128,1024]{1,0:T(8,128)}, bf16[128,1024]{1,0:T(8,128)(2,1)}) custom-call(s32[8,256]{1,0:T(8,128)} %pad_add_fusion.ids_ref, bf16[8,256]{1,0:T(8,128)(2,1)} %slice.104.val_ref, bf16[8192,1024]{1,0:T(8,128)(2,1)} %w_ref.11), custom_call_target="tpu_custom_call" | custom-call | flops 4294967296 | bytes 16777216 | tf_op jit(solution)/shard_map/decode_near/pallas_call | solution.py:217
  113.9 2.0 fusion.11
  119.3 6.0 %collective-permute-done.18 = bf16[128,1024]{1,0:T(8,128)(2,1)} collective-permute-done((bf16[128,1024]{1,0:T(8,128)(2,1)}, bf16[128,1024]{1,0:T(8,128)(2,1)}, u32[]{:S(2)}, u32[]{:S(2)}) %collective-permute-start.18) | collective-permute-done | bytes 262176 | tf_op jit(solution)/shard_map/ppermute | solution.py:323
  125.3 4.7 %collective-permute-done.20 = bf16[128,1024]{1,0:T(8,128)(2,1)} collective-permute-done((bf16[128,1024]{1,0:T(8,128)(2,1)}, bf16[128,1024]{1,0:T(8,128)(2,1)}, u32[]{:S(2)}, u32[]{:S(2)}) %collective-permute-start.20) | collective-permute-done | bytes 262176 | tf_op jit(solution)/shard_map/ppermute | solution.py:323
  131.2 2.4 subtract_convert_fusion
  137.9 1.9 fusion.12
  139.9 3.7 %collective-permute-done.24.refs_2_.refs_4_.refs_12_ = bf16[128,1024]{1,0:T(8,128)(2,1)S(1)} collective-permute-done((bf16[128,1024]{1,0:T(8,128)(2,1)S(1)}, bf16[128,1024]{1,0:T(8,128)(2,1)S(1)}, u32[]{:S(2)}, u32[]{:S(2)}) %collective-permute-start.24) | collective-permute-done | bytes 262176 | tf_op jit(solution)/shard_map/ppermute | solution.py:323
  143.5 2.8 %collective-permute-done.23.refs_1_.refs_3_.refs_11_ = bf16[128,1024]{1,0:T(8,128)(2,1)S(1)} collective-permute-done((bf16[128,1024]{1,0:T(8,128)(2,1)S(1)}, bf16[128,1024]{1,0:T(8,128)(2,1)S(1)}, u32[]{:S(2)}, u32[]{:S(2)}) %collective-permute-start.23) | collective-permute-done | bytes 262176 | tf_op jit(solution)/shard_map/ppermute | solution.py:323
  147.5 11.6 %backward_near.1 = f32[8,256]{1,0:T(8,128)} custom-call(s32[8,256]{1,0:T(8,128)} %pad_add_fusion.ids_ref, bf16[8192,1024]{1,0:T(8,128)(2,1)} %w_ref.11, bf16[128,1024]{1,0:T(8,128)(2,1)} %copy-done.2, bf16[128,1024]{1,0:T(8,128)(2,1)} %copy-done.6), custom_call_target="tpu_custom_call" | custom-call | flops 4294967296 | bytes 16777216 | tf_op jit(solution)/shard_map/backward_near/pallas_call | solution.py:79
  160.6 17.6 %backward_far.1 = f32[8,768]{1,0:T(8,128)} custom-call(s32[8,768]{1,0:T(8,128)} %copy-done.19, bf16[8192,1024]{1,0:T(8,128)(2,1)} %w_ref.11, bf16[128,1024]{1,0:T(8,128)(2,1)} %copy-done.22, bf16[128,1024]{1,0:T(8,128)(2,1)} %copy-done.21, bf16[128,1024]{1,0:T(8,128)(2,1)} %copy-done.20, bf16[128,1024]{1,0:T(8,128)(2,1)} %copy-done.25, ...), custom_call_target="tpu_custom_call" | custom-call | flops 12884901888 | bytes 16777216 | tf_op jit(solution)/shard_map/backward_far/pallas_call | solution.py:79
  179.7 27.9 %grad_dec.1 = bf16[8192,1024]{1,0:T(8,128)(2,1)} custom-call(s32[8,1024]{1,0:T(8,128)} %copy-done.11, bf16[8,1024]{1,0:T(8,128)(2,1)} %copy-done.17, bf16[128,1024]{1,0:T(8,128)(2,1)} %copy-done.2, bf16[128,1024]{1,0:T(8,128)(2,1)} %copy-done.6, bf16[128,1024]{1,0:T(8,128)(2,1)} %copy-done.22, bf16[128,1024]{1,0:T(8,128)(2,1)} %copy-done.21, ...), custom_call_target="tpu_custom_call" | custom-call | flops 17179869184 | bytes 16777216 | tf_op jit(solution)/shard_map/grad_dec/pallas_call | solution.py:156
  208.2 4.2 %skip_grad.1 = (bf16[512,1024]{1,0:T(8,128)(2,1)}, f32[1,1024]{1,0:T(1,128)}) custom-call(bf16[128,512]{1,0:T(8,128)(2,1)} %get-tuple-element.35.refs_0_, bf16[128,512]{1,0:T(8,128)(2,1)} %get-tuple-element.46.refs_1_, bf16[128,512]{1,0:T(8,128)(2,1)} %get-tuple-element.34.refs_2_, bf16[128,512]{1,0:T(8,128)(2,1)} %get-tuple-element.33.refs_3_, ...), custom_call_target="tpu_custom_call" | custom-call | flops 1073741824 | bytes 1048576 | tf_op jit(solution)/shard_map/skip_grad/pallas_call | solution.py:304
  213.1 2.4 bias_grad.1
  215.6 27.9 %grad_enc.1 = bf16[8192,1024]{1,0:T(8,128)(2,1)} custom-call(s32[8,1024]{1,0:T(8,128)} %copy-done.11, bf16[8,1024]{1,0:T(8,128)(2,1)} %get-tuple-element.26.val_ref, bf16[128,1024]{1,0:T(8,128)(2,1)} %refs_0_.3, bf16[128,1024]{1,0:T(8,128)(2,1)} %copy-done.5, bf16[128,1024]{1,0:T(8,128)(2,1)} %collective-permute-done.4.refs_0_.refs_2_, ...), custom_call_target="tpu_custom_call" | custom-call | flops 17179869184 | bytes 16777216 | tf_op jit(solution)/shard_map/grad_enc/pallas_call | solution.py:156
  (137 shorter events, 39.4 us)
Async XLA Ops:
  0.6 10.2 %collective-permute-start.5 = (bf16[128,1024]{1,0:T(8,128)(2,1)}, bf16[128,1024]{1,0:T(8,128)(2,1)}, u32[]{:S(2)}, u32[]{:S(2)}) collective-permute-start(bf16[128,1024]{1,0:T(8,128)(2,1)} %refs_0_.3), channel_id=1, source_target_pairs={{0,16},{4,20},{8,24},{12,28},{16,0},{20,4},{24,8},{28,12},{1,17},{... | collective-permute-start | bytes 786440 | tf_op jit(solution)/shard_map/ppermute | solution.py:323
  5.2 10.6 %collective-permute-start.3 = (bf16[128,1024]{1,0:T(8,128)(2,1)}, bf16[128,1024]{1,0:T(8,128)(2,1)S(1)}, u32[]{:S(2)}, u32[]{:S(2)}) collective-permute-start(bf16[128,1024]{1,0:T(8,128)(2,1)} %refs_0_.3), channel_id=1, source_target_pairs={{0,3},{1,2},{2,1},{3,0},{4,7},{5,6},{6,5},{7,4},{8,11},{9,10},{10,... | collective-permute-start | bytes 786440 | tf_op jit(solution)/shard_map/ppermute | solution.py:323
  8.8 9.9 %collective-permute-start.6 = (bf16[128,1024]{1,0:T(8,128)(2,1)}, bf16[128,1024]{1,0:T(8,128)(2,1)}, u32[]{:S(2)}, u32[]{:S(2)}) collective-permute-start(bf16[128,1024]{1,0:T(8,128)(2,1)} %refs_0_.3), channel_id=1, source_target_pairs={{0,24},{4,28},{8,16},{12,20},{16,8},{20,12},{24,0},{28,4},{1,25},{... | collective-permute-start | bytes 786440 | tf_op jit(solution)/shard_map/ppermute | solution.py:323
  10.9 19.9 %collective-permute-start.2 = (bf16[128,1024]{1,0:T(8,128)(2,1)}, bf16[128,1024]{1,0:T(8,128)(2,1)S(1)}, u32[]{:S(2)}, u32[]{:S(2)}) collective-permute-start(bf16[128,1024]{1,0:T(8,128)(2,1)} %refs_0_.3), channel_id=1, source_target_pairs={{0,2},{1,3},{2,0},{3,1},{4,6},{5,7},{6,4},{7,5},{8,10},{9,11},{10,... | collective-permute-start | bytes 786440 | tf_op jit(solution)/shard_map/ppermute | solution.py:323
  13.4 17.5 %collective-permute-start.1 = (bf16[128,1024]{1,0:T(8,128)(2,1)}, bf16[128,1024]{1,0:T(8,128)(2,1)S(1)}, u32[]{:S(2)}, u32[]{:S(2)}) collective-permute-start(bf16[128,1024]{1,0:T(8,128)(2,1)} %refs_0_.3), channel_id=1, source_target_pairs={{0,1},{1,0},{2,3},{3,2},{4,5},{5,4},{6,7},{7,6},{8,9},{9,8},{10,11... | collective-permute-start | bytes 786440 | tf_op jit(solution)/shard_map/ppermute | solution.py:323
  15.8 16.9 %collective-permute-start.8 = (bf16[128,1024]{1,0:T(8,128)(2,1)}, bf16[128,1024]{1,0:T(8,128)(2,1)}, u32[]{:S(2)}, u32[]{:S(2)}) collective-permute-start(bf16[128,1024]{1,0:T(8,128)(2,1)} %collective-permute-done.5.refs_1_.refs_3_), channel_id=1, source_target_pairs={{0,4},{4,0},{8,12},{12,8},{16,20},{20,16},{24,28},{28,24},{1,5},{5... | collective-permute-start | bytes 786440 | tf_op jit(solution)/shard_map/ppermute | solution.py:323
  15.8 16.9 %collective-permute-start.7 = (bf16[128,1024]{1,0:T(8,128)(2,1)}, bf16[128,1024]{1,0:T(8,128)(2,1)}, u32[]{:S(2)}, u32[]{:S(2)}) collective-permute-start(bf16[128,1024]{1,0:T(8,128)(2,1)} %collective-permute-done.4.refs_0_.refs_2_), channel_id=1, source_target_pairs={{0,4},{4,0},{8,12},{12,8},{16,20},{20,16},{24,28},{28,24},{1,5},{5... | collective-permute-start | bytes 786440 | tf_op jit(solution)/shard_map/ppermute | solution.py:323
  18.7 14.0 %collective-permute-start.9 = (bf16[128,1024]{1,0:T(8,128)(2,1)}, bf16[128,1024]{1,0:T(8,128)(2,1)}, u32[]{:S(2)}, u32[]{:S(2)}) collective-permute-start(bf16[128,1024]{1,0:T(8,128)(2,1)} %collective-permute-done.6.refs_2_.refs_4_), channel_id=1, source_target_pairs={{0,4},{4,0},{8,12},{12,8},{16,20},{20,16},{24,28},{28,24},{1,5},{5... | collective-permute-start | bytes 786440 | tf_op jit(solution)/shard_map/ppermute | solution.py:323
  30.7 65.6 %collective-permute-start.16 = (bf16[512,1024]{1,0:T(8,128)(2,1)S(1)}, bf16[512,1024]{1,0:T(8,128)(2,1)S(1)}, u32[]{:S(2)}, u32[]{:S(2)}) collective-permute-start(bf16[512,1024]{1,0:T(8,128)(2,1)S(1)} %copy-done.3), channel_id=1, source_target_pairs={{0,4},{4,0},{8,12},{12,8},{16,20},{20,16},{24,28},{28,24},{1,5},{5... | collective-permute-start | bytes 3145736 | tf_op jit(solution)/shard_map/ppermute | solution.py:323
  51.0 11.3 %collective-permute-start.10 = (f32[8,1024]{1,0:T(8,128)S(1)}, f32[8,1024]{1,0:T(8,128)S(1)}, u32[]{:S(2)}, u32[]{:S(2)}) collective-permute-start(f32[8,1024]{1,0:T(8,128)S(1)} %pad_maximum_fusion.2), channel_id=1, source_target_pairs={{0,1},{1,0},{2,3},{3,2},{4,5},{5,4},{6,7},{7,6},{8,9},{9,8},{10,11... | collective-permute-start | bytes 98312 | tf_op jit(solution)/shard_map/ppermute | solution.py:323
  66.9 25.9 %collective-permute-start.15 = (bf16[128,1024]{1,0:T(8,128)(2,1)}, bf16[128,1024]{1,0:T(8,128)(2,1)S(1)}, u32[]{:S(2)}, u32[]{:S(2)}) collective-permute-start(bf16[128,1024]{1,0:T(8,128)(2,1)} %get-tuple-element.37), channel_id=1, source_target_pairs={{0,24},{4,28},{8,16},{12,20},{16,8},{20,12},{24,0},{28,4},{1,25},{... | collective-permute-start | bytes 786440 | tf_op jit(solution)/shard_map/ppermute | solution.py:323
  67.3 25.5 %collective-permute-start.14 = (bf16[128,1024]{1,0:T(8,128)(2,1)S(1)}, bf16[128,1024]{1,0:T(8,128)(2,1)S(1)}, u32[]{:S(2)}, u32[]{:S(2)}) collective-permute-start(bf16[128,1024]{1,0:T(8,128)(2,1)S(1)} %get-tuple-element.38), channel_id=1, source_target_pairs={{0,16},{4,20},{8,24},{12,28},{16,0},{20,4},{24,8},{28,12},{1,17},{... | collective-permute-start | bytes 786440 | tf_op jit(solution)/shard_map/ppermute | solution.py:323
  68.9 24.0 %collective-permute-start.13 = (bf16[128,1024]{1,0:T(8,128)(2,1)S(1)}, bf16[128,1024]{1,0:T(8,128)(2,1)S(1)}, u32[]{:S(2)}, u32[]{:S(2)}) collective-permute-start(bf16[128,1024]{1,0:T(8,128)(2,1)S(1)} %get-tuple-element.39), channel_id=1, source_target_pairs={{0,8},{4,12},{8,0},{12,4},{16,24},{20,28},{24,16},{28,20},{1,9},{5... | collective-permute-start | bytes 786440 | tf_op jit(solution)/shard_map/ppermute | solution.py:323
  116.4 13.7 %collective-permute-start.20 = (bf16[128,1024]{1,0:T(8,128)(2,1)}, bf16[128,1024]{1,0:T(8,128)(2,1)}, u32[]{:S(2)}, u32[]{:S(2)}) collective-permute-start(bf16[128,1024]{1,0:T(8,128)(2,1)} %get-tuple-element.41), channel_id=1, source_target_pairs={{0,24},{4,28},{8,16},{12,20},{16,8},{20,12},{24,0},{28,4},{1,25},{... | collective-permute-start | bytes 786440 | tf_op jit(solution)/shard_map/ppermute | solution.py:323
  117.9 13.4 %collective-permute-start.19 = (bf16[128,1024]{1,0:T(8,128)(2,1)S(1)}, bf16[128,1024]{1,0:T(8,128)(2,1)}, u32[]{:S(2)}, u32[]{:S(2)}) collective-permute-start(bf16[128,1024]{1,0:T(8,128)(2,1)S(1)} %get-tuple-element.42), channel_id=1, source_target_pairs={{0,16},{4,20},{8,24},{12,28},{16,0},{20,4},{24,8},{28,12},{1,17},{... | collective-permute-start | bytes 786440 | tf_op jit(solution)/shard_map/ppermute | solution.py:323
  119.3 18.6 %collective-permute-start.30 = (bf16[512,512]{1,0:T(8,128)(2,1)}, bf16[512,512]{1,0:T(8,128)(2,1)}, u32[]{:S(2)}, u32[]{:S(2)}) collective-permute-start(bf16[512,512]{1,0:T(8,128)(2,1)} %constant_dynamic-slice_fusion.1), channel_id=1, source_target_pairs={{0,4},{4,0},{8,12},{12,8},{16,20},{20,16},{24,28},{28,24},{1,5},{5... | collective-permute-start | bytes 1572872 | tf_op jit(solution)/shard_map/ppermute | solution.py:323
  133.6 9.9 %collective-permute-start.24 = (bf16[128,1024]{1,0:T(8,128)(2,1)S(1)}, bf16[128,1024]{1,0:T(8,128)(2,1)S(1)}, u32[]{:S(2)}, u32[]{:S(2)}) collective-permute-start(bf16[128,1024]{1,0:T(8,128)(2,1)S(1)} %get-tuple-element.28.refs_0_.refs_8_), channel_id=1, source_target_pairs={{0,24},{4,28},{8,16},{12,20},{16,8},{20,12},{24,0},{28,4},{1,25},{... | collective-permute-start | bytes 786440 | tf_op jit(solution)/shard_map/ppermute | solution.py:323
  135.1 11.2 %collective-permute-start.23 = (bf16[128,1024]{1,0:T(8,128)(2,1)S(1)}, bf16[128,1024]{1,0:T(8,128)(2,1)S(1)}, u32[]{:S(2)}, u32[]{:S(2)}) collective-permute-start(bf16[128,1024]{1,0:T(8,128)(2,1)S(1)} %get-tuple-element.28.refs_0_.refs_8_), channel_id=1, source_target_pairs={{0,16},{4,20},{8,24},{12,28},{16,0},{20,4},{24,8},{28,12},{1,17},{... | collective-permute-start | bytes 786440 | tf_op jit(solution)/shard_map/ppermute | solution.py:323
  135.6 10.8 %collective-permute-start.22 = (bf16[128,1024]{1,0:T(8,128)(2,1)S(1)}, bf16[128,1024]{1,0:T(8,128)(2,1)S(1)}, u32[]{:S(2)}, u32[]{:S(2)}) collective-permute-start(bf16[128,1024]{1,0:T(8,128)(2,1)S(1)} %get-tuple-element.28.refs_0_.refs_8_), channel_id=1, source_target_pairs={{0,8},{4,12},{8,0},{12,4},{16,24},{20,28},{24,16},{28,20},{1,9},{5... | collective-permute-start | bytes 786440 | tf_op jit(solution)/shard_map/ppermute | solution.py:323
  137.1 9.7 %collective-permute-start.21 = (bf16[128,1024]{1,0:T(8,128)(2,1)S(1)}, bf16[128,1024]{1,0:T(8,128)(2,1)S(1)}, u32[]{:S(2)}, u32[]{:S(2)}) collective-permute-start(bf16[128,1024]{1,0:T(8,128)(2,1)S(1)} %get-tuple-element.28.refs_0_.refs_8_), channel_id=1, source_target_pairs={{0,4},{4,0},{8,12},{12,8},{16,20},{20,16},{24,28},{28,24},{1,5},{5... | collective-permute-start | bytes 786440 | tf_op jit(solution)/shard_map/ppermute | solution.py:323
  143.5 15.6 %collective-permute-start.27 = (bf16[128,1024]{1,0:T(8,128)(2,1)S(1)}, bf16[128,1024]{1,0:T(8,128)(2,1)S(1)}, u32[]{:S(2)}, u32[]{:S(2)}) collective-permute-start(bf16[128,1024]{1,0:T(8,128)(2,1)S(1)} %collective-permute-done.24.refs_2_.refs_4_.refs_12_), channel_id=1, source_target_pairs={{0,4},{4,0},{8,12},{12,8},{16,20},{20,16},{24,28},{28,24},{1,5},{5... | collective-permute-start | bytes 786440 | tf_op jit(solution)/shard_map/ppermute | solution.py:323
  146.3 12.8 %collective-permute-start.26 = (bf16[128,1024]{1,0:T(8,128)(2,1)S(1)}, bf16[128,1024]{1,0:T(8,128)(2,1)S(1)}, u32[]{:S(2)}, u32[]{:S(2)}) collective-permute-start(bf16[128,1024]{1,0:T(8,128)(2,1)S(1)} %collective-permute-done.23.refs_1_.refs_3_.refs_11_), channel_id=1, source_target_pairs={{0,4},{4,0},{8,12},{12,8},{16,20},{20,16},{24,28},{28,24},{1,5},{5... | collective-permute-start | bytes 786440 | tf_op jit(solution)/shard_map/ppermute | solution.py:323
  146.4 12.8 %collective-permute-start.25 = (bf16[128,1024]{1,0:T(8,128)(2,1)S(1)}, bf16[128,1024]{1,0:T(8,128)(2,1)S(1)}, u32[]{:S(2)}, u32[]{:S(2)}) collective-permute-start(bf16[128,1024]{1,0:T(8,128)(2,1)S(1)} %collective-permute-done.22.refs_0_.refs_2_.refs_10_), channel_id=1, source_target_pairs={{0,4},{4,0},{8,12},{12,8},{16,20},{20,16},{24,28},{28,24},{1,5},{5... | collective-permute-start | bytes 786440 | tf_op jit(solution)/shard_map/ppermute | solution.py:323
  179.0 28.6 %collective-permute-start.28 = (f32[8,1024]{1,0:T(8,128)S(1)}, f32[8,1024]{1,0:T(8,128)S(1)}, u32[]{:S(2)}, u32[]{:S(2)}) collective-permute-start(f32[8,1024]{1,0:T(8,128)S(1)} %pad_maximum_fusion.3), channel_id=1, source_target_pairs={{0,1},{1,0},{2,3},{3,2},{4,5},{5,4},{6,7},{7,6},{8,9},{9,8},{10,11... | collective-permute-start | bytes 98312 | tf_op jit(solution)/shard_map/ppermute | solution.py:323
  (33 other events, 311.6 us)

commit v3 on v2

v3 whole, which is shorter than its diff:
```python
import functools

import jax
import jax.numpy as jnp
from jax import lax
from jax.experimental import pallas as pl
from jax.experimental.pallas import tpu as pltpu
from jax.sharding import PartitionSpec as P

VMEM_BYTES = 60 << 20
F32 = jnp.float32
BF16 = jnp.bfloat16
GRAD_WIDE = 256
DECODE_WIDE = 256
SPLIT = 2


def whole(i):
    return (0, 0)


def params():
    return pltpu.CompilerParams(vmem_limit_bytes=VMEM_BYTES)


def cost(features, width, tokens):
    return pl.CostEstimate(
        flops=2 * features * width * tokens,
        bytes_accessed=2 * features * width,
        transcendentals=0,
    )


def lay_out(pieces, rows_ref):
    first = 0
    for piece in pieces:
        rows_ref[first : first + piece.shape[0], :] = piece[...]
        first += piece.shape[0]


def tree_sum(parts):
    while len(parts) > 1:
        parts = [parts[i] + parts[i + 1] for i in range(0, len(parts), 2)]
    return parts[0]


def pick_kernel(sub, first, start, count, ids_ref, old_ref, *refs):
    pieces, out_ref, rows_ref = refs[SPLIT : SPLIT + count], refs[-2], refs[-1]
    step = pl.program_id(0)
    share = refs[0].shape[0]
    tile = SPLIT * share

    @pl.when(step == 0)
    def _():
        out_ref[...] = old_ref[...]
        lay_out(pieces, rows_ref)

    for s in range(tile // sub):
        offset = s * sub % share
        dots = lax.dot_general(
            refs[s * sub // share][offset : offset + sub, :],
            rows_ref[...],
            (((1,), (1,)), ((), ())),
            preferred_element_type=F32,
        )
        for block in range(rows_ref.shape[0] // 128):
            cols = slice(first + block * 128, first + (block + 1) * 128)
            ids = ids_ref[:, cols]
            low = ids & 7
            high = (ids >> 3) - ((step + start) * (tile // 8) + s * (sub // 8))
            kept = out_ref[:, cols]
            for g in range(sub // 8):
                found = jnp.take_along_axis(
                    dots[g * 8 : (g + 1) * 8, block * 128 : (block + 1) * 128], low, axis=0
                )
                kept = jnp.where(high == g, found, kept)
            out_ref[:, cols] = kept


def pick(ids, old, pieces, w, first, half):
    features, width = w.shape
    slots, tokens = ids.shape
    here = sum(piece.shape[0] for piece in pieces)
    tile = min(2048 if here <= 256 else 1024, features)
    steps = features // tile
    start = 0
    if half is not None:
        steps, start = steps // 2, half * (steps // 2)
    return pl.pallas_call(
        functools.partial(pick_kernel, min(256, tile), first, start, len(pieces)),
        grid=(steps,),
        in_specs=[pl.BlockSpec((slots, tokens), whole)] * 2
        + [
            pl.BlockSpec((tile // SPLIT, width), lambda i, at=at: ((i + start) * SPLIT + at, 0))
            for at in range(SPLIT)
        ]
        + [pl.BlockSpec(piece.shape, whole) for piece in pieces],
        out_specs=pl.BlockSpec((slots, tokens), whole),
        out_shape=jax.ShapeDtypeStruct((slots, tokens), F32),
        scratch_shapes=[pltpu.VMEM((here, width), BF16)],
        compiler_params=params(),
        cost_estimate=cost(steps * tile, width, here),
    )(ids, old, *[w] * SPLIT, *pieces)


def table_part(ids_ref, val_ref, first, number):
    slots = ids_ref.shape[0]
    cols = slice(first, first + 128)
    iota = lax.broadcasted_iota(jnp.int32, (16, 128), 0).astype(BF16)
    vals = [jnp.broadcast_to(val_ref[j : j + 1, cols], (16, 128)) for j in range(slots)]
    near = jnp.clip(ids_ref[:, cols] - number * 256, -1, 256).astype(BF16)
    away = [jnp.broadcast_to(near[j : j + 1], (16, 128)) - iota for j in range(slots)]
    part = []
    for g in range(16):
        kept = jnp.zeros((16, 128), BF16)
        for j in range(slots):
            kept = jnp.where(away[j] == 16 * g, vals[j], kept)
        part.append(kept)
    return part


def grad_kernel(sub, wide, count, ids_ref, val_ref, *refs):
    pieces, (out_ref, rows_ref), tables = refs[:count], refs[count : count + 2], refs[count + 2 :]
    step = pl.program_id(0)
    tile, width = out_ref.shape
    blocks = ids_ref.shape[1] // 128
    subs = tile // sub
    chunks = width // wide

    def build(table, number, some):
        for block in some:
            cols = slice(block * 128, (block + 1) * 128)
            part = table_part(ids_ref, val_ref, block * 128, number)
            for g in range(sub // 16):
                table[g * 16 : (g + 1) * 16, cols] = part[g]

    @pl.when(step == 0)
    def _():
        lay_out(pieces, rows_ref)
        build(tables[0], 0, range(blocks))

    for s in range(subs):
        here, after = tables[s % 2], tables[(s + 1) % 2]
        for n in range(chunks):
            cols = slice(n * wide, (n + 1) * wide)
            out_ref[s * sub : (s + 1) * sub, cols] = jnp.dot(
                here[...], rows_ref[:, cols], preferred_element_type=F32
            ).astype(out_ref.dtype)
            some = range(n * blocks // chunks, (n + 1) * blocks // chunks)
            build(after, step * subs + s + 1, some)


def grad_rows(ids, val, pieces, features):
    slots, tokens = ids.shape
    width = pieces[0].shape[1]
    tile, sub = min(1024, features), 256
    assert sub == 256 and (tile // sub) % 2 == 0
    return pl.pallas_call(
        functools.partial(grad_kernel, sub, min(GRAD_WIDE, width), len(pieces)),
        grid=(features // tile,),
        in_specs=[pl.BlockSpec((slots, tokens), whole)] * 2
        + [pl.BlockSpec(piece.shape, whole) for piece in pieces],
        out_specs=pl.BlockSpec((tile, width), lambda i: (i, 0)),
        out_shape=jax.ShapeDtypeStruct((features, width), BF16),
        scratch_shapes=[pltpu.VMEM((tokens, width), BF16)]
        + [pltpu.VMEM((sub, tokens), BF16)] * 2,
        compiler_params=params(),
        cost_estimate=cost(features, width, tokens),
    )(ids, val, *pieces)


def decode_kernel(sub, deep, wide, first_token, count, ids_ref, val_ref, w_ref, pair_ref, *refs):
    skips, (keep_ref, send_ref, total) = refs[:count], refs[count : count + 3]
    tables = refs[count + 3 :]
    step = pl.program_id(0)
    tile, width = w_ref.shape
    tokens = total.shape[0]
    chunks = width // wide
    items = [(u, s) for u in range(tile // deep) for s in range(tokens // sub)]
    work = [(b, q) for b in range(sub // 128) for q in range(deep // 256)]

    def build(table, item, first, n):
        for b, q in work[n * len(work) // chunks : (n + 1) * len(work) // chunks]:
            block = item[1] * (sub // 128) + b
            number = first + item[0] * (deep // 256) + q
            part = table_part(ids_ref, val_ref, first_token + block * 128, number)
            table[b * 128 : (b + 1) * 128, q * 256 : (q + 1) * 256] = jnp.concatenate(
                part, axis=0
            ).T

    @pl.when(step == 0)
    def _():
        total[...] = jnp.zeros_like(total)
        for n in range(chunks):
            build(tables[0], items[0], 0, n)

    for p, piece in enumerate(skips):
        rows = slice(p * piece.shape[0], (p + 1) * piece.shape[0])
        total[rows, :] += jnp.dot(piece[...], pair_ref[...], preferred_element_type=F32)

    for i, (u, s) in enumerate(items):
        following = (i + 1) % len(items)
        here, after = tables[i % len(tables)], tables[following % len(tables)]
        first = (step + (i + 1) // len(items)) * (tile // 256)
        rows = slice(s * sub, (s + 1) * sub)
        for n in range(chunks):
            cols = slice(n * wide, (n + 1) * wide)
            total[rows, cols] += jnp.dot(
                here[...], w_ref[u * deep : (u + 1) * deep, cols], preferred_element_type=F32
            )
            build(after, items[following], first, n)

    @pl.when(step == pl.num_programs(0) - 1)
    def _():
        half = tokens // 2
        keep_ref[...] = total[:half, :]
        send_ref[...] = total[half:, :].astype(BF16)


def decode(ids, val, w, skips, pair, first, tokens):
    features, width = w.shape
    slots, every = ids.shape
    tile = min(1024, features)
    steps = features // tile
    part = pair.shape[0] // steps
    assert part % 128 == 0
    sub = min(256, tokens)
    deep = tile if tokens > sub else tile // 2
    count = (tile // deep) * (tokens // sub)
    half = (tokens // 2, width)
    return pl.pallas_call(
        functools.partial(
            decode_kernel, sub, deep, min(DECODE_WIDE, width), first, len(skips)
        ),
        grid=(steps,),
        in_specs=[pl.BlockSpec((slots, every), whole)] * 2
        + [pl.BlockSpec((tile, width), lambda i: (i, 0))]
        + [pl.BlockSpec((part, width), lambda i: (i, 0))]
        + [pl.BlockSpec((skip.shape[0], part), lambda i: (0, i)) for skip in skips],
        out_specs=[pl.BlockSpec(half, whole)] * 2,
        out_shape=[jax.ShapeDtypeStruct(half, F32), jax.ShapeDtypeStruct(half, BF16)],
        scratch_shapes=[pltpu.VMEM((tokens, width), F32)]
        + [pltpu.VMEM((sub, deep), BF16)] * (2 if count % 2 == 0 else count),
        compiler_params=params(),
        cost_estimate=cost(features, width, tokens),
    )(ids, val, w, pair, *skips)


def bias_kernel(ids_ref, b_ref, out_ref):
    for block in range(out_ref.shape[1] // 128):
        cols = slice(block * 128, (block + 1) * 128)
        ids = ids_ref[:, cols]
        low = ids & 127
        high = ids >> 7
        kept = jnp.zeros(ids.shape, F32)
        for a in range(b_ref.shape[0]):
            row = jnp.broadcast_to(b_ref[a : a + 1, :], ids.shape)
            kept = jnp.where(high == a, jnp.take_along_axis(row, low, axis=1), kept)
        out_ref[:, cols] = kept


def bias_of(ids, bias):
    table = bias.reshape(-1, 128)
    return pl.pallas_call(
        bias_kernel,
        out_shape=jax.ShapeDtypeStruct(ids.shape, F32),
        cost_estimate=pl.CostEstimate(flops=1 << 20, bytes_accessed=1 << 20, transcendentals=0),
        name="bias_of",
    )(ids, table)


def bias_grad_kernel(ids_ref, slope_ref, out_ref):
    slots, tokens = ids_ref.shape
    groups = out_ref.shape[0]
    total = jnp.zeros((3 * groups, 128), F32)
    for j in range(slots):
        ids = ids_ref[j : j + 1, :]
        slope = slope_ref[j : j + 1, :]
        first = slope.astype(BF16).astype(F32)
        second = (slope - first).astype(BF16).astype(F32)
        third = slope - first - second
        high = lax.broadcasted_iota(jnp.int32, (groups, tokens), 0) == (ids >> 7)
        low = lax.broadcasted_iota(jnp.int32, (128, tokens), 0) == (ids & 127)
        low = jnp.where(low, 1.0, 0.0).astype(BF16)
        spread = jnp.concatenate(
            [jnp.where(high, part, 0.0) for part in (first, second, third)], axis=0
        ).astype(BF16)
        total = total + lax.dot_general(
            spread, low, (((1,), (1,)), ((), ())), preferred_element_type=F32
        )
    out_ref[...] = total[:groups] + total[groups : 2 * groups] + total[2 * groups :]


def bias_grad(ids, slope, features):
    out = pl.pallas_call(
        bias_grad_kernel,
        out_shape=jax.ShapeDtypeStruct((features // 128, 128), F32),
        cost_estimate=pl.CostEstimate(flops=1 << 28, bytes_accessed=1 << 20, transcendentals=0),
        name="bias_grad",
    )(ids, slope)
    return out.reshape(features)


def skip_grad_kernel(count, *refs):
    columns, resid = refs[:count], refs[count : 2 * count]
    out_ref, sum_ref, left, right = refs[2 * count :]
    lay_out(columns, left)
    lay_out(resid, right)
    out_ref[...] = lax.dot_general(
        left[...], right[...], (((0,), (0,)), ((), ())), preferred_element_type=F32
    ).astype(BF16)
    sums = [jnp.sum(piece[...].astype(F32), axis=0, keepdims=True) for piece in resid]
    order = piece_order(count)
    sum_ref[...] = tree_sum([sums[order.index(d)] for d in range(count)])


def skip_grad(columns, resid):
    rows, width = resid[0].shape
    height = columns[0].shape[1]
    count = len(resid)
    out, sums = pl.pallas_call(
        functools.partial(skip_grad_kernel, count),
        out_shape=[
            jax.ShapeDtypeStruct((height, width), BF16),
            jax.ShapeDtypeStruct((1, width), F32),
        ],
        scratch_shapes=[
            pltpu.VMEM((count * rows, height), BF16),
            pltpu.VMEM((count * rows, width), BF16),
        ],
        compiler_params=params(),
        cost_estimate=cost(height, width, count * rows),
        name="skip_grad",
    )(*columns, *resid)
    return out, sums.reshape(width)


def swap(value, axis, mask):
    size = lax.axis_size(axis)
    return lax.ppermute(value, axis, [(i, i ^ mask) for i in range(size)])


def sum_over(value, axis):
    mask = 1
    while mask < lax.axis_size(axis):
        value = value + swap(value, axis, mask)
        mask *= 2
    return value


def piece_order(size):
    return [0, 1] + list(range(2, size, 2)) + list(range(3, size, 2))


def exchange(value):
    size = lax.axis_size("seq")
    near = [value, swap(value, "seq", 1)]
    even = [swap(value, "seq", d) for d in range(2, size, 2)]
    return near, even, [swap(piece, "seq", 1) for piece in even]


def order_kernel(size, me_ref, ids_ref, out_ref):
    rows = ids_ref.shape[1] // size
    for at, d in enumerate(piece_order(size)):
        first = pl.multiple_of((me_ref[0] ^ d) * rows, 128)
        out_ref[:, at * rows : (at + 1) * rows] = ids_ref[:, pl.ds(first, rows)]


def relative_slots(ids, size):
    me = lax.axis_index("seq").astype(jnp.int32).reshape(1)
    return pl.pallas_call(
        functools.partial(order_kernel, size),
        in_specs=[pl.BlockSpec(memory_space=pltpu.SMEM), pl.BlockSpec(memory_space=pltpu.VMEM)],
        out_shape=jax.ShapeDtypeStruct(ids.shape, jnp.int32),
        name="order",
    )(me, ids)


def work(inputs, target, feature_slots, w_enc, b_enc, w_dec, b_dec, w_skip):
    size, wide = lax.axis_size("seq"), lax.axis_size("tp")
    me, column = lax.axis_index("seq"), lax.axis_index("tp")
    rows = inputs.shape[0]
    pair_rows = 2 * rows
    far_rows = (size - 2) * rows
    features = w_enc.shape[0]
    height = w_skip.shape[0]
    assert 2 * height == inputs.shape[1]
    ids = relative_slots(feature_slots[:, 0, :].T, size)
    none = jnp.zeros(ids.shape, F32)

    near_tokens, even_tokens, odd_tokens = exchange(inputs)
    far_tokens = even_tokens + odd_tokens
    columns = [inputs] + [swap(inputs, "tp", m) for m in range(1, wide)]
    other_skip = swap(w_skip, "seq", 1)

    pre = pick(ids, none, near_tokens, w_enc, 0, None)
    pre = pick(ids, pre, far_tokens, w_enc, pair_rows, 0)
    columns, pre = lax.optimization_barrier((columns, pre))
    columns = jnp.stack(columns)

    def for_group(mask):
        return lax.dynamic_index_in_dim(columns, ((me ^ mask) // 2) ^ column, 0, False)

    groups = [for_group(d) for d in range(0, size, 2)]
    groups, pre = lax.optimization_barrier((groups, pre))
    groups = groups[:1] + [
        swap(group, "seq", 2 * d + 2) for d, group in enumerate(groups[1:])
    ]
    pre = pick(ids, pre, far_tokens, w_enc, pair_rows, 1)
    (w_skip, other_skip), pre = lax.optimization_barrier(((w_skip, other_skip), pre))
    first_core = me % 2 == 0
    pair = jnp.concatenate(
        [jnp.where(first_core, w_skip, other_skip), jnp.where(first_core, other_skip, w_skip)]
    )
    preact = sum_over(pre, "tp") + bias_of(ids, b_enc)
    gate = (ids >= 0) & (preact > 0.0)
    active = jnp.where(gate, preact, 0.0).astype(BF16)

    far_keep, far_send = decode(ids, active, w_dec, groups[1:], pair, pair_rows, far_rows)
    sent = (far_keep + swap(far_send, "seq", 1).astype(F32)).astype(BF16)
    sent = [sent[i * rows : (i + 1) * rows] for i in range(size // 2 - 1)]
    near_active, sent = lax.optimization_barrier((active, sent))
    parts = [swap(piece, "seq", 2 * d + 2).astype(F32) for d, piece in enumerate(sent)]
    near_keep, near_send = decode(ids, near_active, w_dec, groups[:1], pair, 0, pair_rows)
    parts = [near_keep + swap(near_send, "seq", 1).astype(F32)] + parts
    predicted = tree_sum(parts) + b_dec
    reconstruction = predicted.astype(BF16)
    residual = (predicted - target.astype(F32)).astype(BF16)

    near_resid, even_resid, odd_resid = exchange(residual)
    back = pick(ids, none, near_resid, w_dec, 0, None)
    far_resid = even_resid + odd_resid
    back = pick(ids, back, far_resid, w_dec, pair_rows, None)
    slope = jnp.where(gate, sum_over(back, "tp"), 0.0)
    resid = near_resid + far_resid
    grad_dec = grad_rows(ids, active, resid, features)
    grad_enc = grad_rows(ids, slope.astype(BF16), near_tokens + far_tokens, features)
    grad_benc = bias_grad(ids, slope, features)
    groups, _ = lax.optimization_barrier((groups, back))
    mine = [lax.dynamic_slice_in_dim(g, (me % 2) * height, height, 1) for g in groups]
    other = [lax.dynamic_slice_in_dim(g, (1 - me % 2) * height, height, 1) for g in groups]
    others = swap(jnp.concatenate(other), "seq", 1)
    others = [others[i * rows : (i + 1) * rows] for i in range(size // 2)]
    grad_skip, grad_bdec = skip_grad([mine[0], others[0]] + mine[1:] + others[1:], resid)
    return reconstruction, grad_enc, grad_dec, grad_benc, grad_bdec, grad_skip


def solution(mesh):
    in_specs = (
        P("seq", "tp"),
        P("seq", "tp"),
        P(None, "seq", None),
        P("seq", "tp"),
        P("seq"),
        P("seq", "tp"),
        P("tp"),
        P("seq", "tp"),
    )
    out_specs = (P("seq", "tp"), P("seq", "tp"), P("seq", "tp"), P("seq"), P("tp"), P("seq", "tp"))
    return jax.shard_map(work, mesh=mesh, in_specs=in_specs, out_specs=out_specs, check_vma=False)
```

time: 245 us -> 240 us (0.980)
  waiting for transfers between devices: 22.2 us -> 33.5 us
  starting transfers between devices: 37.8 us -> 30.9 us
  local copies, waits for them, and re-layouts: 13.2 us -> 8.1 us
  Pallas kernels: 156 us -> 159 us
  other arithmetic: 10.3 us -> 7.67 us
  matrix products: 2.58 us -> 0 us
    ppermute x31, waiting for transfers between devices: 22.2 us -> 33.5 us  [swap(): return lax.ppermute(value, axis, [(i, i ^ mask) for i in range(size)])]
    ppermute x31, starting transfers between devices: 37.8 us -> 30.9 us  [swap(): return lax.ppermute(value, axis, [(i, i ^ mask) for i in range(size)])]
    slice x5 -> x2, local copies, waits for them, and re-layouts: 5.88 us -> 0.86 us  [the longest x1 0.8 us: work(): others = [others[i * rows:(i + 1) * rows] for i in range(size // 2)]]
    dot_general x2 -> x0, matrix products: 2.58 us -> none  [the longest x1 1.84 us: shards(): jnp.dot(other, other_skip, preferred_element_type=F32)]
    pallas_call x6 -> x8, Pallas kernels: 91.9 us -> 94.3 us  [the longest x5 57.4 us: pick(): pl.pallas_call(functools.partial(pick_kernel, min(256, tile), first, star...]
    unnamed x62 -> x60, local copies, waits for them, and re-layouts: 5.65 us -> 4.34 us
  transfers between devices with their start and end apart: 31 -> 31, of which waited for: 10 -> 10; matrix products, arithmetic and copies ran while one was open for 7% -> 3% of each run, Pallas kernels for 39% -> 42%
where the time goes in v3:
time: 240 us
  Pallas kernels  159 us (66%)
  waiting for transfers between devices  33.5 us (14%)
  starting transfers between devices  30.9 us (13%)
  local copies, waits for them, and re-layouts  8.1 us (3%)
  other arithmetic  7.67 us (3%)
    pallas_call x5, Pallas kernels, pick(): pl.pallas_call(functools.partial(pick_kernel, min(256, tile), first, star...  57.4 us
    pallas_call x2, Pallas kernels, grad_rows(): pl.pallas_call(functools.partial(grad_kernel, sub, min(GRAD_WIDE, width),...  55.8 us
    pallas_call x2, Pallas kernels, decode(): pl.pallas_call(functools.partial(decode_kernel, sub, deep, min(DECODE_WID...  35.5 us
    ppermute x31, waiting for transfers between devices, swap(): return lax.ppermute(value, axis, [(i, i ^ mask) for i in range(size)])  33.5 us
    ppermute x31, starting transfers between devices, swap(): return lax.ppermute(value, axis, [(i, i ^ mask) for i in range(size)])  30.9 us
  transfers between devices with their start and end apart: 31, of which 10 were waited for; matrix products, arithmetic and copies ran while one was open for 3% of the time, Pallas kernels for 42%

profile of v3, /device:TPU:0, one launch (start us, length us, event | category | flops | bytes accessed | tf_op | source)
XLA Modules:
  0.0 239.8 jit_solution(685191568863141779)
XLA Ops:
  0.6 4.0 %collective-permute-start.7 = (bf16[128,1024]{1,0:T(8,128)(2,1)}, bf16[128,1024]{1,0:T(8,128)(2,1)S(1)}, u32[]{:S(2)}, u32[]{:S(2)}) collective-permute-start(bf16[128,1024]{1,0:T(8,128)(2,1)} %refs_0_.11), channel_id=1, source_target_pairs={{0,24},{4,28},{8,16},{12,20},{16,8},{20,12},{24,0},{28,4},{1,25},{... | collective-permute-start | bytes 786440 | tf_op jit(solution)/shard_map/ppermute | solution.py:340
  5.3 4.0 %collective-permute-start.3 = (bf16[128,1024]{1,0:T(8,128)(2,1)}, bf16[128,1024]{1,0:T(8,128)(2,1)S(1)}, u32[]{:S(2)}, u32[]{:S(2)}) collective-permute-start(bf16[128,1024]{1,0:T(8,128)(2,1)} %refs_0_.11), channel_id=1, source_target_pairs={{0,3},{1,2},{2,1},{3,0},{4,7},{5,6},{6,5},{7,4},{8,11},{9,10},{10,... | collective-permute-start | bytes 786440 | tf_op jit(solution)/shard_map/ppermute | solution.py:340
  10.6 2.0 bias_of.1
  12.7 2.4 %collective-permute-start.2 = (bf16[128,1024]{1,0:T(8,128)(2,1)}, bf16[128,1024]{1,0:T(8,128)(2,1)}, u32[]{:S(2)}, u32[]{:S(2)}) collective-permute-start(bf16[128,1024]{1,0:T(8,128)(2,1)} %refs_0_.11), channel_id=1, source_target_pairs={{0,2},{1,3},{2,0},{3,1},{4,6},{5,7},{6,4},{7,5},{8,10},{9,11},{10,... | collective-permute-start | bytes 786440 | tf_op jit(solution)/shard_map/ppermute | solution.py:340
  18.2 9.6 %shard_map.127.old_ref = f32[8,1024]{1,0:T(8,128)} custom-call(s32[8,1024]{1,0:T(8,128)} %order.1.ids_ref, f32[8,1024]{1,0:T(8,128)} %broadcast_1_old_ref.2.old_ref, bf16[8192,1024]{1,0:T(8,128)(2,1)} %refs_1_.7, bf16[8192,1024]{1,0:T(8,128)(2,1)} %refs_1_.7, bf16[128,1024]{1,0:T(8,128)(2,1)} %refs_0_.11, bf16[128,1024]{1,0:T(8,128)(2,1)} %copy-done.11), custom_call_target="tpu_custom_call" | custom-call | flops 4294967296 | bytes 16777216 | tf_op jit(solution)/shard_map/pallas_call | solution.py:89
  30.9 10.2 %shard_map.128.old_ref = f32[8,1024]{1,0:T(8,128)} custom-call(s32[8,1024]{1,0:T(8,128)} %order.1.ids_ref, f32[8,1024]{1,0:T(8,128)} %shard_map.127.old_ref, bf16[8192,1024]{1,0:T(8,128)(2,1)} %refs_1_.7, bf16[8192,1024]{1,0:T(8,128)(2,1)} %refs_1_.7, bf16[128,1024]{1,0:T(8,128)(2,1)} %copy-done.4, bf16[128,1024]{1,0:T(8,128)(2,1)} %copy-done.3, ...), custom_call_target="tpu_custom_call" | custom-call | flops 6442450944 | bytes 8388608 | tf_op jit(solution)/shard_map/pallas_call | solution.py:89
  46.6 10.2 %shard_map.129 = f32[8,1024]{1,0:T(8,128)} custom-call(s32[8,1024]{1,0:T(8,128)} %order.1.ids_ref, f32[8,1024]{1,0:T(8,128)} %shard_map.128.old_ref, bf16[8192,1024]{1,0:T(8,128)(2,1)} %refs_1_.7, bf16[8192,1024]{1,0:T(8,128)(2,1)} %refs_1_.7, bf16[128,1024]{1,0:T(8,128)(2,1)} %copy-done.4, bf16[128,1024]{1,0:T(8,128)(2,1)} %copy-done.3, ...), custom_call_target="tpu_custom_call" | custom-call | flops 6442450944 | bytes 8388608 | tf_op jit(solution)/shard_map/pallas_call | solution.py:89
  57.5 3.5 %collective-permute-done.11 = f32[8,1024]{1,0:T(8,128)S(1)} collective-permute-done((f32[8,1024]{1,0:T(8,128)}, f32[8,1024]{1,0:T(8,128)S(1)}, u32[]{:S(2)}, u32[]{:S(2)}) %collective-permute-start.11) | collective-permute-done | bytes 32800 | tf_op jit(solution)/shard_map/ppermute | solution.py:340
  61.0 2.9 %collective-permute-start.12 = (f32[8,1024]{1,0:T(8,128)S(1)}, f32[8,1024]{1,0:T(8,128)S(1)}, u32[]{:S(2)}, u32[]{:S(2)}) collective-permute-start(f32[8,1024]{1,0:T(8,128)S(1)} %add.83), channel_id=1, source_target_pairs={{0,2},{1,3},{2,0},{3,1},{4,6},{5,7},{6,4},{7,5},{8,10},{9,11},{10,... | collective-permute-start | bytes 98312 | tf_op jit(solution)/shard_map/ppermute | solution.py:340
  67.6 22.9 %shard_map.130 = (f32[384,1024]{1,0:T(8,128)}, bf16[384,1024]{1,0:T(8,128)(2,1)}) custom-call(s32[8,1024]{1,0:T(8,128)} %order.1.ids_ref, bf16[8,1024]{1,0:T(8,128)(2,1)} %get-tuple-element.47.val_ref, bf16[8192,1024]{1,0:T(8,128)(2,1)} %refs_1_.9, bf16[1024,1024]{1,0:T(8,128)(2,1)} %pad_maximum_fusion.pair_ref, bf16[128,1024]{1,0:T(8,128)(2,1)} %copy-done.16, ...), custom_call_target="tpu_custom_call" | custom-call | flops 12884901888 | bytes 16777216 | tf_op jit(solution)/shard_map/pallas_call | solution.py:231
  90.6 2.5 %collective-permute-done.16 = bf16[384,1024]{1,0:T(8,128)(2,1)S(1)} collective-permute-done((bf16[384,1024]{1,0:T(8,128)(2,1)}, bf16[384,1024]{1,0:T(8,128)(2,1)S(1)}, u32[]{:S(2)}, u32[]{:S(2)}) %collective-permute-start.16) | collective-permute-done | bytes 786464 | tf_op jit(solution)/shard_map/ppermute | solution.py:340
  94.8 12.6 %shard_map.131 = (f32[128,1024]{1,0:T(8,128)}, bf16[128,1024]{1,0:T(8,128)(2,1)}) custom-call(s32[8,1024]{1,0:T(8,128)} %order.1.ids_ref, bf16[8,1024]{1,0:T(8,128)(2,1)} %get-tuple-element.47.val_ref, bf16[8192,1024]{1,0:T(8,128)(2,1)} %refs_1_.9, bf16[1024,1024]{1,0:T(8,128)(2,1)} %pad_maximum_fusion.pair_ref, bf16[128,1024]{1,0:T(8,128)(2,1)} %get-tuple-element.54.refs_0_), custom_call_target="tpu_custom_call" | custom-call | flops 4294967296 | bytes 16777216 | tf_op jit(solution)/shard_map/pallas_call | solution.py:231
  111.0 5.7 %collective-permute-done.18 = bf16[128,1024]{1,0:T(8,128)(2,1)S(1)} collective-permute-done((bf16[128,1024]{1,0:T(8,128)(2,1)S(1)}, bf16[128,1024]{1,0:T(8,128)(2,1)S(1)}, u32[]{:S(2)}, u32[]{:S(2)}) %collective-permute-start.18) | collective-permute-done | bytes 262176 | tf_op jit(solution)/shard_map/ppermute | solution.py:340
  116.7 6.2 %collective-permute-done.19 = bf16[128,1024]{1,0:T(8,128)(2,1)S(1)} collective-permute-done((bf16[128,1024]{1,0:T(8,128)(2,1)S(1)}, bf16[128,1024]{1,0:T(8,128)(2,1)S(1)}, u32[]{:S(2)}, u32[]{:S(2)}) %collective-permute-start.19) | collective-permute-done | bytes 262176 | tf_op jit(solution)/shard_map/ppermute | solution.py:340
  128.5 6.6 %collective-permute-done.24.refs_4_.refs_12_ = bf16[128,1024]{1,0:T(8,128)(2,1)S(1)} collective-permute-done((bf16[128,1024]{1,0:T(8,128)(2,1)S(1)}, bf16[128,1024]{1,0:T(8,128)(2,1)S(1)}, u32[]{:S(2)}, u32[]{:S(2)}) %collective-permute-start.24) | collective-permute-done | bytes 262176 | tf_op jit(solution)/shard_map/ppermute | solution.py:340
  135.1 3.9 %collective-permute-done.23.refs_3_.refs_11_ = bf16[128,1024]{1,0:T(8,128)(2,1)S(1)} collective-permute-done((bf16[128,1024]{1,0:T(8,128)(2,1)S(1)}, bf16[128,1024]{1,0:T(8,128)(2,1)S(1)}, u32[]{:S(2)}, u32[]{:S(2)}) %collective-permute-start.23) | collective-permute-done | bytes 262176 | tf_op jit(solution)/shard_map/ppermute | solution.py:340
  140.3 9.5 %shard_map.132.old_ref = f32[8,1024]{1,0:T(8,128)} custom-call(s32[8,1024]{1,0:T(8,128)} %order.1.ids_ref, f32[8,1024]{1,0:T(8,128)} %broadcast_1_old_ref.2.old_ref, bf16[8192,1024]{1,0:T(8,128)(2,1)} %refs_1_.9, bf16[8192,1024]{1,0:T(8,128)(2,1)} %refs_1_.9, bf16[128,1024]{1,0:T(8,128)(2,1)} %copy-done.8, bf16[128,1024]{1,0:T(8,128)(2,1)} %copy-done.12), custom_call_target="tpu_custom_call" | custom-call | flops 4294967296 | bytes 16777216 | tf_op jit(solution)/shard_map/pallas_call | solution.py:89
  151.4 17.8 %shard_map.133 = f32[8,1024]{1,0:T(8,128)} custom-call(s32[8,1024]{1,0:T(8,128)} %order.1.ids_ref, f32[8,1024]{1,0:T(8,128)} %shard_map.132.old_ref, bf16[8192,1024]{1,0:T(8,128)(2,1)} %refs_1_.9, bf16[8192,1024]{1,0:T(8,128)(2,1)} %refs_1_.9, bf16[128,1024]{1,0:T(8,128)(2,1)} %copy-done.26, bf16[128,1024]{1,0:T(8,128)(2,1)} %copy-done.25, ...), custom_call_target="tpu_custom_call" | custom-call | flops 12884901888 | bytes 16777216 | tf_op jit(solution)/shard_map/pallas_call | solution.py:89
  171.0 2.3 collective-permute-done.28
  173.3 2.6 %collective-permute-start.29 = (f32[8,1024]{1,0:T(8,128)S(1)}, f32[8,1024]{1,0:T(8,128)S(1)}, u32[]{:S(2)}, u32[]{:S(2)}) collective-permute-start(f32[8,1024]{1,0:T(8,128)S(1)} %add.94), channel_id=1, source_target_pairs={{0,2},{1,3},{2,0},{3,1},{4,6},{5,7},{6,4},{7,5},{8,10},{9,11},{10,... | collective-permute-start | bytes 98312 | tf_op jit(solution)/shard_map/ppermute | solution.py:340
  175.9 27.9 %shard_map.135 = bf16[8192,1024]{1,0:T(8,128)(2,1)} custom-call(s32[8,1024]{1,0:T(8,128)} %order.1.ids_ref, bf16[8,1024]{1,0:T(8,128)(2,1)} %get-tuple-element.47.val_ref, bf16[128,1024]{1,0:T(8,128)(2,1)} %copy-done.8, bf16[128,1024]{1,0:T(8,128)(2,1)} %copy-done.12, bf16[128,1024]{1,0:T(8,128)(2,1)} %copy-done.26, bf16[128,1024]{1,0:T(8,128)(2,1)} %copy-done.25, ...), custom_call_target="tpu_custom_call" | custom-call | flops 17179869184 | bytes 16777216 | tf_op jit(solution)/shard_map/pallas_call | solution.py:158
  204.5 27.9 %shard_map.134 = bf16[8192,1024]{1,0:T(8,128)(2,1)} custom-call(s32[8,1024]{1,0:T(8,128)} %order.1.ids_ref, bf16[8,1024]{1,0:T(8,128)(2,1)} %get-tuple-element.60.val_ref, bf16[128,1024]{1,0:T(8,128)(2,1)} %refs_0_.11, bf16[128,1024]{1,0:T(8,128)(2,1)} %copy-done.11, bf16[128,1024]{1,0:T(8,128)(2,1)} %copy-done.4, bf16[128,1024]{1,0:T(8,128)(2,1)} %copy-done.3, ...), custom_call_target="tpu_custom_call" | custom-call | flops 17179869184 | bytes 16777216 | tf_op jit(solution)/shard_map/pallas_call | solution.py:158
  232.4 2.4 %bias_grad.1 = f32[64,128]{1,0:T(8,128)} custom-call(s32[8,1024]{1,0:T(8,128)} %order.1.ids_ref, f32[8,1024]{1,0:T(8,128)} %get-tuple-element.61.slope_ref), custom_call_target="tpu_custom_call" | custom-call | flops 268435456 | bytes 1048576 | tf_op jit(solution)/shard_map/bias_grad/pallas_call | solution.py:295
  235.6 4.2 %skip_grad.1 = (bf16[512,1024]{1,0:T(8,128)(2,1)}, f32[1,1024]{1,0:T(1,128)}) custom-call(bf16[128,512]{1,0:T(8,128)(2,1)} %get-tuple-element.89.refs_0_, bf16[128,512]{1,0:T(8,128)(2,1)} %get-tuple-element.78.refs_1_, bf16[128,512]{1,0:T(8,128)(2,1)} %get-tuple-element.83.refs_2_, bf16[128,512]{1,0:T(8,128)(2,1)} %get-tuple-element.88.refs_3_, ...), custom_call_target="tpu_custom_call" | custom-call | flops 1073741824 | bytes 1048576 | tf_op jit(solution)/shard_map/skip_grad/pallas_call | solution.py:321
  (127 shorter events, 34.8 us)
Async XLA Ops:
  0.6 12.0 %collective-permute-start.7 = (bf16[128,1024]{1,0:T(8,128)(2,1)}, bf16[128,1024]{1,0:T(8,128)(2,1)S(1)}, u32[]{:S(2)}, u32[]{:S(2)}) collective-permute-start(bf16[128,1024]{1,0:T(8,128)(2,1)} %refs_0_.11), channel_id=1, source_target_pairs={{0,24},{4,28},{8,16},{12,20},{16,8},{20,12},{24,0},{28,4},{1,25},{... | collective-permute-start | bytes 786440 | tf_op jit(solution)/shard_map/ppermute | solution.py:340
  4.6 12.1 %collective-permute-start.6 = (bf16[128,1024]{1,0:T(8,128)(2,1)}, bf16[128,1024]{1,0:T(8,128)(2,1)S(1)}, u32[]{:S(2)}, u32[]{:S(2)}) collective-permute-start(bf16[128,1024]{1,0:T(8,128)(2,1)} %refs_0_.11), channel_id=1, source_target_pairs={{0,16},{4,20},{8,24},{12,28},{16,0},{20,4},{24,8},{28,12},{1,17},{... | collective-permute-start | bytes 786440 | tf_op jit(solution)/shard_map/ppermute | solution.py:340
  5.1 11.9 %collective-permute-start.5 = (bf16[128,1024]{1,0:T(8,128)(2,1)}, bf16[128,1024]{1,0:T(8,128)(2,1)S(1)}, u32[]{:S(2)}, u32[]{:S(2)}) collective-permute-start(bf16[128,1024]{1,0:T(8,128)(2,1)} %refs_0_.11), channel_id=1, source_target_pairs={{0,8},{4,12},{8,0},{12,4},{16,24},{20,28},{24,16},{28,20},{1,9},{5... | collective-permute-start | bytes 786440 | tf_op jit(solution)/shard_map/ppermute | solution.py:340
  5.3 12.0 %collective-permute-start.4 = (bf16[128,1024]{1,0:T(8,128)(2,1)}, bf16[128,1024]{1,0:T(8,128)(2,1)S(1)}, u32[]{:S(2)}, u32[]{:S(2)}) collective-permute-start(bf16[128,1024]{1,0:T(8,128)(2,1)} %refs_0_.11), channel_id=1, source_target_pairs={{0,4},{4,0},{8,12},{12,8},{16,20},{20,16},{24,28},{28,24},{1,5},{5... | collective-permute-start | bytes 786440 | tf_op jit(solution)/shard_map/ppermute | solution.py:340
  5.3 35.9 %collective-permute-start.3 = (bf16[128,1024]{1,0:T(8,128)(2,1)}, bf16[128,1024]{1,0:T(8,128)(2,1)S(1)}, u32[]{:S(2)}, u32[]{:S(2)}) collective-permute-start(bf16[128,1024]{1,0:T(8,128)(2,1)} %refs_0_.11), channel_id=1, source_target_pairs={{0,3},{1,2},{2,1},{3,0},{4,7},{5,6},{6,5},{7,4},{8,11},{9,10},{10,... | collective-permute-start | bytes 786440 | tf_op jit(solution)/shard_map/ppermute | solution.py:340
  12.7 28.5 %collective-permute-start.2 = (bf16[128,1024]{1,0:T(8,128)(2,1)}, bf16[128,1024]{1,0:T(8,128)(2,1)}, u32[]{:S(2)}, u32[]{:S(2)}) collective-permute-start(bf16[128,1024]{1,0:T(8,128)(2,1)} %refs_0_.11), channel_id=1, source_target_pairs={{0,2},{1,3},{2,0},{3,1},{4,6},{5,7},{6,4},{7,5},{8,10},{9,11},{10,... | collective-permute-start | bytes 786440 | tf_op jit(solution)/shard_map/ppermute | solution.py:340
  16.8 11.1 %collective-permute-start.10 = (bf16[128,1024]{1,0:T(8,128)(2,1)S(1)}, bf16[128,1024]{1,0:T(8,128)(2,1)S(1)}, u32[]{:S(2)}, u32[]{:S(2)}) collective-permute-start(bf16[128,1024]{1,0:T(8,128)(2,1)S(1)} %collective-permute-done.7.refs_4_), channel_id=1, source_target_pairs={{0,4},{4,0},{8,12},{12,8},{16,20},{20,16},{24,28},{28,24},{1,5},{5... | collective-permute-start | bytes 786440 | tf_op jit(solution)/shard_map/ppermute | solution.py:340
  17.0 12.5 %collective-permute-start.9 = (bf16[128,1024]{1,0:T(8,128)(2,1)S(1)}, bf16[128,1024]{1,0:T(8,128)(2,1)S(1)}, u32[]{:S(2)}, u32[]{:S(2)}) collective-permute-start(bf16[128,1024]{1,0:T(8,128)(2,1)S(1)} %collective-permute-done.6.refs_3_), channel_id=1, source_target_pairs={{0,4},{4,0},{8,12},{12,8},{16,20},{20,16},{24,28},{28,24},{1,5},{5... | collective-permute-start | bytes 786440 | tf_op jit(solution)/shard_map/ppermute | solution.py:340
  17.3 12.4 %collective-permute-start.8 = (bf16[128,1024]{1,0:T(8,128)(2,1)S(1)}, bf16[128,1024]{1,0:T(8,128)(2,1)S(1)}, u32[]{:S(2)}, u32[]{:S(2)}) collective-permute-start(bf16[128,1024]{1,0:T(8,128)(2,1)S(1)} %collective-permute-done.5.refs_2_), channel_id=1, source_target_pairs={{0,4},{4,0},{8,12},{12,8},{16,20},{20,16},{24,28},{28,24},{1,5},{5... | collective-permute-start | bytes 786440 | tf_op jit(solution)/shard_map/ppermute | solution.py:340
  27.9 13.3 %collective-permute-start.1 = (bf16[128,1024]{1,0:T(8,128)(2,1)S(1)}, bf16[128,1024]{1,0:T(8,128)(2,1)S(1)}, u32[]{:S(2)}, u32[]{:S(2)}) collective-permute-start(bf16[128,1024]{1,0:T(8,128)(2,1)S(1)} %copy-done.9), channel_id=1, source_target_pairs={{0,1},{1,0},{2,3},{3,2},{4,5},{5,4},{6,7},{7,6},{8,9},{9,8},{10,11... | collective-permute-start | bytes 786440 | tf_op jit(solution)/shard_map/ppermute | solution.py:340
  29.5 27.3 %collective-permute-start = (bf16[512,1024]{1,0:T(8,128)(2,1)S(1)}, bf16[512,1024]{1,0:T(8,128)(2,1)S(1)}, u32[]{:S(2)}, u32[]{:S(2)}) collective-permute-start(bf16[512,1024]{1,0:T(8,128)(2,1)S(1)} %copy-done.10), channel_id=1, source_target_pairs={{0,4},{4,0},{8,12},{12,8},{16,20},{20,16},{24,28},{28,24},{1,5},{5... | collective-permute-start | bytes 3145736 | tf_op jit(solution)/shard_map/ppermute | solution.py:340
  43.1 23.7 %collective-permute-start.13 = (bf16[128,1024]{1,0:T(8,128)(2,1)S(1)}, bf16[128,1024]{1,0:T(8,128)(2,1)S(1)}, u32[]{:S(2)}, u32[]{:S(2)}) collective-permute-start(bf16[128,1024]{1,0:T(8,128)(2,1)S(1)} %get-tuple-element.42), channel_id=1, source_target_pairs={{0,8},{4,12},{8,0},{12,4},{16,24},{20,28},{24,16},{28,20},{1,9},{5... | collective-permute-start | bytes 786440 | tf_op jit(solution)/shard_map/ppermute | solution.py:340
  44.6 22.2 %collective-permute-start.14 = (bf16[128,1024]{1,0:T(8,128)(2,1)S(1)}, bf16[128,1024]{1,0:T(8,128)(2,1)S(1)}, u32[]{:S(2)}, u32[]{:S(2)}) collective-permute-start(bf16[128,1024]{1,0:T(8,128)(2,1)S(1)} %get-tuple-element.43), channel_id=1, source_target_pairs={{0,16},{4,20},{8,24},{12,28},{16,0},{20,4},{24,8},{28,12},{1,17},{... | collective-permute-start | bytes 786440 | tf_op jit(solution)/shard_map/ppermute | solution.py:340
  45.4 21.4 %collective-permute-start.15 = (bf16[128,1024]{1,0:T(8,128)(2,1)S(1)}, bf16[128,1024]{1,0:T(8,128)(2,1)S(1)}, u32[]{:S(2)}, u32[]{:S(2)}) collective-permute-start(bf16[128,1024]{1,0:T(8,128)(2,1)S(1)} %get-tuple-element.44), channel_id=1, source_target_pairs={{0,24},{4,28},{8,16},{12,20},{16,8},{20,12},{24,0},{28,4},{1,25},{... | collective-permute-start | bytes 786440 | tf_op jit(solution)/shard_map/ppermute | solution.py:340
  109.1 13.9 %collective-permute-start.19 = (bf16[128,1024]{1,0:T(8,128)(2,1)S(1)}, bf16[128,1024]{1,0:T(8,128)(2,1)S(1)}, u32[]{:S(2)}, u32[]{:S(2)}) collective-permute-start(bf16[128,1024]{1,0:T(8,128)(2,1)S(1)} %get-tuple-element.52), channel_id=1, source_target_pairs={{0,16},{4,20},{8,24},{12,28},{16,0},{20,4},{24,8},{28,12},{1,17},{... | collective-permute-start | bytes 786440 | tf_op jit(solution)/shard_map/ppermute | solution.py:340
  109.8 13.2 %collective-permute-start.20 = (bf16[128,1024]{1,0:T(8,128)(2,1)S(1)}, bf16[128,1024]{1,0:T(8,128)(2,1)S(1)}, u32[]{:S(2)}, u32[]{:S(2)}) collective-permute-start(bf16[128,1024]{1,0:T(8,128)(2,1)S(1)} %get-tuple-element.53), channel_id=1, source_target_pairs={{0,24},{4,28},{8,16},{12,20},{16,8},{20,12},{24,0},{28,4},{1,25},{... | collective-permute-start | bytes 786440 | tf_op jit(solution)/shard_map/ppermute | solution.py:340
  126.5 12.5 %collective-permute-start.23 = (bf16[128,1024]{1,0:T(8,128)(2,1)S(1)}, bf16[128,1024]{1,0:T(8,128)(2,1)S(1)}, u32[]{:S(2)}, u32[]{:S(2)}) collective-permute-start(bf16[128,1024]{1,0:T(8,128)(2,1)S(1)} %get-tuple-element.62.refs_2_.refs_0_.refs_8_), channel_id=1, source_target_pairs={{0,16},{4,20},{8,24},{12,28},{16,0},{20,4},{24,8},{28,12},{1,17},{... | collective-permute-start | bytes 786440 | tf_op jit(solution)/shard_map/ppermute | solution.py:340
  127.0 12.1 %collective-permute-start.22 = (bf16[128,1024]{1,0:T(8,128)(2,1)S(1)}, bf16[128,1024]{1,0:T(8,128)(2,1)S(1)}, u32[]{:S(2)}, u32[]{:S(2)}) collective-permute-start(bf16[128,1024]{1,0:T(8,128)(2,1)S(1)} %get-tuple-element.62.refs_2_.refs_0_.refs_8_), channel_id=1, source_target_pairs={{0,8},{4,12},{8,0},{12,4},{16,24},{20,28},{24,16},{28,20},{1,9},{5... | collective-permute-start | bytes 786440 | tf_op jit(solution)/shard_map/ppermute | solution.py:340
  128.5 11.1 %collective-permute-start.21 = (bf16[128,1024]{1,0:T(8,128)(2,1)S(1)}, bf16[128,1024]{1,0:T(8,128)(2,1)S(1)}, u32[]{:S(2)}, u32[]{:S(2)}) collective-permute-start(bf16[128,1024]{1,0:T(8,128)(2,1)S(1)} %get-tuple-element.62.refs_2_.refs_0_.refs_8_), channel_id=1, source_target_pairs={{0,4},{4,0},{8,12},{12,8},{16,20},{20,16},{24,28},{28,24},{1,5},{5... | collective-permute-start | bytes 786440 | tf_op jit(solution)/shard_map/ppermute | solution.py:340
  135.1 14.7 %collective-permute-start.27 = (bf16[128,1024]{1,0:T(8,128)(2,1)S(1)}, bf16[128,1024]{1,0:T(8,128)(2,1)S(1)}, u32[]{:S(2)}, u32[]{:S(2)}) collective-permute-start(bf16[128,1024]{1,0:T(8,128)(2,1)S(1)} %collective-permute-done.24.refs_4_.refs_12_), channel_id=1, source_target_pairs={{0,4},{4,0},{8,12},{12,8},{16,20},{20,16},{24,28},{28,24},{1,5},{5... | collective-permute-start | bytes 786440 | tf_op jit(solution)/shard_map/ppermute | solution.py:340
  139.0 10.8 %collective-permute-start.26 = (bf16[128,1024]{1,0:T(8,128)(2,1)S(1)}, bf16[128,1024]{1,0:T(8,128)(2,1)S(1)}, u32[]{:S(2)}, u32[]{:S(2)}) collective-permute-start(bf16[128,1024]{1,0:T(8,128)(2,1)S(1)} %collective-permute-done.23.refs_3_.refs_11_), channel_id=1, source_target_pairs={{0,4},{4,0},{8,12},{12,8},{16,20},{20,16},{24,28},{28,24},{1,5},{5... | collective-permute-start | bytes 786440 | tf_op jit(solution)/shard_map/ppermute | solution.py:340
  139.1 10.8 %collective-permute-start.25 = (bf16[128,1024]{1,0:T(8,128)(2,1)S(1)}, bf16[128,1024]{1,0:T(8,128)(2,1)S(1)}, u32[]{:S(2)}, u32[]{:S(2)}) collective-permute-start(bf16[128,1024]{1,0:T(8,128)(2,1)S(1)} %collective-permute-done.22.refs_2_.refs_10_), channel_id=1, source_target_pairs={{0,4},{4,0},{8,12},{12,8},{16,20},{20,16},{24,28},{28,24},{1,5},{5... | collective-permute-start | bytes 786440 | tf_op jit(solution)/shard_map/ppermute | solution.py:340
  170.9 63.9 %collective-permute-start.30 = (bf16[512,512]{1,0:T(8,128)(2,1)S(1)}, bf16[512,512]{1,0:T(8,128)(2,1)S(1)}, u32[]{:S(2)}, u32[]{:S(2)}) collective-permute-start(bf16[512,512]{1,0:T(8,128)(2,1)S(1)} %pad_maximum_fusion.2), channel_id=1, source_target_pairs={{0,4},{4,0},{8,12},{12,8},{16,20},{20,16},{24,28},{28,24},{1,5},{5... | collective-permute-start | bytes 1572872 | tf_op jit(solution)/shard_map/ppermute | solution.py:340
  173.3 30.6 %collective-permute-start.29 = (f32[8,1024]{1,0:T(8,128)S(1)}, f32[8,1024]{1,0:T(8,128)S(1)}, u32[]{:S(2)}, u32[]{:S(2)}) collective-permute-start(f32[8,1024]{1,0:T(8,128)S(1)} %add.94), channel_id=1, source_target_pairs={{0,2},{1,3},{2,0},{3,1},{4,6},{5,7},{6,4},{7,5},{8,10},{9,11},{10,... | collective-permute-start | bytes 98312 | tf_op jit(solution)/shard_map/ppermute | solution.py:340
  (37 other events, 305.9 us)

commit v4 on v3

--- a/solution.py
+++ b/solution.py
@@ -10,7 +10,7 @@
 VMEM_BYTES = 60 << 20
 F32 = jnp.float32
 BF16 = jnp.bfloat16
-GRAD_WIDE = 256
+GRAD_WIDE = 512
 DECODE_WIDE = 256
 SPLIT = 2
 
@@ -36,6 +36,20 @@
     for piece in pieces:
         rows_ref[first : first + piece.shape[0], :] = piece[...]
         first += piece.shape[0]
+
+
+def lay_out_blocks(pieces, rows_ref):
+    first = 0
+    for piece in pieces:
+        for block in range(rows_ref.shape[0]):
+            rows_ref[block, first : first + piece.shape[0], :] = piece[
+                :, block * 128 : (block + 1) * 128
+            ]
+        first += piece.shape[0]
+
+
+def from_blocks(ref, first, last):
+    return jnp.concatenate([ref[block] for block in range(first, last)], axis=1)
 
 
 def tree_sum(parts):
@@ -129,14 +143,15 @@
 
     def build(table, number, some):
         for block in some:
-            cols = slice(block * 128, (block + 1) * 128)
-            part = table_part(ids_ref, val_ref, block * 128, number)
-            for g in range(sub // 16):
-                table[g * 16 : (g + 1) * 16, cols] = part[g]
+            for q in range(sub // 256):
+                part = table_part(ids_ref, val_ref, block * 128, number * (sub // 256) + q)
+                for g in range(16):
+                    first = q * 256 + g * 16
+                    table[block, first : first + 16, :] = part[g]
 
     @pl.when(step == 0)
     def _():
-        lay_out(pieces, rows_ref)
+        lay_out_blocks(pieces, rows_ref)
         build(tables[0], 0, range(blocks))
 
     for s in range(subs):
@@ -144,7 +159,9 @@
         for n in range(chunks):
             cols = slice(n * wide, (n + 1) * wide)
             out_ref[s * sub : (s + 1) * sub, cols] = jnp.dot(
-                here[...], rows_ref[:, cols], preferred_element_type=F32
+                from_blocks(here, 0, blocks),
+                from_blocks(rows_ref, n * wide // 128, (n + 1) * wide // 128),
+                preferred_element_type=F32,
             ).astype(out_ref.dtype)
             some = range(n * blocks // chunks, (n + 1) * blocks // chunks)
             build(after, step * subs + s + 1, some)
@@ -153,8 +170,8 @@
 def grad_rows(ids, val, pieces, features):
     slots, tokens = ids.shape
     width = pieces[0].shape[1]
-    tile, sub = min(1024, features), 256
-    assert sub == 256 and (tile // sub) % 2 == 0
+    tile, sub = min(1024, features), 512
+    assert (tile // sub) % 2 == 0
     return pl.pallas_call(
         functools.partial(grad_kernel, sub, min(GRAD_WIDE, width), len(pieces)),
         grid=(features // tile,),
@@ -162,8 +179,8 @@
         + [pl.BlockSpec(piece.shape, whole) for piece in pieces],
         out_specs=pl.BlockSpec((tile, width), lambda i: (i, 0)),
         out_shape=jax.ShapeDtypeStruct((features, width), BF16),
-        scratch_shapes=[pltpu.VMEM((tokens, width), BF16)]
-        + [pltpu.VMEM((sub, tokens), BF16)] * 2,
+        scratch_shapes=[pltpu.VMEM((width // 128, tokens, 128), BF16)]
+        + [pltpu.VMEM((tokens // 128, sub, 128), BF16)] * 2,
         compiler_params=params(),
         cost_estimate=cost(features, width, tokens),
     )(ids, val, *pieces)
@@ -184,9 +201,10 @@
             block = item[1] * (sub // 128) + b
             number = first + item[0] * (deep // 256) + q
             part = table_part(ids_ref, val_ref, first_token + block * 128, number)
-            table[b * 128 : (b + 1) * 128, q * 256 : (q + 1) * 256] = jnp.concatenate(
-                part, axis=0
-            ).T
+            for h in range(2):
+                table[2 * q + h, b * 128 : (b + 1) * 128, :] = jnp.concatenate(
+                    part[8 * h : 8 * h + 8], axis=0
+                ).T
 
     @pl.when(step == 0)
     def _():
@@ -206,7 +224,9 @@
         for n in range(chunks):
             cols = slice(n * wide, (n + 1) * wide)
             total[rows, cols] += jnp.dot(
-                here[...], w_ref[u * deep : (u + 1) * deep, cols], preferred_element_type=F32
+                from_blocks(here, 0, deep // 128),
+                w_ref[u * deep : (u + 1) * deep, cols],
+                preferred_element_type=F32,
             )
             build(after, items[following], first, n)
 
@@ -220,7 +240,7 @@
 def decode(ids, val, w, skips, pair, first, tokens):
     features, width = w.shape
     slots, every = ids.shape
-    tile = min(1024, features)
+    tile = min(2048 if tokens <= 256 else 1024, features)
     steps = features // tile
     part = pair.shape[0] // steps
     assert part % 128 == 0
@@ -240,7 +260,7 @@
         out_specs=[pl.BlockSpec(half, whole)] * 2,
         out_shape=[jax.ShapeDtypeStruct(half, F32), jax.ShapeDtypeStruct(half, BF16)],
         scratch_shapes=[pltpu.VMEM((tokens, width), F32)]
-        + [pltpu.VMEM((sub, deep), BF16)] * (2 if count % 2 == 0 else count),
+        + [pltpu.VMEM((deep // 128, sub, 128), BF16)] * (2 if count % 2 == 0 else count),
         compiler_params=params(),
         cost_estimate=cost(features, width, tokens),
     )(ids, val, w, pair, *skips)
@@ -304,7 +324,11 @@
 def skip_grad_kernel(count, *refs):
     columns, resid = refs[:count], refs[count : 2 * count]
     out_ref, sum_ref, left, right = refs[2 * count :]
-    lay_out(columns, left)
+
+    @pl.when(pl.program_id(0) == 0)
+    def _():
+        lay_out(columns, left)
+
     lay_out(resid, right)
     out_ref[...] = lax.dot_general(
         left[...], right[...], (((0,), (0,)), ((), ())), preferred_element_type=F32
@@ -318,15 +342,23 @@
     rows, width = resid[0].shape
     height = columns[0].shape[1]
     count = len(resid)
+    wide = min(512, width)
     out, sums = pl.pallas_call(
         functools.partial(skip_grad_kernel, count),
+        grid=(width // wide,),
+        in_specs=[pl.BlockSpec((rows, height), whole)] * count
+        + [pl.BlockSpec((rows, wide), lambda i: (0, i))] * count,
+        out_specs=[
+            pl.BlockSpec((height, wide), lambda i: (0, i)),
+            pl.BlockSpec((1, wide), lambda i: (0, i)),
+        ],
         out_shape=[
             jax.ShapeDtypeStruct((height, width), BF16),
             jax.ShapeDtypeStruct((1, width), F32),
         ],
         scratch_shapes=[
             pltpu.VMEM((count * rows, height), BF16),
-            pltpu.VMEM((count * rows, width), BF16),
+            pltpu.VMEM((count * rows, wide), BF16),
         ],
         compiler_params=params(),
         cost_estimate=cost(height, width, count * rows),

time: 240 us -> 240 us (level)
  no operation moved by 1% of the time
where the time goes in v4:
time: 240 us
  Pallas kernels  159 us (66%)
  waiting for transfers between devices  33.6 us (14%)
  starting transfers between devices  30.8 us (13%)
  local copies, waits for them, and re-layouts  8.1 us (3%)
  other arithmetic  7.67 us (3%)
    pallas_call x5, Pallas kernels, pick(): pl.pallas_call(functools.partial(pick_kernel, min(256, tile), first, star...  57.4 us
    pallas_call x2, Pallas kernels, grad_rows(): pl.pallas_call(functools.partial(grad_kernel, sub, min(GRAD_WIDE, width),...  55.6 us
    pallas_call x2, Pallas kernels, decode(): pl.pallas_call(functools.partial(decode_kernel, sub, deep, min(DECODE_WID...  35.6 us
    ppermute x31, waiting for transfers between devices, swap(): return lax.ppermute(value, axis, [(i, i ^ mask) for i in range(size)])  33.6 us
    ppermute x31, starting transfers between devices, swap(): return lax.ppermute(value, axis, [(i, i ^ mask) for i in range(size)])  30.8 us
  transfers between devices with their start and end apart: 31, of which 10 were waited for; matrix products, arithmetic and copies ran while one was open for 3% of the time, Pallas kernels for 42%

profile of v4, /device:TPU:0, one launch (start us, length us, event | category | flops | bytes accessed | tf_op | source)
XLA Modules:
  0.0 239.9 jit_solution(11488945288593213447)
XLA Ops:
  0.6 4.0 %collective-permute-start.7 = (bf16[128,1024]{1,0:T(8,128)(2,1)}, bf16[128,1024]{1,0:T(8,128)(2,1)S(1)}, u32[]{:S(2)}, u32[]{:S(2)}) collective-permute-start(bf16[128,1024]{1,0:T(8,128)(2,1)} %refs_0_.11), channel_id=1, source_target_pairs={{0,24},{4,28},{8,16},{12,20},{16,8},{20,12},{24,0},{28,4},{1,25},{... | collective-permute-start | bytes 786440 | tf_op jit(solution)/shard_map/ppermute | solution.py:372
  5.3 4.0 %collective-permute-start.3 = (bf16[128,1024]{1,0:T(8,128)(2,1)}, bf16[128,1024]{1,0:T(8,128)(2,1)S(1)}, u32[]{:S(2)}, u32[]{:S(2)}) collective-permute-start(bf16[128,1024]{1,0:T(8,128)(2,1)} %refs_0_.11), channel_id=1, source_target_pairs={{0,3},{1,2},{2,1},{3,0},{4,7},{5,6},{6,5},{7,4},{8,11},{9,10},{10,... | collective-permute-start | bytes 786440 | tf_op jit(solution)/shard_map/ppermute | solution.py:372
  10.6 2.0 bias_of.1
  12.7 2.4 %collective-permute-start.2 = (bf16[128,1024]{1,0:T(8,128)(2,1)}, bf16[128,1024]{1,0:T(8,128)(2,1)}, u32[]{:S(2)}, u32[]{:S(2)}) collective-permute-start(bf16[128,1024]{1,0:T(8,128)(2,1)} %refs_0_.11), channel_id=1, source_target_pairs={{0,2},{1,3},{2,0},{3,1},{4,6},{5,7},{6,4},{7,5},{8,10},{9,11},{10,... | collective-permute-start | bytes 786440 | tf_op jit(solution)/shard_map/ppermute | solution.py:372
  18.2 9.6 %shard_map.127.old_ref = f32[8,1024]{1,0:T(8,128)} custom-call(s32[8,1024]{1,0:T(8,128)} %order.1.ids_ref, f32[8,1024]{1,0:T(8,128)} %broadcast_1_old_ref.2.old_ref, bf16[8192,1024]{1,0:T(8,128)(2,1)} %refs_1_.7, bf16[8192,1024]{1,0:T(8,128)(2,1)} %refs_1_.7, bf16[128,1024]{1,0:T(8,128)(2,1)} %refs_0_.11, bf16[128,1024]{1,0:T(8,128)(2,1)} %copy-done.11), custom_call_target="tpu_custom_call" | custom-call | flops 4294967296 | bytes 16777216 | tf_op jit(solution)/shard_map/pallas_call | solution.py:103
  30.9 10.2 %shard_map.128.old_ref = f32[8,1024]{1,0:T(8,128)} custom-call(s32[8,1024]{1,0:T(8,128)} %order.1.ids_ref, f32[8,1024]{1,0:T(8,128)} %shard_map.127.old_ref, bf16[8192,1024]{1,0:T(8,128)(2,1)} %refs_1_.7, bf16[8192,1024]{1,0:T(8,128)(2,1)} %refs_1_.7, bf16[128,1024]{1,0:T(8,128)(2,1)} %copy-done.4, bf16[128,1024]{1,0:T(8,128)(2,1)} %copy-done.3, ...), custom_call_target="tpu_custom_call" | custom-call | flops 6442450944 | bytes 8388608 | tf_op jit(solution)/shard_map/pallas_call | solution.py:103
  46.6 10.2 %shard_map.129 = f32[8,1024]{1,0:T(8,128)} custom-call(s32[8,1024]{1,0:T(8,128)} %order.1.ids_ref, f32[8,1024]{1,0:T(8,128)} %shard_map.128.old_ref, bf16[8192,1024]{1,0:T(8,128)(2,1)} %refs_1_.7, bf16[8192,1024]{1,0:T(8,128)(2,1)} %refs_1_.7, bf16[128,1024]{1,0:T(8,128)(2,1)} %copy-done.4, bf16[128,1024]{1,0:T(8,128)(2,1)} %copy-done.3, ...), custom_call_target="tpu_custom_call" | custom-call | flops 6442450944 | bytes 8388608 | tf_op jit(solution)/shard_map/pallas_call | solution.py:103
  57.5 3.5 %collective-permute-done.11 = f32[8,1024]{1,0:T(8,128)S(1)} collective-permute-done((f32[8,1024]{1,0:T(8,128)}, f32[8,1024]{1,0:T(8,128)S(1)}, u32[]{:S(2)}, u32[]{:S(2)}) %collective-permute-start.11) | collective-permute-done | bytes 32800 | tf_op jit(solution)/shard_map/ppermute | solution.py:372
  61.0 2.9 %collective-permute-start.12 = (f32[8,1024]{1,0:T(8,128)S(1)}, f32[8,1024]{1,0:T(8,128)S(1)}, u32[]{:S(2)}, u32[]{:S(2)}) collective-permute-start(f32[8,1024]{1,0:T(8,128)S(1)} %add.83), channel_id=1, source_target_pairs={{0,2},{1,3},{2,0},{3,1},{4,6},{5,7},{6,4},{7,5},{8,10},{9,11},{10,... | collective-permute-start | bytes 98312 | tf_op jit(solution)/shard_map/ppermute | solution.py:372
  67.6 24.3 %shard_map.130 = (f32[384,1024]{1,0:T(8,128)}, bf16[384,1024]{1,0:T(8,128)(2,1)}) custom-call(s32[8,1024]{1,0:T(8,128)} %order.1.ids_ref, bf16[8,1024]{1,0:T(8,128)(2,1)} %get-tuple-element.47.val_ref, bf16[8192,1024]{1,0:T(8,128)(2,1)} %refs_1_.9, bf16[1024,1024]{1,0:T(8,128)(2,1)} %pad_maximum_fusion.pair_ref, bf16[128,1024]{1,0:T(8,128)(2,1)} %copy-done.16, ...), custom_call_target="tpu_custom_call" | custom-call | flops 12884901888 | bytes 16777216 | tf_op jit(solution)/shard_map/pallas_call | solution.py:251
  91.9 2.5 %collective-permute-done.16 = bf16[384,1024]{1,0:T(8,128)(2,1)S(1)} collective-permute-done((bf16[384,1024]{1,0:T(8,128)(2,1)}, bf16[384,1024]{1,0:T(8,128)(2,1)S(1)}, u32[]{:S(2)}, u32[]{:S(2)}) %collective-permute-start.16) | collective-permute-done | bytes 786464 | tf_op jit(solution)/shard_map/ppermute | solution.py:372
  96.2 11.3 %shard_map.131 = (f32[128,1024]{1,0:T(8,128)}, bf16[128,1024]{1,0:T(8,128)(2,1)}) custom-call(s32[8,1024]{1,0:T(8,128)} %order.1.ids_ref, bf16[8,1024]{1,0:T(8,128)(2,1)} %get-tuple-element.47.val_ref, bf16[8192,1024]{1,0:T(8,128)(2,1)} %refs_1_.9, bf16[1024,1024]{1,0:T(8,128)(2,1)} %pad_maximum_fusion.pair_ref, bf16[128,1024]{1,0:T(8,128)(2,1)} %get-tuple-element.54.refs_0_), custom_call_target="tpu_custom_call" | custom-call | flops 4294967296 | bytes 16777216 | tf_op jit(solution)/shard_map/pallas_call | solution.py:251
  111.1 5.7 %collective-permute-done.18 = bf16[128,1024]{1,0:T(8,128)(2,1)S(1)} collective-permute-done((bf16[128,1024]{1,0:T(8,128)(2,1)S(1)}, bf16[128,1024]{1,0:T(8,128)(2,1)S(1)}, u32[]{:S(2)}, u32[]{:S(2)}) %collective-permute-start.18) | collective-permute-done | bytes 262176 | tf_op jit(solution)/shard_map/ppermute | solution.py:372
  116.8 6.2 %collective-permute-done.19 = bf16[128,1024]{1,0:T(8,128)(2,1)S(1)} collective-permute-done((bf16[128,1024]{1,0:T(8,128)(2,1)S(1)}, bf16[128,1024]{1,0:T(8,128)(2,1)S(1)}, u32[]{:S(2)}, u32[]{:S(2)}) %collective-permute-start.19) | collective-permute-done | bytes 262176 | tf_op jit(solution)/shard_map/ppermute | solution.py:372
  128.5 6.6 %collective-permute-done.24.refs_4_.refs_12_ = bf16[128,1024]{1,0:T(8,128)(2,1)S(1)} collective-permute-done((bf16[128,1024]{1,0:T(8,128)(2,1)S(1)}, bf16[128,1024]{1,0:T(8,128)(2,1)S(1)}, u32[]{:S(2)}, u32[]{:S(2)}) %collective-permute-start.24) | collective-permute-done | bytes 262176 | tf_op jit(solution)/shard_map/ppermute | solution.py:372
  135.2 3.9 %collective-permute-done.23.refs_3_.refs_11_ = bf16[128,1024]{1,0:T(8,128)(2,1)S(1)} collective-permute-done((bf16[128,1024]{1,0:T(8,128)(2,1)S(1)}, bf16[128,1024]{1,0:T(8,128)(2,1)S(1)}, u32[]{:S(2)}, u32[]{:S(2)}) %collective-permute-start.23) | collective-permute-done | bytes 262176 | tf_op jit(solution)/shard_map/ppermute | solution.py:372
  140.3 9.5 %shard_map.132.old_ref = f32[8,1024]{1,0:T(8,128)} custom-call(s32[8,1024]{1,0:T(8,128)} %order.1.ids_ref, f32[8,1024]{1,0:T(8,128)} %broadcast_1_old_ref.2.old_ref, bf16[8192,1024]{1,0:T(8,128)(2,1)} %refs_1_.9, bf16[8192,1024]{1,0:T(8,128)(2,1)} %refs_1_.9, bf16[128,1024]{1,0:T(8,128)(2,1)} %copy-done.8, bf16[128,1024]{1,0:T(8,128)(2,1)} %copy-done.12), custom_call_target="tpu_custom_call" | custom-call | flops 4294967296 | bytes 16777216 | tf_op jit(solution)/shard_map/pallas_call | solution.py:103
  151.4 17.8 %shard_map.133 = f32[8,1024]{1,0:T(8,128)} custom-call(s32[8,1024]{1,0:T(8,128)} %order.1.ids_ref, f32[8,1024]{1,0:T(8,128)} %shard_map.132.old_ref, bf16[8192,1024]{1,0:T(8,128)(2,1)} %refs_1_.9, bf16[8192,1024]{1,0:T(8,128)(2,1)} %refs_1_.9, bf16[128,1024]{1,0:T(8,128)(2,1)} %copy-done.26, bf16[128,1024]{1,0:T(8,128)(2,1)} %copy-done.25, ...), custom_call_target="tpu_custom_call" | custom-call | flops 12884901888 | bytes 16777216 | tf_op jit(solution)/shard_map/pallas_call | solution.py:103
  171.0 2.3 collective-permute-done.28
  173.3 2.6 %collective-permute-start.29 = (f32[8,1024]{1,0:T(8,128)S(1)}, f32[8,1024]{1,0:T(8,128)S(1)}, u32[]{:S(2)}, u32[]{:S(2)}) collective-permute-start(f32[8,1024]{1,0:T(8,128)S(1)} %add.94), channel_id=1, source_target_pairs={{0,2},{1,3},{2,0},{3,1},{4,6},{5,7},{6,4},{7,5},{8,10},{9,11},{10,... | collective-permute-start | bytes 98312 | tf_op jit(solution)/shard_map/ppermute | solution.py:372
  176.0 27.8 %shard_map.135 = bf16[8192,1024]{1,0:T(8,128)(2,1)} custom-call(s32[8,1024]{1,0:T(8,128)} %order.1.ids_ref, bf16[8,1024]{1,0:T(8,128)(2,1)} %get-tuple-element.47.val_ref, bf16[128,1024]{1,0:T(8,128)(2,1)} %copy-done.8, bf16[128,1024]{1,0:T(8,128)(2,1)} %copy-done.12, bf16[128,1024]{1,0:T(8,128)(2,1)} %copy-done.26, bf16[128,1024]{1,0:T(8,128)(2,1)} %copy-done.25, ...), custom_call_target="tpu_custom_call" | custom-call | flops 17179869184 | bytes 16777216 | tf_op jit(solution)/shard_map/pallas_call | solution.py:175
  204.4 27.8 %shard_map.134 = bf16[8192,1024]{1,0:T(8,128)(2,1)} custom-call(s32[8,1024]{1,0:T(8,128)} %order.1.ids_ref, bf16[8,1024]{1,0:T(8,128)(2,1)} %get-tuple-element.60.val_ref, bf16[128,1024]{1,0:T(8,128)(2,1)} %refs_0_.11, bf16[128,1024]{1,0:T(8,128)(2,1)} %copy-done.11, bf16[128,1024]{1,0:T(8,128)(2,1)} %copy-done.4, bf16[128,1024]{1,0:T(8,128)(2,1)} %copy-done.3, ...), custom_call_target="tpu_custom_call" | custom-call | flops 17179869184 | bytes 16777216 | tf_op jit(solution)/shard_map/pallas_call | solution.py:175
  232.3 2.4 %bias_grad.1 = f32[64,128]{1,0:T(8,128)} custom-call(s32[8,1024]{1,0:T(8,128)} %order.1.ids_ref, f32[8,1024]{1,0:T(8,128)} %get-tuple-element.61.slope_ref), custom_call_target="tpu_custom_call" | custom-call | flops 268435456 | bytes 1048576 | tf_op jit(solution)/shard_map/bias_grad/pallas_call | solution.py:315
  235.5 4.3 %skip_grad.1 = (bf16[512,1024]{1,0:T(8,128)(2,1)}, f32[1,1024]{1,0:T(1,128)}) custom-call(bf16[128,512]{1,0:T(8,128)(2,1)} %get-tuple-element.89.refs_0_, bf16[128,512]{1,0:T(8,128)(2,1)} %get-tuple-element.78.refs_1_, bf16[128,512]{1,0:T(8,128)(2,1)} %get-tuple-element.83.refs_2_, bf16[128,512]{1,0:T(8,128)(2,1)} %get-tuple-element.88.refs_3_, ...), custom_call_target="tpu_custom_call" | custom-call | flops 1073741824 | bytes 1048576 | tf_op jit(solution)/shard_map/skip_grad/pallas_call | solution.py:346
  (127 shorter events, 34.8 us)
Async XLA Ops:
  0.6 12.0 %collective-permute-start.7 = (bf16[128,1024]{1,0:T(8,128)(2,1)}, bf16[128,1024]{1,0:T(8,128)(2,1)S(1)}, u32[]{:S(2)}, u32[]{:S(2)}) collective-permute-start(bf16[128,1024]{1,0:T(8,128)(2,1)} %refs_0_.11), channel_id=1, source_target_pairs={{0,24},{4,28},{8,16},{12,20},{16,8},{20,12},{24,0},{28,4},{1,25},{... | collective-permute-start | bytes 786440 | tf_op jit(solution)/shard_map/ppermute | solution.py:372
  4.6 12.1 %collective-permute-start.6 = (bf16[128,1024]{1,0:T(8,128)(2,1)}, bf16[128,1024]{1,0:T(8,128)(2,1)S(1)}, u32[]{:S(2)}, u32[]{:S(2)}) collective-permute-start(bf16[128,1024]{1,0:T(8,128)(2,1)} %refs_0_.11), channel_id=1, source_target_pairs={{0,16},{4,20},{8,24},{12,28},{16,0},{20,4},{24,8},{28,12},{1,17},{... | collective-permute-start | bytes 786440 | tf_op jit(solution)/shard_map/ppermute | solution.py:372
  5.1 11.9 %collective-permute-start.5 = (bf16[128,1024]{1,0:T(8,128)(2,1)}, bf16[128,1024]{1,0:T(8,128)(2,1)S(1)}, u32[]{:S(2)}, u32[]{:S(2)}) collective-permute-start(bf16[128,1024]{1,0:T(8,128)(2,1)} %refs_0_.11), channel_id=1, source_target_pairs={{0,8},{4,12},{8,0},{12,4},{16,24},{20,28},{24,16},{28,20},{1,9},{5... | collective-permute-start | bytes 786440 | tf_op jit(solution)/shard_map/ppermute | solution.py:372
  5.3 12.0 %collective-permute-start.4 = (bf16[128,1024]{1,0:T(8,128)(2,1)}, bf16[128,1024]{1,0:T(8,128)(2,1)S(1)}, u32[]{:S(2)}, u32[]{:S(2)}) collective-permute-start(bf16[128,1024]{1,0:T(8,128)(2,1)} %refs_0_.11), channel_id=1, source_target_pairs={{0,4},{4,0},{8,12},{12,8},{16,20},{20,16},{24,28},{28,24},{1,5},{5... | collective-permute-start | bytes 786440 | tf_op jit(solution)/shard_map/ppermute | solution.py:372
  5.3 35.9 %collective-permute-start.3 = (bf16[128,1024]{1,0:T(8,128)(2,1)}, bf16[128,1024]{1,0:T(8,128)(2,1)S(1)}, u32[]{:S(2)}, u32[]{:S(2)}) collective-permute-start(bf16[128,1024]{1,0:T(8,128)(2,1)} %refs_0_.11), channel_id=1, source_target_pairs={{0,3},{1,2},{2,1},{3,0},{4,7},{5,6},{6,5},{7,4},{8,11},{9,10},{10,... | collective-permute-start | bytes 786440 | tf_op jit(solution)/shard_map/ppermute | solution.py:372
  12.7 28.5 %collective-permute-start.2 = (bf16[128,1024]{1,0:T(8,128)(2,1)}, bf16[128,1024]{1,0:T(8,128)(2,1)}, u32[]{:S(2)}, u32[]{:S(2)}) collective-permute-start(bf16[128,1024]{1,0:T(8,128)(2,1)} %refs_0_.11), channel_id=1, source_target_pairs={{0,2},{1,3},{2,0},{3,1},{4,6},{5,7},{6,4},{7,5},{8,10},{9,11},{10,... | collective-permute-start | bytes 786440 | tf_op jit(solution)/shard_map/ppermute | solution.py:372
  16.8 11.1 %collective-permute-start.10 = (bf16[128,1024]{1,0:T(8,128)(2,1)S(1)}, bf16[128,1024]{1,0:T(8,128)(2,1)S(1)}, u32[]{:S(2)}, u32[]{:S(2)}) collective-permute-start(bf16[128,1024]{1,0:T(8,128)(2,1)S(1)} %collective-permute-done.7.refs_4_), channel_id=1, source_target_pairs={{0,4},{4,0},{8,12},{12,8},{16,20},{20,16},{24,28},{28,24},{1,5},{5... | collective-permute-start | bytes 786440 | tf_op jit(solution)/shard_map/ppermute | solution.py:372
  17.0 12.5 %collective-permute-start.9 = (bf16[128,1024]{1,0:T(8,128)(2,1)S(1)}, bf16[128,1024]{1,0:T(8,128)(2,1)S(1)}, u32[]{:S(2)}, u32[]{:S(2)}) collective-permute-start(bf16[128,1024]{1,0:T(8,128)(2,1)S(1)} %collective-permute-done.6.refs_3_), channel_id=1, source_target_pairs={{0,4},{4,0},{8,12},{12,8},{16,20},{20,16},{24,28},{28,24},{1,5},{5... | collective-permute-start | bytes 786440 | tf_op jit(solution)/shard_map/ppermute | solution.py:372
  17.3 12.4 %collective-permute-start.8 = (bf16[128,1024]{1,0:T(8,128)(2,1)S(1)}, bf16[128,1024]{1,0:T(8,128)(2,1)S(1)}, u32[]{:S(2)}, u32[]{:S(2)}) collective-permute-start(bf16[128,1024]{1,0:T(8,128)(2,1)S(1)} %collective-permute-done.5.refs_2_), channel_id=1, source_target_pairs={{0,4},{4,0},{8,12},{12,8},{16,20},{20,16},{24,28},{28,24},{1,5},{5... | collective-permute-start | bytes 786440 | tf_op jit(solution)/shard_map/ppermute | solution.py:372
  27.9 13.3 %collective-permute-start.1 = (bf16[128,1024]{1,0:T(8,128)(2,1)S(1)}, bf16[128,1024]{1,0:T(8,128)(2,1)S(1)}, u32[]{:S(2)}, u32[]{:S(2)}) collective-permute-start(bf16[128,1024]{1,0:T(8,128)(2,1)S(1)} %copy-done.9), channel_id=1, source_target_pairs={{0,1},{1,0},{2,3},{3,2},{4,5},{5,4},{6,7},{7,6},{8,9},{9,8},{10,11... | collective-permute-start | bytes 786440 | tf_op jit(solution)/shard_map/ppermute | solution.py:372
  29.5 27.3 %collective-permute-start = (bf16[512,1024]{1,0:T(8,128)(2,1)S(1)}, bf16[512,1024]{1,0:T(8,128)(2,1)S(1)}, u32[]{:S(2)}, u32[]{:S(2)}) collective-permute-start(bf16[512,1024]{1,0:T(8,128)(2,1)S(1)} %copy-done.10), channel_id=1, source_target_pairs={{0,4},{4,0},{8,12},{12,8},{16,20},{20,16},{24,28},{28,24},{1,5},{5... | collective-permute-start | bytes 3145736 | tf_op jit(solution)/shard_map/ppermute | solution.py:372
  43.1 23.7 %collective-permute-start.13 = (bf16[128,1024]{1,0:T(8,128)(2,1)S(1)}, bf16[128,1024]{1,0:T(8,128)(2,1)S(1)}, u32[]{:S(2)}, u32[]{:S(2)}) collective-permute-start(bf16[128,1024]{1,0:T(8,128)(2,1)S(1)} %get-tuple-element.42), channel_id=1, source_target_pairs={{0,8},{4,12},{8,0},{12,4},{16,24},{20,28},{24,16},{28,20},{1,9},{5... | collective-permute-start | bytes 786440 | tf_op jit(solution)/shard_map/ppermute | solution.py:372
  44.6 22.2 %collective-permute-start.14 = (bf16[128,1024]{1,0:T(8,128)(2,1)S(1)}, bf16[128,1024]{1,0:T(8,128)(2,1)S(1)}, u32[]{:S(2)}, u32[]{:S(2)}) collective-permute-start(bf16[128,1024]{1,0:T(8,128)(2,1)S(1)} %get-tuple-element.43), channel_id=1, source_target_pairs={{0,16},{4,20},{8,24},{12,28},{16,0},{20,4},{24,8},{28,12},{1,17},{... | collective-permute-start | bytes 786440 | tf_op jit(solution)/shard_map/ppermute | solution.py:372
  45.4 21.4 %collective-permute-start.15 = (bf16[128,1024]{1,0:T(8,128)(2,1)S(1)}, bf16[128,1024]{1,0:T(8,128)(2,1)S(1)}, u32[]{:S(2)}, u32[]{:S(2)}) collective-permute-start(bf16[128,1024]{1,0:T(8,128)(2,1)S(1)} %get-tuple-element.44), channel_id=1, source_target_pairs={{0,24},{4,28},{8,16},{12,20},{16,8},{20,12},{24,0},{28,4},{1,25},{... | collective-permute-start | bytes 786440 | tf_op jit(solution)/shard_map/ppermute | solution.py:372
  109.1 13.9 %collective-permute-start.19 = (bf16[128,1024]{1,0:T(8,128)(2,1)S(1)}, bf16[128,1024]{1,0:T(8,128)(2,1)S(1)}, u32[]{:S(2)}, u32[]{:S(2)}) collective-permute-start(bf16[128,1024]{1,0:T(8,128)(2,1)S(1)} %get-tuple-element.52), channel_id=1, source_target_pairs={{0,16},{4,20},{8,24},{12,28},{16,0},{20,4},{24,8},{28,12},{1,17},{... | collective-permute-start | bytes 786440 | tf_op jit(solution)/shard_map/ppermute | solution.py:372
  109.8 13.2 %collective-permute-start.20 = (bf16[128,1024]{1,0:T(8,128)(2,1)S(1)}, bf16[128,1024]{1,0:T(8,128)(2,1)S(1)}, u32[]{:S(2)}, u32[]{:S(2)}) collective-permute-start(bf16[128,1024]{1,0:T(8,128)(2,1)S(1)} %get-tuple-element.53), channel_id=1, source_target_pairs={{0,24},{4,28},{8,16},{12,20},{16,8},{20,12},{24,0},{28,4},{1,25},{... | collective-permute-start | bytes 786440 | tf_op jit(solution)/shard_map/ppermute | solution.py:372
  126.5 12.5 %collective-permute-start.23 = (bf16[128,1024]{1,0:T(8,128)(2,1)S(1)}, bf16[128,1024]{1,0:T(8,128)(2,1)S(1)}, u32[]{:S(2)}, u32[]{:S(2)}) collective-permute-start(bf16[128,1024]{1,0:T(8,128)(2,1)S(1)} %get-tuple-element.62.refs_2_.refs_0_.refs_8_), channel_id=1, source_target_pairs={{0,16},{4,20},{8,24},{12,28},{16,0},{20,4},{24,8},{28,12},{1,17},{... | collective-permute-start | bytes 786440 | tf_op jit(solution)/shard_map/ppermute | solution.py:372
  127.0 12.1 %collective-permute-start.22 = (bf16[128,1024]{1,0:T(8,128)(2,1)S(1)}, bf16[128,1024]{1,0:T(8,128)(2,1)S(1)}, u32[]{:S(2)}, u32[]{:S(2)}) collective-permute-start(bf16[128,1024]{1,0:T(8,128)(2,1)S(1)} %get-tuple-element.62.refs_2_.refs_0_.refs_8_), channel_id=1, source_target_pairs={{0,8},{4,12},{8,0},{12,4},{16,24},{20,28},{24,16},{28,20},{1,9},{5... | collective-permute-start | bytes 786440 | tf_op jit(solution)/shard_map/ppermute | solution.py:372
  128.5 11.1 %collective-permute-start.21 = (bf16[128,1024]{1,0:T(8,128)(2,1)S(1)}, bf16[128,1024]{1,0:T(8,128)(2,1)S(1)}, u32[]{:S(2)}, u32[]{:S(2)}) collective-permute-start(bf16[128,1024]{1,0:T(8,128)(2,1)S(1)} %get-tuple-element.62.refs_2_.refs_0_.refs_8_), channel_id=1, source_target_pairs={{0,4},{4,0},{8,12},{12,8},{16,20},{20,16},{24,28},{28,24},{1,5},{5... | collective-permute-start | bytes 786440 | tf_op jit(solution)/shard_map/ppermute | solution.py:372
  135.2 14.7 %collective-permute-start.27 = (bf16[128,1024]{1,0:T(8,128)(2,1)S(1)}, bf16[128,1024]{1,0:T(8,128)(2,1)S(1)}, u32[]{:S(2)}, u32[]{:S(2)}) collective-permute-start(bf16[128,1024]{1,0:T(8,128)(2,1)S(1)} %collective-permute-done.24.refs_4_.refs_12_), channel_id=1, source_target_pairs={{0,4},{4,0},{8,12},{12,8},{16,20},{20,16},{24,28},{28,24},{1,5},{5... | collective-permute-start | bytes 786440 | tf_op jit(solution)/shard_map/ppermute | solution.py:372
  139.1 10.8 %collective-permute-start.26 = (bf16[128,1024]{1,0:T(8,128)(2,1)S(1)}, bf16[128,1024]{1,0:T(8,128)(2,1)S(1)}, u32[]{:S(2)}, u32[]{:S(2)}) collective-permute-start(bf16[128,1024]{1,0:T(8,128)(2,1)S(1)} %collective-permute-done.23.refs_3_.refs_11_), channel_id=1, source_target_pairs={{0,4},{4,0},{8,12},{12,8},{16,20},{20,16},{24,28},{28,24},{1,5},{5... | collective-permute-start | bytes 786440 | tf_op jit(solution)/shard_map/ppermute | solution.py:372
  139.1 10.8 %collective-permute-start.25 = (bf16[128,1024]{1,0:T(8,128)(2,1)S(1)}, bf16[128,1024]{1,0:T(8,128)(2,1)S(1)}, u32[]{:S(2)}, u32[]{:S(2)}) collective-permute-start(bf16[128,1024]{1,0:T(8,128)(2,1)S(1)} %collective-permute-done.22.refs_2_.refs_10_), channel_id=1, source_target_pairs={{0,4},{4,0},{8,12},{12,8},{16,20},{20,16},{24,28},{28,24},{1,5},{5... | collective-permute-start | bytes 786440 | tf_op jit(solution)/shard_map/ppermute | solution.py:372
  170.9 63.8 %collective-permute-start.30 = (bf16[512,512]{1,0:T(8,128)(2,1)S(1)}, bf16[512,512]{1,0:T(8,128)(2,1)S(1)}, u32[]{:S(2)}, u32[]{:S(2)}) collective-permute-start(bf16[512,512]{1,0:T(8,128)(2,1)S(1)} %pad_maximum_fusion.2), channel_id=1, source_target_pairs={{0,4},{4,0},{8,12},{12,8},{16,20},{20,16},{24,28},{28,24},{1,5},{5... | collective-permute-start | bytes 1572872 | tf_op jit(solution)/shard_map/ppermute | solution.py:372
  173.3 30.5 %collective-permute-start.29 = (f32[8,1024]{1,0:T(8,128)S(1)}, f32[8,1024]{1,0:T(8,128)S(1)}, u32[]{:S(2)}, u32[]{:S(2)}) collective-permute-start(f32[8,1024]{1,0:T(8,128)S(1)} %add.94), channel_id=1, source_target_pairs={{0,2},{1,3},{2,0},{3,1},{4,6},{5,7},{6,4},{7,5},{8,10},{9,11},{10,... | collective-permute-start | bytes 98312 | tf_op jit(solution)/shard_map/ppermute | solution.py:372
  (37 other events, 303.1 us)
